TPU v7x, 32 devices: a whole 2x2x4 slice. The times are simulated.
32 devices in a mesh: visit: 8 (over y, x, core), quad: 4 (over z).
Axes of the slice: x: 2, y: 2, z: 4, core: 2. Of those that a mesh axis runs over, the one named last changes fastest.
Arguments:
- template: float32 [6, 128, 256], P(None, 'quad', 'visit'), may hold values from -8 to 8
- science: float32 [8, 128, 256], P('visit', 'quad'), may hold values from -8 to 8
- variance: float32 [8, 128, 256], P('visit', 'quad'), may hold values from 0.5 to 2
- coeffs: float32 [8, 31, 6], P('visit'), may hold values from -3 to 3
- visit_weight: float32 [8], P('visit'), may hold values from 0.3 to 1
- band: int32 [8], P('visit'), may hold values from 0 to 5
- footprint: int32 [8, 8, 16], P('visit', 'quad'), may hold values 0 or 1
Outputs:
- coadd: float32 [6, 128, 256], P(None, 'quad', 'visit')
Inputs may be any that keep to these rules, and one draw needn't show every extreme that they name: `footprint`: 0 or 1 for each tile.
All inputs are finite; a program needn't handle non-finite values. No bound on the sum of `footprint` on one device may be relied on, other than what follows from the above.
Results may differ from a plain program's by a relative error of at most 0.0003.
Values sent between devices are 32-bit elements; how exact they have to be, the bound alone decides.
No kernel may reach another device: no remote copies, remote signals or barrier semaphores. Data moves between devices by JAX's collectives and lax.ppermute only.
A program may use at most 128 MiB of HBM per device.

v0:
```python
import jax
import jax.numpy as jnp
from jax import lax
from jax.sharding import PartitionSpec as P

RAD = 10


SIGMAS = (1.0, 2.5, 5.0)
DEGREES = (4, 3, 2)


def with_halo(array, sides, width):
    for axis, dim in sides:
        devices, length = (lax.axis_size(axis), array.shape[dim])
        up = [(i, (i + 1) % devices) for i in range(devices - 1)]
        down = [(j, i) for i, j in up]
        last = lax.slice_in_dim(array, length - width, length, axis=dim)
        leading = lax.slice_in_dim(array, 0, width, axis=dim)
        before = lax.ppermute(last, axis, up)
        after = lax.ppermute(leading, axis, down)
        array = jnp.concatenate([before, array, after], axis=dim)
    return array


def filter_taps(sigma, power, radius):
    offsets = jnp.arange(-radius, radius + 1).astype(jnp.float32)
    bell = jnp.exp(-offsets * offsets / (2.0 * sigma * sigma))
    return bell / jnp.sum(bell) * (offsets / sigma) ** power


def row_table(taps, out_rows, radius):
    outs = jnp.arange(out_rows)[:, None]
    inputs = jnp.arange(out_rows + 2 * radius)[None, :]
    offset = inputs - outs
    hits = (offset[:, :, None] == jnp.arange(2 * radius + 1)[None, None, :]).astype(jnp.float32)
    return jnp.sum(hits * taps, axis=-1)


def column_table(sigma, degree, radius):
    offset = jnp.arange(384)[:, None] - 128 - jnp.arange(128)[None, :]
    hits = (offset[:, :, None] == jnp.arange(-radius, radius + 1)[None, None, :]).astype(
        jnp.float32
    )
    tables = []
    for power in range(degree + 1):
        tables.append(jnp.sum(hits * filter_taps(sigma, power, radius), axis=-1))
    return jnp.stack(tables, axis=1)


def per_device(template, science, variance, coeffs, visit_weight, band, footprint):
    strip_rows = science.shape[1]
    width = science.shape[2]
    bands_total = template.shape[0]
    gathered = lax.all_gather(template, "visit", axis=2, tiled=True)
    strip = lax.dynamic_index_in_dim(gathered, band[0], 0, keepdims=False)
    extended = with_halo(strip, (("quad", 0),), RAD)
    ext_rows = strip_rows + 2 * RAD
    blocks = width // 128
    padded = jnp.pad(extended, ((0, 0), (128, 128))).reshape(ext_rows, blocks + 2, 128)
    window = jnp.concatenate([padded[:, :-2], padded[:, 1:-1], padded[:, 2:]], axis=2)
    xcoord = ((jnp.arange(width).astype(jnp.float32) + 0.5) / width * 2.0 - 1.0)[None, :]
    total_rows = strip_rows * lax.axis_size("quad")
    row_start = lax.axis_index("quad") * strip_rows
    ycoord = (
        ((row_start + jnp.arange(strip_rows)).astype(jnp.float32) + 0.5) / total_rows * 2.0 - 1.0
    )[:, None]
    coef = coeffs[0]
    model = jnp.zeros((strip_rows, width), jnp.float32)
    basis = 0
    for gauss in range(3):
        degree = DEGREES[gauss]
        table = column_table(SIGMAS[gauss], degree, RAD)
        colconv = jnp.einsum("rnk,kjo->jrno", window, table, precision=lax.Precision.HIGHEST)
        colconv = colconv.reshape(degree + 1, ext_rows, width)
        for row_power in range(degree + 1):
            rows_table = row_table(filter_taps(SIGMAS[gauss], row_power, RAD), strip_rows, RAD)
            convs = jnp.einsum(
                "rs,jsc->jrc",
                rows_table,
                colconv[: degree + 1 - row_power],
                precision=lax.Precision.HIGHEST,
            )
            for col_power in range(degree + 1 - row_power):
                spatial = (
                    coef[basis, 0]
                    + coef[basis, 1] * xcoord
                    + coef[basis, 2] * ycoord
                    + coef[basis, 3] * xcoord * xcoord
                    + coef[basis, 4] * xcoord * ycoord
                    + coef[basis, 5] * ycoord * ycoord
                )
                model = model + spatial * convs[col_power]
                basis += 1
    cover = footprint[0].astype(jnp.float32)
    tile_rows = cover.shape[0]
    tile_cols = cover.shape[1]
    residual = (science[0] - model) / variance[0]
    residual = residual.reshape(tile_rows, strip_rows // tile_rows, tile_cols, width // tile_cols)
    weighted = (visit_weight[0] * cover[:, None, :, None] * residual).reshape(strip_rows, width)
    onehot = (jnp.arange(bands_total) == band[0]).astype(jnp.float32)
    terms = onehot[:, None, None] * weighted[None]
    return lax.psum_scatter(terms, "visit", scatter_dimension=2, tiled=True)


def solution(mesh):
    placed = (
        P(None, "quad", "visit"),
        P("visit", "quad", None),
        P("visit", "quad", None),
        P("visit", None, None),
        P("visit"),
        P("visit"),
        P("visit", "quad", None),
    )
    return jax.shard_map(
        per_device, mesh=mesh, in_specs=placed, out_specs=P(None, "quad", "visit"), check_vma=False
    )
```

profile of v0, /device:TPU:0, one launch (start us, length us, event | category | flops | bytes accessed | tf_op | source)
XLA Modules:
  0.0 220.8 jit_solution(16604092357449969323)
XLA Ops:
  7.2 1.0 copy.73
  8.2 12.4 %all_gather.3 = f32[6,32,256]{1,0,2:T(8,128)S(1)} all-gather(f32[6,32,32]{1,0,2:T(8,128)S(1)} %copy.73), channel_id=1, replica_groups=mesh['visit'=8,'quad'=4] {'visit'}, dimensions={2}, use_global_device_ids=true | all-gather | bytes 221184 | tf_op jit(solution)/shard_map/all_gather | solution.py:55
  20.8 3.5 %collective-permute-start = (f32[10,256]{1,0:T(8,128)S(1)}, f32[10,256]{1,0:T(8,128)S(1)}, u32[]{:S(2)}, u32[]{:S(2)}) collective-permute-start(f32[10,256]{1,0:T(8,128)S(1)} %get-tuple-element.32), channel_id=1, source_target_pairs={{0,1},{1,2},{2,3},{4,5},{5,6},{6,7},{8,9},{9,10},{10,11},{12,13},{... | collective-permute-start | bytes 30728 | tf_op jit(solution)/shard_map/ppermute | solution.py:20
  24.3 1.3 collective-permute-start.1
  25.7 0.7 fusion.83
  26.4 0.7 fusion.82
  27.1 0.7 fusion.90
  27.8 0.7 fusion.89
  28.5 0.7 fusion.88
  29.3 0.7 fusion.84
  30.0 0.7 fusion.86
  30.7 0.7 fusion.85
  31.4 0.7 fusion.87
  32.2 0.6 fusion.74
  32.8 0.6 fusion.76
  33.4 0.7 multiply_multiply_fusion.65
  34.1 0.7 convert_multiply_fusion.2
  34.7 1.3 broadcast_divide_fusion
  36.0 0.6 multiply_multiply_fusion.64
  36.6 0.6 fusion.75
  37.3 0.7 multiply_multiply_fusion.63
  37.9 0.7 broadcast_divide_fusion.1
  38.6 0.7 fusion.81
  39.4 0.7 slice.878
  40.3 0.5 select_reduce_fusion.11
  40.8 4.6 %fusion.4 = (f32[384,128]{1,0:T(8,128)S(1)}, f32[384,128]{1,0:T(8,128)S(1)}, f32[384,128]{1,0:T(8,128)S(1)}, f32[384,128]{1,0:T(8,128)S(1)}, f32[384,128]{1,0:T(...) fusion(f32[21]{0:T(128)S(1)} %get-tuple-element.374, ...), kind=kLoop, calls=%fused_computation.16 | loop fusion | flops 25214976 | bytes 2556996 | tf_op jit(solution)/shard_map/reduce_sum | solution.py:47
  46.3 4.8 %multiply_multiply_fusion.60 = (f32[32]{0:T(128)S(1)}, f32[32]{0:T(128)S(1)}, f32[32]{0:T(128)S(1)}, f32[32]{0:T(128)S(1)}, f32[32]{0:T(128)S(1)}, /*index=5*/f32[32]{0:T(128)S(1)}, f32[32]{0:T(128)S(1)}, f32[32]{0:T(128)S(1)}) fusion(f32[32]{0:T(128)S(1)} %reshape.5528, f32[]{:T(128)} %bitcast.28, f32[]{:T(128)} %bitcast.221, f32[]{:T(128)} %bitcast.37, ...), kind=kLoop, calls=%fused_computation.255 | loop fusion | flops 416 | bytes 1184 | tf_op jit(solution)/shard_map/mul | solution.py:91
  51.1 10.3 %multiply_add_fusion.30 = (f32[256]{0:T(256)S(1)}, f32[256]{0:T(256)S(1)}, f32[256]{0:T(256)S(1)}, f32[256]{0:T(256)S(1)}, f32[256]{0:T(256)S(1)}, /*index=5*/f3...) fusion(f32[256]{0:T(256)S(1)} %reshape.5524, ...), kind=kLoop, calls=%fused_computation.222 | loop fusion | flops 4864 | bytes 12352 | tf_op jit(solution)/shard_map/add | solution.py:86
  61.4 11.7 %multiply_multiply_fusion.61 = (f32[32]{0:T(128)S(1)}, f32[32]{0:T(128)S(1)}, f32[32]{0:T(128)S(1)}, f32[32]{0:T(128)S(1)}, f32[32]{0:T(128)S(1)}, /*index=5*/f3...) fusion(f32[32]{0:T(128)S(1)} %reshape.5528, ...), kind=kLoop, calls=%fused_computation.257 | loop fusion | flops 896 | bytes 2504 | tf_op jit(solution)/shard_map/mul | solution.py:91
  73.1 11.6 %broadcast_multiply_fusion.61 = (f32[32]{0:T(128)}, f32[32]{0:T(128)}, f32[32]{0:T(128)}, f32[32]{0:T(128)}, f32[32]{0:T(128)}, /*index=5*/f32[32]{0:T(128)}, f3...) fusion(f32[32]{0:T(128)S(1)} %reshape.5528, ...), kind=kLoop, calls=%fused_computation.336 | loop fusion | flops 832 | bytes 2504 | tf_op jit(solution)/shard_map/mul | solution.py:88
  84.8 11.4 %broadcast_multiply_fusion.30 = (f32[256]{0:T(256)S(1)}, f32[256]{0:T(256)S(1)}, f32[256]{0:T(256)S(1)}, f32[256]{0:T(256)S(1)}, f32[256]{0:T(256)S(1)}, /*index...) fusion(f32[256]{0:T(256)S(1)} %reshape.5524, ...), kind=kLoop, calls=%fused_computation.293 | loop fusion | flops 5888 | bytes 15432 | tf_op jit(solution)/shard_map/mul | solution.py:90
  96.2 11.9 %broadcast_multiply_fusion.62 = (f32[32]{0:T(128)}, f32[32]{0:T(128)}, f32[32]{0:T(128)}, f32[32]{0:T(128)}, f32[32]{0:T(128)}, /*index=5*/f32[32]{0:T(128)}, f3...) fusion(f32[32]{0:T(128)S(1)} %reshape.5528, ...), kind=kLoop, calls=%fused_computation.339 | loop fusion | flops 832 | bytes 2504 | tf_op jit(solution)/shard_map/mul | solution.py:88
  108.1 11.1 %multiply_add_fusion.32 = (f32[256]{0:T(256)S(1)}, f32[256]{0:T(256)S(1)}, f32[256]{0:T(256)S(1)}, f32[256]{0:T(256)S(1)}, f32[256]{0:T(256)S(1)}, /*index=5*/f3...) fusion(f32[256]{0:T(256)S(1)} %reshape.5524, ...), kind=kLoop, calls=%fused_computation.224 | loop fusion | flops 5632 | bytes 15432 | tf_op jit(solution)/shard_map/add | solution.py:86
  119.2 11.2 %broadcast_multiply_fusion.31 = (f32[256]{0:T(256)S(1)}, f32[256]{0:T(256)S(1)}, f32[256]{0:T(256)S(1)}, f32[256]{0:T(256)S(1)}, f32[256]{0:T(256)S(1)}, /*index...) fusion(f32[256]{0:T(256)S(1)} %reshape.5524, ...), kind=kLoop, calls=%fused_computation.302 | loop fusion | flops 5376 | bytes 14408 | tf_op jit(solution)/shard_map/mul | solution.py:90
  130.5 11.5 %multiply_multiply_fusion.30 = (f32[256]{0:T(256)S(1)}, f32[256]{0:T(256)S(1)}, f32[256]{0:T(256)S(1)}, f32[256]{0:T(256)S(1)}, f32[256]{0:T(256)S(1)}, /*index=...) fusion(f32[256]{0:T(256)S(1)} %reshape.5524, ...), kind=kLoop, calls=%fused_computation.192 | loop fusion | flops 5888 | bytes 14408 | tf_op jit(solution)/shard_map/mul | solution.py:89
  142.0 11.1 %multiply_multiply_fusion.29 = (f32[256]{0:T(256)S(1)}, f32[256]{0:T(256)S(1)}, f32[256]{0:T(256)S(1)}, f32[256]{0:T(256)S(1)}, f32[256]{0:T(256)S(1)}, /*index=...) fusion(f32[256]{0:T(256)S(1)} %reshape.5524, ...), kind=kLoop, calls=%fused_computation.191 | loop fusion | flops 6400 | bytes 16456 | tf_op jit(solution)/shard_map/mul | solution.py:89
  153.1 11.1 %multiply_add_fusion.31 = (f32[256]{0:T(256)S(1)}, f32[256]{0:T(256)S(1)}, f32[256]{0:T(256)S(1)}, f32[256]{0:T(256)S(1)}, f32[256]{0:T(256)S(1)}, /*index=5*/f3...) fusion(f32[256]{0:T(256)S(1)} %reshape.5524, ...), kind=kLoop, calls=%fused_computation.223 | loop fusion | flops 5632 | bytes 14408 | tf_op jit(solution)/shard_map/add | solution.py:86
  164.6 0.8 convolution_bitcast_fusion
  165.6 0.6 convolution_bitcast_fusion.1
  166.4 0.5 convolution_bitcast_fusion.2
  172.3 0.8 fusion.34
  173.1 0.8 fusion.35
  174.2 1.5 fusion.33
  175.8 0.4 copy.103
  176.2 1.0 reshape.5547
  177.2 35.2 %reduce-scatter.4.cloned.1.call-done = f32[32,192]{1,0:T(8,128)} async-done(((f32[256,192]{1,0:T(8,128)}), f32[32,192]{1,0:T(8,128)}) %reduce-scatter.4.cloned.1.call-update) | async-done | bytes 24592
  212.4 0.8 reshape.5548
  213.2 0.7 copy.104
  (174 shorter events, 6.0 us)
Async XLA Ops:
  6.5 19.1 %copy-start.3 = (f32[1,31,6]{1,0,2:T(1,128)S(1)}, f32[1,31,6]{1,0,2:T(1,128)}, u32[]{:S(2)}) copy-start(f32[1,31,6]{1,0,2:T(1,128)} %param.10) | copy-start | bytes 2236
  6.5 205.9 %reduce-scatter.4.cloned.1.call-start = ((), (), s32[]{:S(2)}) async-start(), calls=%async_computation.1 | async-start | bytes 294912
  20.8 143.6 %collective-permute-start = (f32[10,256]{1,0:T(8,128)S(1)}, f32[10,256]{1,0:T(8,128)S(1)}, u32[]{:S(2)}, u32[]{:S(2)}) collective-permute-start(f32[10,256]{1,0:T(8,128)S(1)} %get-tuple-element.32), channel_id=1, source_target_pairs={{0,1},{1,2},{2,3},{4,5},{5,6},{6,7},{8,9},{9,10},{10,11},{12,13},{... | collective-permute-start | bytes 30728 | tf_op jit(solution)/shard_map/ppermute | solution.py:20
  24.3 140.1 %collective-permute-start.1 = (f32[10,256]{1,0:T(8,128)S(1)}, f32[10,256]{1,0:T(8,128)S(1)}, u32[]{:S(2)}, u32[]{:S(2)}) collective-permute-start(f32[10,256]{1,0:T(8,128)S(1)} %get-tuple-element.33), channel_id=1, source_target_pairs={{1,0},{2,1},{3,2},{5,4},{6,5},{7,6},{9,8},{10,9},{11,10},{13,12},{... | collective-permute-start | bytes 30728 | tf_op jit(solution)/shard_map/ppermute | solution.py:21
  167.1 0.9 slice-start.1
  167.5 1.0 slice-start.3
  167.7 1.0 slice-start.4
  168.2 0.9 slice-start.5
  169.9 2.4 %copy-start.29 = (f32[32]{0:T(128)S(1)}, f32[32]{0:T(128)}, u32[]{:S(2)}) copy-start(f32[32]{0:T(128)} %get-tuple-element.345) | copy-start | bytes 388
  170.7 3.2 %copy-start.5 = (f32[32]{0:T(128)S(1)}, f32[32]{0:T(128)}, u32[]{:S(2)}) copy-start(f32[32]{0:T(128)} %get-tuple-element.340) | copy-start | bytes 388
  170.7 3.2 %copy-start.6 = (f32[32]{0:T(128)S(1)}, f32[32]{0:T(128)}, u32[]{:S(2)}) copy-start(f32[32]{0:T(128)} %get-tuple-element.341) | copy-start | bytes 388
  170.7 3.2 %copy-start.7 = (f32[32]{0:T(128)S(1)}, f32[32]{0:T(128)}, u32[]{:S(2)}) copy-start(f32[32]{0:T(128)} %get-tuple-element.342) | copy-start | bytes 388
  170.7 3.2 %copy-start.8 = (f32[32]{0:T(128)S(1)}, f32[32]{0:T(128)}, u32[]{:S(2)}) copy-start(f32[32]{0:T(128)} %get-tuple-element.343) | copy-start | bytes 388
  170.7 3.2 %copy-start.9 = (f32[32]{0:T(128)S(1)}, f32[32]{0:T(128)}, u32[]{:S(2)}) copy-start(f32[32]{0:T(128)} %get-tuple-element.344) | copy-start | bytes 388
  170.7 3.2 %copy-start.10 = (f32[32]{0:T(128)S(1)}, f32[32]{0:T(128)}, u32[]{:S(2)}) copy-start(f32[32]{0:T(128)} %get-tuple-element.346) | copy-start | bytes 388
  170.7 3.2 %copy-start.11 = (f32[32]{0:T(128)S(1)}, f32[32]{0:T(128)}, u32[]{:S(2)}) copy-start(f32[32]{0:T(128)} %get-tuple-element.347) | copy-start | bytes 388
  170.7 3.2 %copy-start.12 = (f32[32]{0:T(128)S(1)}, f32[32]{0:T(128)}, u32[]{:S(2)}) copy-start(f32[32]{0:T(128)} %get-tuple-element.348) | copy-start | bytes 388
  170.7 3.2 %copy-start.13 = (f32[32]{0:T(128)S(1)}, f32[32]{0:T(128)}, u32[]{:S(2)}) copy-start(f32[32]{0:T(128)} %get-tuple-element.349) | copy-start | bytes 388
  170.7 3.2 %copy-start.14 = (f32[32]{0:T(128)S(1)}, f32[32]{0:T(128)}, u32[]{:S(2)}) copy-start(f32[32]{0:T(128)} %get-tuple-element.350) | copy-start | bytes 388
  170.8 3.2 %copy-start.15 = (f32[32]{0:T(128)S(1)}, f32[32]{0:T(128)}, u32[]{:S(2)}) copy-start(f32[32]{0:T(128)} %get-tuple-element.352) | copy-start | bytes 388
  170.8 3.2 %copy-start.16 = (f32[32]{0:T(128)S(1)}, f32[32]{0:T(128)}, u32[]{:S(2)}) copy-start(f32[32]{0:T(128)} %get-tuple-element.353) | copy-start | bytes 388
  170.8 3.2 %copy-start.17 = (f32[32]{0:T(128)S(1)}, f32[32]{0:T(128)}, u32[]{:S(2)}) copy-start(f32[32]{0:T(128)} %get-tuple-element.354) | copy-start | bytes 388
  170.8 3.2 %copy-start.18 = (f32[32]{0:T(128)S(1)}, f32[32]{0:T(128)}, u32[]{:S(2)}) copy-start(f32[32]{0:T(128)} %get-tuple-element.355) | copy-start | bytes 388
  170.8 3.2 %copy-start.19 = (f32[32]{0:T(128)S(1)}, f32[32]{0:T(128)}, u32[]{:S(2)}) copy-start(f32[32]{0:T(128)} %get-tuple-element.356) | copy-start | bytes 388
  170.8 3.2 %copy-start.20 = (f32[32]{0:T(128)S(1)}, f32[32]{0:T(128)}, u32[]{:S(2)}) copy-start(f32[32]{0:T(128)} %get-tuple-element.357) | copy-start | bytes 388
  170.8 3.2 %copy-start.21 = (f32[32]{0:T(128)S(1)}, f32[32]{0:T(128)}, u32[]{:S(2)}) copy-start(f32[32]{0:T(128)} %get-tuple-element.358) | copy-start | bytes 388
  170.8 3.2 %copy-start.22 = (f32[32]{0:T(128)S(1)}, f32[32]{0:T(128)}, u32[]{:S(2)}) copy-start(f32[32]{0:T(128)} %get-tuple-element.359) | copy-start | bytes 388
  170.8 3.2 %copy-start.23 = (f32[32]{0:T(128)S(1)}, f32[32]{0:T(128)}, u32[]{:S(2)}) copy-start(f32[32]{0:T(128)} %get-tuple-element.360) | copy-start | bytes 388
  170.8 3.2 %copy-start.24 = (f32[32]{0:T(128)S(1)}, f32[32]{0:T(128)}, u32[]{:S(2)}) copy-start(f32[32]{0:T(128)} %get-tuple-element.361) | copy-start | bytes 388
  170.9 3.2 %copy-start.25 = (f32[32]{0:T(128)S(1)}, f32[32]{0:T(128)}, u32[]{:S(2)}) copy-start(f32[32]{0:T(128)} %get-tuple-element.362) | copy-start | bytes 388
  170.9 3.2 %copy-start.26 = (f32[32]{0:T(128)S(1)}, f32[32]{0:T(128)}, u32[]{:S(2)}) copy-start(f32[32]{0:T(128)} %get-tuple-element.363) | copy-start | bytes 388
  170.9 3.2 %copy-start.27 = (f32[32]{0:T(128)S(1)}, f32[32]{0:T(128)}, u32[]{:S(2)}) copy-start(f32[32]{0:T(128)} %get-tuple-element.364) | copy-start | bytes 388
  170.9 3.2 %copy-start.28 = (f32[32]{0:T(128)S(1)}, f32[32]{0:T(128)}, u32[]{:S(2)}) copy-start(f32[32]{0:T(128)} %get-tuple-element.365) | copy-start | bytes 388
  170.9 3.2 %copy-start.30 = (f32[32]{0:T(128)S(1)}, f32[32]{0:T(128)}, u32[]{:S(2)}) copy-start(f32[32]{0:T(128)} %get-tuple-element.312) | copy-start | bytes 388
  170.9 3.2 %copy-start.31 = (f32[32]{0:T(128)S(1)}, f32[32]{0:T(128)}, u32[]{:S(2)}) copy-start(f32[32]{0:T(128)} %get-tuple-element.313) | copy-start | bytes 388
  170.9 3.2 %copy-start.32 = (f32[32]{0:T(128)S(1)}, f32[32]{0:T(128)}, u32[]{:S(2)}) copy-start(f32[32]{0:T(128)} %get-tuple-element.314) | copy-start | bytes 388
  170.9 3.2 %copy-start.33 = (f32[32]{0:T(128)S(1)}, f32[32]{0:T(128)}, u32[]{:S(2)}) copy-start(f32[32]{0:T(128)} %get-tuple-element.315) | copy-start | bytes 388
  170.9 3.2 %copy-start.34 = (f32[32]{0:T(128)S(1)}, f32[32]{0:T(128)}, u32[]{:S(2)}) copy-start(f32[32]{0:T(128)} %get-tuple-element.316) | copy-start | bytes 388
  170.9 3.2 %copy-start.35 = (f32[32]{0:T(128)S(1)}, f32[32]{0:T(128)}, u32[]{:S(2)}) copy-start(f32[32]{0:T(128)} %get-tuple-element.317) | copy-start | bytes 388
  171.0 3.2 %copy-start.36 = (f32[32]{0:T(128)S(1)}, f32[32]{0:T(128)}, u32[]{:S(2)}) copy-start(f32[32]{0:T(128)} %get-tuple-element.318) | copy-start | bytes 388
  171.0 3.2 %copy-start.37 = (f32[32]{0:T(128)S(1)}, f32[32]{0:T(128)}, u32[]{:S(2)}) copy-start(f32[32]{0:T(128)} %get-tuple-element.319) | copy-start | bytes 388
  171.0 3.2 %copy-start.38 = (f32[32]{0:T(128)S(1)}, f32[32]{0:T(128)}, u32[]{:S(2)}) copy-start(f32[32]{0:T(128)} %get-tuple-element.320) | copy-start | bytes 388
  171.0 3.2 %copy-start.39 = (f32[32]{0:T(128)S(1)}, f32[32]{0:T(128)}, u32[]{:S(2)}) copy-start(f32[32]{0:T(128)} %get-tuple-element.321) | copy-start | bytes 388
  171.0 3.2 %copy-start.40 = (f32[32]{0:T(128)S(1)}, f32[32]{0:T(128)}, u32[]{:S(2)}) copy-start(f32[32]{0:T(128)} %get-tuple-element.322) | copy-start | bytes 388
  171.0 3.2 %copy-start.41 = (f32[32]{0:T(128)S(1)}, f32[32]{0:T(128)}, u32[]{:S(2)}) copy-start(f32[32]{0:T(128)} %get-tuple-element.323) | copy-start | bytes 388
  171.0 3.2 %copy-start.42 = (f32[32]{0:T(128)S(1)}, f32[32]{0:T(128)}, u32[]{:S(2)}) copy-start(f32[32]{0:T(128)} %get-tuple-element.324) | copy-start | bytes 388
  171.0 3.2 %copy-start.43 = (f32[32]{0:T(128)S(1)}, f32[32]{0:T(128)}, u32[]{:S(2)}) copy-start(f32[32]{0:T(128)} %get-tuple-element.325) | copy-start | bytes 388
  171.0 3.2 %copy-start.44 = (f32[32]{0:T(128)S(1)}, f32[32]{0:T(128)}, u32[]{:S(2)}) copy-start(f32[32]{0:T(128)} %get-tuple-element.326) | copy-start | bytes 388
  (7 other events, 5.8 us)
Sparse Core Ops, SparseCore 0:
  177.3 35.0 reduce-scatter.3
where the time goes:
time: 223 us; the launch traced here: 221 us
  other arithmetic  130 us (58%)
  waiting for transfers between devices  35.2 us (16%)
  between operations  16.1 us (7%)
  local copies, waits for them, and re-layouts  15.4 us (7%)
  blocking collectives  12.4 us (6%)
  matrix products  7.24 us (3%)
  starting transfers between devices  4.78 us (2%)
    unnamed x2, waiting for transfers between devices  35.2 us
    add x3, other arithmetic, per_device(): coef[basis, 0] + coef[basis, 1] * xcoord + coef[basis, 2] * ycoord  32.5 us
    mul x2, other arithmetic, per_device(): coef[basis, 2] * ycoord  23.6 us
    mul x2, other arithmetic, per_device(): coef[basis, 4] * xcoord * ycoord  22.6 us
    mul x2, other arithmetic, per_device(): coef[basis, 3] * xcoord * xcoord  22.6 us
    mul x2, other arithmetic, per_device(): coef[basis, 5] * ycoord * ycoord  16.5 us
    all_gather x1, blocking collectives, per_device(): gathered = lax.all_gather(template, 'visit', axis=2, tiled=True)  12.4 us
    dot_general x12, matrix products, per_device(): jnp.einsum('rs,jsc->jrc', rows_table, colconv[:degree + 1 - row_power], p...  5.21 us
  transfers between devices with their start and end apart: 3, of which 1 were waited for; matrix products, arithmetic and copies ran while one was open for 62% of the time, Pallas kernels for 0%

commit v1 on v0

v1 whole, which is shorter than its diff:
```python
import math

import jax
import jax.numpy as jnp
import numpy as np
from jax import lax
from jax.experimental import pallas as pl
from jax.experimental.pallas import tpu as pltpu
from jax.sharding import PartitionSpec as P

RAD = 10
EDGE = 16
SIGMAS = (1.0, 2.5, 5.0)
DEGREES = (4, 3, 2)
GROUP = 4
F32 = jnp.float32
BF16 = jnp.bfloat16


def taps(sigma, power):
    offsets = np.arange(-RAD, RAD + 1).astype(np.float64)
    bell = np.exp(-offsets * offsets / (2.0 * sigma * sigma))
    return bell / bell.sum() * (offsets / sigma) ** power


def band_matrix(positions, outs):
    tables = []
    for sigma, degree in zip(SIGMAS, DEGREES):
        for power in range(degree + 1):
            filt = taps(sigma, power)
            offset = positions[None, :] - np.arange(outs)[:, None]
            inside = np.abs(offset) <= RAD
            tables.append(np.where(inside, filt[np.clip(offset + RAD, 0, 2 * RAD)], 0.0))
    return np.stack(tables).astype(np.float32)


def split(array):
    high = array.astype(BF16)
    low = (array.astype(F32) - high.astype(F32)).astype(BF16)
    return high, low


def np_split(array):
    high = array.astype(jnp.bfloat16)
    low = (array - high.astype(np.float32)).astype(jnp.bfloat16)
    return high, low


def row_weights(rows):
    positions = np.concatenate(
        [np.arange(rows), np.arange(EDGE) - EDGE, rows + np.arange(EDGE)]
    )
    table = band_matrix(positions, rows).reshape(-1, rows + 2 * EDGE)
    high, low = np_split(table)
    return np.concatenate([high, high, low], axis=1)


def column_weights(cols, lanes):
    far = 10 * cols + 1000
    positions = np.concatenate(
        [
            np.arange(cols),
            np.arange(RAD) - RAD,
            cols + np.arange(RAD),
            np.full(lanes - cols - 2 * RAD, far),
        ]
    )
    table = band_matrix(positions, cols)
    count = table.shape[0]
    wide = np.zeros((GROUP, lanes, count, GROUP, cols), np.float32)
    for v in range(GROUP):
        wide[v, :, :, v, :] = table.transpose(2, 0, 1)
    return np_split(wide.reshape(GROUP * lanes, count * GROUP * cols))


def pack_kernel(
    visits, t_ref, n_ref, s_ref, sci_ref, var_ref, coef_ref, foot_ref, w_ref, band_ref, out_ref, own
):
    bands, rows, cols = t_ref.shape
    ext = rows + 2 * EDGE
    me = lax.axis_index("visit")
    lane = lax.broadcasted_iota(jnp.int32, (ext, 128), 1)
    for b in range(bands):
        own[b, 0:rows, 0:cols] = t_ref[b]
        own[b, rows : rows + EDGE, 0:cols] = n_ref[b]
        own[b, rows + EDGE : ext, 0:cols] = s_ref[b]
    left = jnp.zeros((ext, 128), F32)
    right = jnp.zeros((ext, 128), F32)
    for b in range(bands):
        tile = own[b]
        at = 64 + RAD * b
        here = (lane >= at) & (lane < at + RAD)
        left = jnp.where(here, pltpu.roll(tile, at, 1), left)
        right = jnp.where(here, pltpu.roll(tile, (at - (cols - RAD)) % 128, 1), right)
    weight = w_ref[0]
    tile_rows, tile_cols = foot_ref.shape[1], foot_ref.shape[2]
    foot = foot_ref[0].astype(F32)
    width = sci_ref.shape[2]
    side = rows // tile_rows
    span = width // tile_cols
    per = 128 // span
    tcol = lax.broadcasted_iota(jnp.int32, (tile_cols, 128), 0)
    tlane = lax.broadcasted_iota(jnp.int32, (tile_cols, 128), 1) // span
    band_value = band_ref[0].astype(F32)
    parts = []
    for chunk in range(width // 128):
        pick = jnp.where(tcol == tlane + chunk * per, 1.0, 0.0).astype(F32)
        cover = jnp.dot(foot, pick, preferred_element_type=F32)
        cover = jnp.concatenate(
            [jnp.broadcast_to(cover[k : k + 1], (side, 128)) for k in range(tile_rows)], axis=0
        )
        at = slice(chunk * 128, chunk * 128 + 128)
        scale = weight * cover / var_ref[0, :, at]
        parts.append((scale * sci_ref[0, :, at], scale))
    top = lane[:rows]
    zero = jnp.zeros((ext - rows, 128), F32)
    for d in range(visits):
        whole, inner = (d * cols) // 128, (d * cols) % 128
        first, second = parts[whole]
        pair = jnp.where(
            top < 32,
            pltpu.roll(first, (128 - inner) % 128, 1),
            pltpu.roll(second, (160 - inner) % 128, 1),
        )
        edge = jnp.where(d < me, left, right)
        out_ref[d] = jnp.where(lane < 64, jnp.concatenate([pair, zero], axis=0), edge)
        out_ref[d, rows : rows + coef_ref.shape[1], 0 : coef_ref.shape[2]] = coef_ref[0]
        out_ref[d, ext - 1 : ext, 0:64] = jnp.full((1, 64), band_value, F32)


def model_kernel(
    visits, quads, g_ref, t_ref, n_ref, s_ref, tab_ref, dh_ref, dl_ref, out_ref, own, acc
):
    bands, rows, cols = t_ref.shape
    ext = rows + 2 * EDGE
    width = visits * cols
    total = quads * rows
    me = lax.axis_index("visit")
    quad = lax.axis_index("quad")
    lane = lax.broadcasted_iota(jnp.int32, (ext, 128), 1)
    for b in range(bands):
        own[b, 0:rows, 0:cols] = t_ref[b]
        own[b, rows : rows + EDGE, 0:cols] = n_ref[b]
        own[b, rows + EDGE : ext, 0:cols] = s_ref[b]
    west = jnp.where(me > 0, g_ref[jnp.maximum(me - 1, 0)], 0.0)
    east = jnp.where(me < visits - 1, g_ref[jnp.minimum(me + 1, visits - 1)], 0.0)
    for b in range(bands):
        at = 64 + RAD * b
        tile = jnp.where(
            lane < cols,
            own[b],
            jnp.where(
                lane < cols + RAD,
                pltpu.roll(west, (cols - at) % 128, 1),
                jnp.where(
                    lane < cols + 2 * RAD, pltpu.roll(east, (cols + RAD - at) % 128, 1), 0.0
                ),
            ),
        )
        own[b] = jnp.where(lane < 64, tile, pltpu.roll(tile, 64, 1))
    tlane = lax.broadcasted_iota(jnp.int32, (rows, 128), 1)
    trow = lax.broadcasted_iota(jnp.int32, (rows, 128), 0)
    x = (((tlane % cols) + me * cols).astype(F32) + 0.5) / width * 2.0 - 1.0
    y = ((trow + quad * rows).astype(F32) + 0.5) / total * 2.0 - 1.0
    yy = y * y
    acc[...] = jnp.zeros_like(acc)

    def group(start):
        band_rows = [g_ref[start + v, ext - 1 : ext, :] for v in range(GROUP)]
        pairs = []
        for p in range(GROUP // 2):
            which = jnp.where(
                lane[:1] < 64, band_rows[2 * p], pltpu.roll(band_rows[2 * p + 1], 64, 1)
            )
            which = jnp.broadcast_to(which, (ext, 128))
            tile = jnp.zeros((ext, 128), F32)
            for b in range(bands):
                tile = jnp.where(which == float(b), own[b], tile)
            pairs.append(tile)
        high, low = split(jnp.concatenate(pairs, axis=1))
        rowed = jnp.dot(
            tab_ref[...], jnp.concatenate([high, low, high], axis=0), preferred_element_type=F32
        )
        rhigh, rlow = split(rowed)
        cmat = jnp.zeros((rows, 128), F32)
        first = jnp.zeros((rows, 128), F32)
        second = jnp.zeros((rows, 128), F32)
        which = jnp.zeros((1, 128), F32)
        for v in range(GROUP):
            here = (tlane >= v * cols) & (tlane < (v + 1) * cols)
            block = g_ref[start + v, 0:rows, :]
            coef = g_ref[start + v, rows : 2 * rows, :]
            first = jnp.where(here, pltpu.roll(block, v * cols, 1), first)
            second = jnp.where(here, pltpu.roll(block, (v * cols - 32) % 128, 1), second)
            cmat = jnp.where(here, pltpu.roll(coef, v * cols, 1), cmat)
            turned = band_rows[v] if v < 2 else pltpu.roll(band_rows[v], 64, 1)
            which = jnp.where(here[:1], turned, which)
        base = tlane - tlane % cols
        terms = [jnp.take_along_axis(cmat, base + s, axis=1) for s in range(6)]
        poly0 = terms[0] + x * (terms[1] + x * terms[3])
        poly1 = terms[2] + x * terms[4]
        poly2 = terms[5]
        model = jnp.zeros((rows, 128), F32)
        basis_start = 0
        filt = 0
        for degree in DEGREES:
            count = degree + 1
            index = {}
            k = basis_start
            for i in range(count):
                for j in range(count - i):
                    index[i, j] = k
                    k += 1
            for j0 in range(0, count, 2):
                js = range(j0, min(j0 + 2, count))
                tall = (count - j0) * rows
                at = slice((filt + j0) * 128, (filt + js[-1] + 1) * 128)
                dh, dl = dh_ref[:, at], dl_ref[:, at]
                rh = rhigh[filt * rows : filt * rows + tall]
                rl = rlow[filt * rows : filt * rows + tall]
                conv = (
                    jnp.dot(rh, dh, preferred_element_type=F32)
                    + jnp.dot(rl, dh, preferred_element_type=F32)
                    + jnp.dot(rh, dl, preferred_element_type=F32)
                )
                for j in js:
                    for i in range(count - j):
                        n = index[i, j]
                        part = conv[i * rows : (i + 1) * rows, (j - j0) * 128 : (j - j0 + 1) * 128]
                        spatial = (
                            poly0[n : n + 1] + y * poly1[n : n + 1] + yy * poly2[n : n + 1]
                        )
                        model = model + spatial * part
            basis_start = k
            filt += count
        term = first - second * model
        which = jnp.broadcast_to(which, (rows, 128))
        for b in range(bands):
            acc[b] += jnp.where(which == float(b), term, 0.0)

    if visits // GROUP <= 2:
        for g in range(visits // GROUP):
            group(g * GROUP)
    else:

        @pl.loop(0, visits // GROUP)
        def _(g):
            group(g * GROUP)

    for b in range(bands):
        half = acc[b] + pltpu.roll(acc[b], 64, 1)
        out_ref[b] = (half + pltpu.roll(half, 96, 1))[:, 0:cols]


def per_device(template, science, variance, coeffs, visit_weight, band, footprint):
    visits, quads = lax.axis_size("visit"), lax.axis_size("quad")
    bands, rows, cols = template.shape
    ext = rows + 2 * EDGE
    up = [(i, i + 1) for i in range(quads - 1)]
    down = [(i + 1, i) for i in range(quads - 1)]
    north = lax.ppermute(template[:, rows - EDGE :], "quad", up)
    south = lax.ppermute(template[:, :EDGE], "quad", down)
    vmem = pl.BlockSpec(memory_space=pltpu.VMEM)
    smem = pl.BlockSpec(memory_space=pltpu.SMEM)

    def packing(*refs):
        pack_kernel(visits, *refs)

    def modelling(*refs):
        model_kernel(visits, quads, *refs)

    blocks = pl.pallas_call(
        packing,
        out_shape=jax.ShapeDtypeStruct((visits, ext, 128), F32),
        in_specs=[vmem] * 7 + [smem] * 2,
        out_specs=vmem,
        scratch_shapes=[pltpu.VMEM((bands, ext, 128), F32)],
        name="pack",
    )(template, north, south, science, variance, coeffs, footprint, visit_weight, band)
    gathered = lax.all_to_all(blocks, "visit", 0, 0, tiled=True)
    table = jnp.asarray(row_weights(rows))
    dh, dl = column_weights(cols, 64)
    return pl.pallas_call(
        modelling,
        out_shape=jax.ShapeDtypeStruct((bands, rows, cols), F32),
        in_specs=[vmem] * 7,
        out_specs=vmem,
        scratch_shapes=[
            pltpu.VMEM((bands, ext, 128), F32),
            pltpu.VMEM((bands, rows, 128), F32),
        ],
        name="model",
    )(gathered, template, north, south, table, jnp.asarray(dh), jnp.asarray(dl))


def solution(mesh):
    placed = (
        P(None, "quad", "visit"),
        P("visit", "quad", None),
        P("visit", "quad", None),
        P("visit", None, None),
        P("visit"),
        P("visit"),
        P("visit", "quad", None),
    )
    return jax.shard_map(
        per_device, mesh=mesh, in_specs=placed, out_specs=P(None, "quad", "visit"), check_vma=False
    )
```

time: 223 us -> 28.2 us (0.13)
  other arithmetic: 130 us -> 0 us
  waiting for transfers between devices: 35.2 us -> 0.01 us
  between operations: 16.1 us -> 1.33 us
  local copies, waits for them, and re-layouts: 15.4 us -> 2.76 us
  matrix products: 7.24 us -> 0 us
  Pallas kernels: 0 us -> 5.66 us
    mul x14 -> x0, other arithmetic: 88 us -> none  [the longest x2 23.6 us: per_device(): coef[basis, 2] * ycoord]
    unnamed x2 -> x0, waiting for transfers between devices: 35.2 us -> none
    add x4 -> x0, other arithmetic: 32.5 us -> none  [the longest x3 32.5 us: per_device(): coef[basis, 0] + coef[basis, 1] * xcoord + coef[basis, 2] * ycoord]
    all_gather x1 -> x0, blocking collectives: 12.4 us -> none  [per_device(): gathered = lax.all_gather(template, 'visit', axis=2, tiled=True)]
    all_to_all x0 -> x1, blocking collectives: none -> 11.2 us  [per_device(): gathered = lax.all_to_all(blocks, 'visit', 0, 0, tiled=True)]
    slice x44 -> x1, local copies, waits for them, and re-layouts: 9.59 us -> 0.83 us  [per_device(): south = lax.ppermute(template[:, :EDGE], 'quad', down)]
    dot_general x15 -> x0, matrix products: 7.24 us -> none  [the longest x12 5.21 us: per_device(): jnp.einsum('rs,jsc->jrc', rows_table, colconv[:degree + 1 - row_power], p...]
    reduce_sum x5 -> x0, other arithmetic: 7.03 us -> none  [the longest x1 4.64 us: column_table(): tables.append(jnp.sum(hits * filter_taps(sigma, power, radius), axis=-1))]
  transfers between devices with their start and end apart: 3 -> 2, of which waited for: 1 -> 0; matrix products, arithmetic and copies ran while one was open for 62% -> 3% of each run, Pallas kernels for 0% -> 0%
where the time goes in v1:
time: 28.2 us; the launch traced here: 27.8 us
  blocking collectives  11.2 us (40%)
  starting transfers between devices  6.88 us (24%)
  Pallas kernels  5.66 us (20%)
  local copies, waits for them, and re-layouts  2.76 us (10%)
  between operations  1.33 us (5%)
    all_to_all x1, blocking collectives, per_device(): gathered = lax.all_to_all(blocks, 'visit', 0, 0, tiled=True)  11.2 us
    ppermute x1, starting transfers between devices, per_device(): north = lax.ppermute(template[:, rows - EDGE:], 'quad', up)  5.59 us
    pallas_call x1, Pallas kernels, per_device(): pl.pallas_call(modelling, out_shape=jax.ShapeDtypeStruct((bands, rows, co...  3.75 us
    unnamed x7, local copies, waits for them, and re-layouts  1.93 us
    pallas_call x1, Pallas kernels, per_device(): pl.pallas_call(packing, out_shape=jax.ShapeDtypeStruct((visits, ext, 128)...  1.91 us
    ppermute x1, starting transfers between devices, per_device(): south = lax.ppermute(template[:, :EDGE], 'quad', down)  1.29 us
    slice x1, local copies, waits for them, and re-layouts, per_device(): south = lax.ppermute(template[:, :EDGE], 'quad', down)  0.83 us
  transfers between devices with their start and end apart: 2, of which 0 were waited for; matrix products, arithmetic and copies ran while one was open for 3% of the time, Pallas kernels for 0%

profile of v1, /device:TPU:0, one launch (start us, length us, event | category | flops | bytes accessed | tf_op | source)
XLA Modules:
  0.0 27.8 jit_solution(14255788600622492004)
XLA Ops:
  0.0 0.8 %fusion = (f32[6,16,32]{2,1,0:T(8,128)S(1)}, f32[6,16,32]{2,1,0:T(8,128)S(1)}) fusion(f32[6,32,32]{2,1,0:T(8,128)} %refs_1_.1), kind=kLoop, calls=%fused_computation | loop fusion | bytes 49152 | tf_op jit(solution)/shard_map/slice | solution.py:262
  0.8 0.0 copy-start.2
  0.8 1.3 %collective-permute-start.1 = (f32[6,16,32]{2,1,0:T(8,128)S(1)}, f32[6,16,32]{2,1,0:T(8,128)S(1)}, u32[]{:S(2)}, u32[]{:S(2)}) collective-permute-start(f32[6,16,32]{2,1,0:T(8,128)S(1)} %get-tuple-element.5), channel_id=1, source_target_pairs={{1,0},{2,1},{3,2},{5,4},{6,5},{7,6},{9,8},{10,9},{11,10},{13,12},{... | collective-permute-start | bytes 36872 | tf_op jit(solution)/shard_map/ppermute | solution.py:262
  2.1 5.6 %collective-permute-start = (f32[6,16,32]{2,1,0:T(8,128)S(1)}, f32[6,16,32]{2,1,0:T(8,128)S(1)}, u32[]{:S(2)}, u32[]{:S(2)}) collective-permute-start(f32[6,16,32]{2,1,0:T(8,128)S(1)} %get-tuple-element.6), channel_id=1, source_target_pairs={{0,1},{1,2},{2,3},{4,5},{5,6},{6,7},{8,9},{9,10},{10,11},{12,13},{... | collective-permute-start | bytes 36872 | tf_op jit(solution)/shard_map/ppermute | solution.py:261
  9.0 0.0 copy-done.2
  9.0 0.7 %copy.11.refs_5_ = f32[1,31,6]{2,1,0:T(8,128)} copy(f32[1,31,6]{1,0,2:T(1,128)S(1)} %copy-done.2) | data formatting | bytes 1488 | tf_op args[3]
  9.7 0.0 collective-permute-done.1.refs_2_.refs_3_
  9.7 0.0 copy-start
  9.7 0.0 collective-permute-done.refs_1_.refs_2_
  9.7 0.6 %copy-done = f32[6,16,32]{2,1,0:T(8,128)} copy-done((f32[6,16,32]{2,1,0:T(8,128)}, f32[6,16,32]{2,1,0:T(8,128)S(1)}, u32[]{:S(2)}) %copy-start) | copy-done | bytes 12312
  10.4 0.0 copy-start.1
  10.4 0.6 %copy-done.1 = f32[6,16,32]{2,1,0:T(8,128)} copy-done((f32[6,16,32]{2,1,0:T(8,128)}, f32[6,16,32]{2,1,0:T(8,128)S(1)}, u32[]{:S(2)}) %copy-start.1) | copy-done | bytes 12312
  11.0 1.9 %pack.1 = f32[8,64,128]{2,1,0:T(8,128)} custom-call(f32[6,32,32]{2,1,0:T(8,128)} %refs_1_.1, f32[6,16,32]{2,1,0:T(8,128)} %copy-done.1, f32[6,16,32]{2,1,0:T(8,128)} %copy-done, f32[1,32,256]{2,1,0:T(8,128)} %refs_3_.1, f32[1,32,256]{2,1,0:T(8,128)} %refs_4_.2, f32[1,31,6]{2,1,0:T(8,128)} %copy.11.refs_5_, s32[1,2,16]{2,1,0:T(2,128)} %refs_6_.2, ...), custom_call_target="tpu_custom_call" | custom-call | tf_op jit(solution)/shard_map/pack/pallas_call | solution.py:272
  12.9 11.2 %all_to_all.5.refs_0_ = f32[8,64,128]{2,1,0:T(8,128)} all-to-all(f32[8,64,128]{2,1,0:T(8,128)} %pack.1), channel_id=1, replica_groups=mesh['visit'=8,'quad'=4] {'visit'}, dimensions={0} | all-to-all | bytes 524288 | tf_op jit(solution)/shard_map/all_to_all | solution.py:280
  24.0 3.7 %model.1 = f32[6,32,32]{2,1,0:T(8,128)} custom-call(f32[8,64,128]{2,1,0:T(8,128)} %all_to_all.5.refs_0_, f32[6,32,32]{2,1,0:T(8,128)} %refs_1_.1, f32[6,16,32]{2,1,0:T(8,128)} %copy-done.1, f32[6,16,32]{2,1,0:T(8,128)} %copy-done, bf16[384,192]{1,0:T(8,128)(2,1)} %constant.6.clone.refs_4_, bf16[256,1536]{1,0:T(8,128)(2,1)} %constant.7.clone.refs_5_, ...), custom_call_target="tpu_custom_call" | custom-call | tf_op jit(solution)/shard_map/model/pallas_call | solution.py:283
Async XLA Ops:
  0.8 8.2 %copy-start.2 = (f32[1,31,6]{1,0,2:T(1,128)S(1)}, f32[1,31,6]{1,0,2:T(1,128)}, u32[]{:S(2)}) copy-start(f32[1,31,6]{1,0,2:T(1,128)} %param.13) | copy-start | bytes 2236
  0.8 8.9 %collective-permute-start.1 = (f32[6,16,32]{2,1,0:T(8,128)S(1)}, f32[6,16,32]{2,1,0:T(8,128)S(1)}, u32[]{:S(2)}, u32[]{:S(2)}) collective-permute-start(f32[6,16,32]{2,1,0:T(8,128)S(1)} %get-tuple-element.5), channel_id=1, source_target_pairs={{1,0},{2,1},{3,2},{5,4},{6,5},{7,6},{9,8},{10,9},{11,10},{13,12},{... | collective-permute-start | bytes 36872 | tf_op jit(solution)/shard_map/ppermute | solution.py:262
  2.1 7.6 %collective-permute-start = (f32[6,16,32]{2,1,0:T(8,128)S(1)}, f32[6,16,32]{2,1,0:T(8,128)S(1)}, u32[]{:S(2)}, u32[]{:S(2)}) collective-permute-start(f32[6,16,32]{2,1,0:T(8,128)S(1)} %get-tuple-element.6), channel_id=1, source_target_pairs={{0,1},{1,2},{2,3},{4,5},{5,6},{6,7},{8,9},{9,10},{10,11},{12,13},{... | collective-permute-start | bytes 36872 | tf_op jit(solution)/shard_map/ppermute | solution.py:261
  9.7 0.6 %copy-start = (f32[6,16,32]{2,1,0:T(8,128)}, f32[6,16,32]{2,1,0:T(8,128)S(1)}, u32[]{:S(2)}) copy-start(f32[6,16,32]{2,1,0:T(8,128)S(1)} %collective-permute-done.1.refs_2_.refs_3_) | copy-start | bytes 36868
  10.4 0.6 %copy-start.1 = (f32[6,16,32]{2,1,0:T(8,128)}, f32[6,16,32]{2,1,0:T(8,128)S(1)}, u32[]{:S(2)}) copy-start(f32[6,16,32]{2,1,0:T(8,128)S(1)} %collective-permute-done.refs_1_.refs_2_) | copy-start | bytes 36868

commit v2 on v1

--- a/solution.py
+++ b/solution.py
@@ -1,5 +1,3 @@
-import math
-
 import jax
 import jax.numpy as jnp
 import numpy as np
@@ -7,6 +5,7 @@
 from jax.experimental import pallas as pl
 from jax.experimental.pallas import tpu as pltpu
 from jax.sharding import PartitionSpec as P
+
 
 RAD = 10
 EDGE = 16
@@ -73,26 +72,42 @@
     return np_split(wide.reshape(GROUP * lanes, count * GROUP * cols))
 
 
-def pack_kernel(
-    visits, t_ref, n_ref, s_ref, sci_ref, var_ref, coef_ref, foot_ref, w_ref, band_ref, out_ref, own
-):
+def lanes_of(shape):
+    return lax.broadcasted_iota(jnp.int32, shape, 1)
+
+
+def load_kernel(count, *refs):
+    sources, core_ref, other_ref = refs[:count], refs[count], refs[count + 1]
+    targets, sems, tile_ref = refs[count + 2 : -2], refs[-2], refs[-1]
+    copies = [
+        pltpu.make_async_copy(a, b, sems.at[i]) for i, (a, b) in enumerate(zip(sources, targets))
+    ]
+    for copy in copies:
+        copy.start()
+    for copy in copies:
+        copy.wait()
+    t_ref = targets[0]
     bands, rows, cols = t_ref.shape
-    ext = rows + 2 * EDGE
-    me = lax.axis_index("visit")
-    lane = lax.broadcasted_iota(jnp.int32, (ext, 128), 1)
+    lane = lanes_of((rows, 128))
+    left = jnp.zeros((rows, 128), F32)
+    right = jnp.zeros((rows, 128), F32)
     for b in range(bands):
-        own[b, 0:rows, 0:cols] = t_ref[b]
-        own[b, rows : rows + EDGE, 0:cols] = n_ref[b]
-        own[b, rows + EDGE : ext, 0:cols] = s_ref[b]
-    left = jnp.zeros((ext, 128), F32)
-    right = jnp.zeros((ext, 128), F32)
-    for b in range(bands):
-        tile = own[b]
-        at = 64 + RAD * b
+        tile_ref[0:rows, 0:cols] = t_ref[b]
+        tile = tile_ref[...]
+        at = RAD * b
         here = (lane >= at) & (lane < at + RAD)
         left = jnp.where(here, pltpu.roll(tile, at, 1), left)
         right = jnp.where(here, pltpu.roll(tile, (at - (cols - RAD)) % 128, 1), right)
-    weight = w_ref[0]
+    even = lax.axis_index("visit") % 2 == 0
+    core_ref[...] = jnp.where(even, right, left)
+    other_ref[...] = jnp.where(even, left, right)
+
+
+def pack_kernel(visits, cols, sci_ref, var_ref, coef_ref, foot_ref, meta_ref, out_ref):
+    rows = sci_ref.shape[1]
+    lane = lanes_of((rows, 128))
+    weight = jnp.broadcast_to(meta_ref[:, 0:1], (rows, 128))
+    which = jnp.broadcast_to(meta_ref[:, 1:2], (1, 64))
     tile_rows, tile_cols = foot_ref.shape[1], foot_ref.shape[2]
     foot = foot_ref[0].astype(F32)
     width = sci_ref.shape[2]
@@ -100,8 +115,7 @@
     span = width // tile_cols
     per = 128 // span
     tcol = lax.broadcasted_iota(jnp.int32, (tile_cols, 128), 0)
-    tlane = lax.broadcasted_iota(jnp.int32, (tile_cols, 128), 1) // span
-    band_value = band_ref[0].astype(F32)
+    tlane = lanes_of((tile_cols, 128)) // span
     parts = []
     for chunk in range(width // 128):
         pick = jnp.where(tcol == tlane + chunk * per, 1.0, 0.0).astype(F32)
@@ -112,43 +126,35 @@
         at = slice(chunk * 128, chunk * 128 + 128)
         scale = weight * cover / var_ref[0, :, at]
         parts.append((scale * sci_ref[0, :, at], scale))
-    top = lane[:rows]
-    zero = jnp.zeros((ext - rows, 128), F32)
+    coef = coef_ref[:, 0, :]
+    terms, basis = coef.shape
     for d in range(visits):
         whole, inner = (d * cols) // 128, (d * cols) % 128
         first, second = parts[whole]
-        pair = jnp.where(
-            top < 32,
+        out_ref[d] = jnp.where(
+            lane < 32,
             pltpu.roll(first, (128 - inner) % 128, 1),
             pltpu.roll(second, (160 - inner) % 128, 1),
         )
-        edge = jnp.where(d < me, left, right)
-        out_ref[d] = jnp.where(lane < 64, jnp.concatenate([pair, zero], axis=0), edge)
-        out_ref[d, rows : rows + coef_ref.shape[1], 0 : coef_ref.shape[2]] = coef_ref[0]
-        out_ref[d, ext - 1 : ext, 0:64] = jnp.full((1, 64), band_value, F32)
-
-
-def model_kernel(
-    visits, quads, g_ref, t_ref, n_ref, s_ref, tab_ref, dh_ref, dl_ref, out_ref, own, acc
-):
+        for s in range(terms):
+            out_ref[d, s : s + 1, 64 : 64 + basis] = coef[s : s + 1]
+        out_ref[d, 8:9, 64:128] = which
+
+
+def widen_kernel(t_ref, core_ref, other_ref, near_ref, first_ref, second_ref):
     bands, rows, cols = t_ref.shape
-    ext = rows + 2 * EDGE
-    width = visits * cols
-    total = quads * rows
-    me = lax.axis_index("visit")
-    quad = lax.axis_index("quad")
-    lane = lax.broadcasted_iota(jnp.int32, (ext, 128), 1)
+    lane = lanes_of((rows, 128))
+    even = lax.axis_index("visit") % 2 == 0
+    upper = lax.axis_index("quad") % 2 == 0
+    core, other = core_ref[...], other_ref[...]
+    west = jnp.where(even, other, core)
+    east = jnp.where(even, core, other)
+    near_ref[:, :, 0:cols] = t_ref[...]
     for b in range(bands):
-        own[b, 0:rows, 0:cols] = t_ref[b]
-        own[b, rows : rows + EDGE, 0:cols] = n_ref[b]
-        own[b, rows + EDGE : ext, 0:cols] = s_ref[b]
-    west = jnp.where(me > 0, g_ref[jnp.maximum(me - 1, 0)], 0.0)
-    east = jnp.where(me < visits - 1, g_ref[jnp.minimum(me + 1, visits - 1)], 0.0)
-    for b in range(bands):
-        at = 64 + RAD * b
+        at = RAD * b
         tile = jnp.where(
             lane < cols,
-            own[b],
+            near_ref[b],
             jnp.where(
                 lane < cols + RAD,
                 pltpu.roll(west, (cols - at) % 128, 1),
@@ -157,21 +163,62 @@
                 ),
             ),
         )
-        own[b] = jnp.where(lane < 64, tile, pltpu.roll(tile, 64, 1))
-    tlane = lax.broadcasted_iota(jnp.int32, (rows, 128), 1)
+        tile = jnp.where(lane < 64, tile, pltpu.roll(tile, 64, 1))
+        near_ref[b] = tile
+        last, leading = tile[rows - EDGE :], tile[:EDGE]
+        first_ref[b] = jnp.where(upper, last, leading)
+        second_ref[b] = jnp.where(upper, leading, last)
+
+
+def model_kernel(
+    visits,
+    quads,
+    g_ref,
+    near_ref,
+    a_ref,
+    b_ref,
+    tab_hbm,
+    dh_hbm,
+    dl_hbm,
+    out_ref,
+    own,
+    acc,
+    tab_ref,
+    dh_ref,
+    dl_ref,
+    sems,
+):
+    tables = ((tab_hbm, tab_ref), (dh_hbm, dh_ref), (dl_hbm, dl_ref))
+    copies = [pltpu.make_async_copy(a, b, sems.at[i]) for i, (a, b) in enumerate(tables)]
+    for copy in copies:
+        copy.start()
+    bands, rows, cols = out_ref.shape
+    ext = rows + 2 * EDGE
+    width = visits * cols
+    total = quads * rows
+    me = lax.axis_index("visit")
+    quad = lax.axis_index("quad")
+    lane = lanes_of((ext, 128))
+    upper = quad % 2 == 0
+    for b in range(bands):
+        own[b, 0:rows] = near_ref[b]
+        own[b, rows : rows + EDGE] = jnp.where(upper, b_ref[b], a_ref[b])
+        own[b, rows + EDGE : ext] = jnp.where(upper, a_ref[b], b_ref[b])
+    tlane = lanes_of((rows, 128))
     trow = lax.broadcasted_iota(jnp.int32, (rows, 128), 0)
     x = (((tlane % cols) + me * cols).astype(F32) + 0.5) / width * 2.0 - 1.0
     y = ((trow + quad * rows).astype(F32) + 0.5) / total * 2.0 - 1.0
     yy = y * y
     acc[...] = jnp.zeros_like(acc)
+    for copy in copies:
+        copy.wait()
 
     def group(start):
-        band_rows = [g_ref[start + v, ext - 1 : ext, :] for v in range(GROUP)]
+        high_rows = [g_ref[start + v, 8:9, :] for v in range(GROUP)]
+        low_rows = [pltpu.roll(row, 64, 1) for row in high_rows]
         pairs = []
         for p in range(GROUP // 2):
-            which = jnp.where(
-                lane[:1] < 64, band_rows[2 * p], pltpu.roll(band_rows[2 * p + 1], 64, 1)
-            )
+            which = jnp.where(lane[:1] < 64, low_rows[2 * p], high_rows[2 * p + 1])
             which = jnp.broadcast_to(which, (ext, 128))
             tile = jnp.zeros((ext, 128), F32)
             for b in range(bands):
@@ -182,20 +229,21 @@
             tab_ref[...], jnp.concatenate([high, low, high], axis=0), preferred_element_type=F32
         )
         rhigh, rlow = split(rowed)
-        cmat = jnp.zeros((rows, 128), F32)
         first = jnp.zeros((rows, 128), F32)
         second = jnp.zeros((rows, 128), F32)
         which = jnp.zeros((1, 128), F32)
+        packed = []
         for v in range(GROUP):
             here = (tlane >= v * cols) & (tlane < (v + 1) * cols)
-            block = g_ref[start + v, 0:rows, :]
-            coef = g_ref[start + v, rows : 2 * rows, :]
+            block = g_ref[start + v]
             first = jnp.where(here, pltpu.roll(block, v * cols, 1), first)
             second = jnp.where(here, pltpu.roll(block, (v * cols - 32) % 128, 1), second)
-            cmat = jnp.where(here, pltpu.roll(coef, v * cols, 1), cmat)
-            turned = band_rows[v] if v < 2 else pltpu.roll(band_rows[v], 64, 1)
+            packed.append(pltpu.roll(block[0:8], 64, 1))
+            turned = low_rows[v] if v < 2 else high_rows[v]
             which = jnp.where(here[:1], turned, which)
-        base = tlane - tlane % cols
+        packed.append(jnp.zeros((128 - 8 * GROUP, 128), F32))
+        cmat = jnp.transpose(jnp.concatenate(packed, axis=0))[0:rows]
+        base = 8 * (tlane // cols)
         terms = [jnp.take_along_axis(cmat, base + s, axis=1) for s in range(6)]
         poly0 = terms[0] + x * (terms[1] + x * terms[3])
         poly1 = terms[2] + x * terms[4]
@@ -252,45 +300,90 @@
         out_ref[b] = (half + pltpu.roll(half, 96, 1))[:, 0:cols]
 
 
+def swaps(count, start):
+    pairs = [(i, i + 1) for i in range(start, count - 1, 2)]
+    return pairs + [(j, i) for i, j in pairs]
+
+
+def stay(array):
+    return pltpu.with_memory_space_constraint(array, pltpu.HBM)
+
+
 def per_device(template, science, variance, coeffs, visit_weight, band, footprint):
     visits, quads = lax.axis_size("visit"), lax.axis_size("quad")
     bands, rows, cols = template.shape
     ext = rows + 2 * EDGE
-    up = [(i, i + 1) for i in range(quads - 1)]
-    down = [(i + 1, i) for i in range(quads - 1)]
-    north = lax.ppermute(template[:, rows - EDGE :], "quad", up)
-    south = lax.ppermute(template[:, :EDGE], "quad", down)
     vmem = pl.BlockSpec(memory_space=pltpu.VMEM)
-    smem = pl.BlockSpec(memory_space=pltpu.SMEM)
+    hbm = pl.BlockSpec(memory_space=pltpu.HBM)
+    params = pltpu.CompilerParams(vmem_limit_bytes=24 * 1024 * 1024)
 
     def packing(*refs):
-        pack_kernel(visits, *refs)
+        pack_kernel(visits, cols, *refs)
 
     def modelling(*refs):
         model_kernel(visits, quads, *refs)
 
+    turned = jnp.transpose(coeffs, (2, 0, 1))
+    sources = [stay(array) for array in (template, science, variance, turned, footprint)]
+    strip = jax.ShapeDtypeStruct((rows, 128), F32)
+
+    def loading(*refs):
+        load_kernel(len(sources), *refs)
+
+    to_core, to_other, tile, *loaded = pl.pallas_call(
+        loading,
+        out_shape=[strip, strip] + [jax.ShapeDtypeStruct(a.shape, a.dtype) for a in sources],
+        in_specs=[hbm] * len(sources),
+        out_specs=[vmem] * (2 + len(sources)),
+        scratch_shapes=[
+            pltpu.SemaphoreType.DMA((len(sources),)),
+            pltpu.VMEM((rows, 128), F32),
+        ],
+        compiler_params=params,
+        name="load",
+    )(*sources)
+    core = lax.ppermute(to_core, "visit", swaps(visits, 0))
+    other = lax.ppermute(to_other, "visit", swaps(visits, 1))
+    meta = lax.pad(visit_weight, np.float32(0), ((0, 127, 0),)) + lax.pad(
+        band.astype(F32), np.float32(0), ((1, 126, 0),)
+    )
     blocks = pl.pallas_call(
         packing,
-        out_shape=jax.ShapeDtypeStruct((visits, ext, 128), F32),
-        in_specs=[vmem] * 7 + [smem] * 2,
+        out_shape=jax.ShapeDtypeStruct((visits, rows, 128), F32),
+        in_specs=[vmem] * 5,
         out_specs=vmem,
-        scratch_shapes=[pltpu.VMEM((bands, ext, 128), F32)],
+        compiler_params=params,
         name="pack",
-    )(template, north, south, science, variance, coeffs, footprint, visit_weight, band)
+    )(*loaded, meta[None])
     gathered = lax.all_to_all(blocks, "visit", 0, 0, tiled=True)
-    table = jnp.asarray(row_weights(rows))
-    dh, dl = column_weights(cols, 64)
+    edge = jax.ShapeDtypeStruct((bands, EDGE, 128), F32)
+    near, first, second = pl.pallas_call(
+        widen_kernel,
+        out_shape=(jax.ShapeDtypeStruct((bands, rows, 128), F32), edge, edge),
+        in_specs=[vmem] * 3,
+        out_specs=[vmem] * 3,
+        compiler_params=params,
+        name="widen",
+    )(tile, core, other)
+    halo_a = lax.ppermute(first, "quad", swaps(quads, 0))
+    halo_b = lax.ppermute(second, "quad", swaps(quads, 1))
+    tables = [
+        stay(jnp.asarray(array)) for array in (row_weights(rows),) + column_weights(cols, 64)
+    ]
     return pl.pallas_call(
         modelling,
         out_shape=jax.ShapeDtypeStruct((bands, rows, cols), F32),
-        in_specs=[vmem] * 7,
+        in_specs=[vmem] * 4 + [hbm] * 3,
         out_specs=vmem,
         scratch_shapes=[
             pltpu.VMEM((bands, ext, 128), F32),
             pltpu.VMEM((bands, rows, 128), F32),
-        ],
+        ]
+        + [pltpu.VMEM(a.shape, a.dtype) for a in tables]
+        + [pltpu.SemaphoreType.DMA((3,))],
+        compiler_params=params,
         name="model",
-    )(gathered, template, north, south, table, jnp.asarray(dh), jnp.asarray(dl))
+    )(gathered, near, halo_a, halo_b, *tables)
 
 
 def solution(mesh):

time: 28.2 us -> 25.2 us (0.89)
  the two profiles are of different devices: /device:TPU:0 before, /device:TPU:20 now
where the time goes in v2:
time: 25.2 us; the launch traced here: 24.9 us
  starting transfers between devices  11.2 us (44%)
  waiting for transfers between devices  6.63 us (26%)
  Pallas kernels  5.63 us (22%)
  between operations  1.34 us (5%)
    all_to_all x1, starting transfers between devices, per_device(): gathered = lax.all_to_all(blocks, 'visit', 0, 0, tiled=True)  4.23 us
    pallas_call x1, Pallas kernels, per_device(): pl.pallas_call(modelling, out_shape=jax.ShapeDtypeStruct((bands, rows, co...  3.47 us
    ppermute x1, waiting for transfers between devices, per_device(): halo_b = lax.ppermute(second, 'quad', swaps(quads, 1))  3.46 us
    ppermute x1, starting transfers between devices, per_device(): other = lax.ppermute(to_other, 'visit', swaps(visits, 1))  3.36 us
    ppermute x1, waiting for transfers between devices, per_device(): other = lax.ppermute(to_other, 'visit', swaps(visits, 1))  2.57 us
    ppermute x1, starting transfers between devices, per_device(): halo_b = lax.ppermute(second, 'quad', swaps(quads, 1))  1.91 us
    ppermute x1, starting transfers between devices, per_device(): halo_a = lax.ppermute(first, 'quad', swaps(quads, 0))  1.64 us
    pallas_call x1, Pallas kernels, per_device(): pl.pallas_call(loading, out_shape=[strip, strip] + [jax.ShapeDtypeStruct(...  1.07 us
  transfers between devices with their start and end apart: 5, of which 3 were waited for; matrix products, arithmetic and copies ran while one was open for 0% of the time, Pallas kernels for 1%

profile of v2, /device:TPU:20, one launch (start us, length us, event | category | flops | bytes accessed | tf_op | source)
XLA Modules:
  0.0 24.9 jit_solution(2647380928078374673)
XLA Ops:
  1.3 0.1 add_bitcast_fusion.refs_4_
  1.4 1.1 %load.1 = (f32[32,128]{1,0:T(8,128)S(1)}, f32[32,128]{1,0:T(8,128)S(1)}, f32[6,32,32]{2,1,0:T(8,128)S(1)}, f32[1,32,256]{2,1,0:T(8,128)S(1)}, f32[1,32,256]{2,1,...) custom-call(f32[6,32,32]{2,1,0:T(8,128)} %refs_0_.1, f32[1,32,256]{2,1,0:T(8,128)} %refs_1_.1, ...), custom_call_target="tpu_custom_call" | custom-call | tf_op jit(solution)/shard_map/load/pallas_call | solution.py:333
  2.5 0.9 %pack.1 = f32[8,32,128]{2,1,0:T(8,128)} custom-call(f32[1,32,256]{2,1,0:T(8,128)S(1)} %get-tuple-element.15.refs_0_, f32[1,32,256]{2,1,0:T(8,128)S(1)} %get-tuple-element.16.refs_1_, f32[6,1,31]{2,1,0:T(1,128)S(1)} %get-tuple-element.17.refs_2_, s32[1,2,16]{2,1,0:T(2,128)S(1)} %get-tuple-element.18.refs_3_, f32[1,128]{1,0:T(1,128)S(1)} %add_bitcast_fusion.refs_4_), custom_call_target="tpu_custom_call" | custom-call | tf_op jit(solution)/shard_map/pack/pallas_call | solution.py:350
  3.3 4.2 %all-to-all-start = ((f32[8,32,128]{2,1,0:T(8,128)}), f32[8,32,128]{2,1,0:T(8,128)S(1)}, u32[]{:S(2)}, u32[]{:S(2)}) async-start(f32[8,32,128]{2,1,0:T(8,128)} %pack.1), calls=%async_computation | async-start | bytes 262144 | tf_op jit(solution)/shard_map/all_to_all | solution.py:358
  7.6 0.1 collective-permute-start
  7.7 3.4 %collective-permute-start.1 = (f32[32,128]{1,0:T(8,128)S(1)}, f32[32,128]{1,0:T(8,128)S(1)}, u32[]{:S(2)}, u32[]{:S(2)}) collective-permute-start(f32[32,128]{1,0:T(8,128)S(1)} %get-tuple-element.21), channel_id=1, source_target_pairs={{4,8},{12,16},{20,24},{8,4},{16,12},{24,20},{5,9},{13,17},{21,25},... | collective-permute-start | bytes 49160 | tf_op jit(solution)/shard_map/ppermute | solution.py:346
  11.1 0.0 collective-permute-done.core_ref
  11.1 2.6 %collective-permute-done.1.other_ref = f32[32,128]{1,0:T(8,128)S(1)} collective-permute-done((f32[32,128]{1,0:T(8,128)S(1)}, f32[32,128]{1,0:T(8,128)S(1)}, u32[]{:S(2)}, u32[]{:S(2)}) %collective-permute-start.1) | collective-permute-done | bytes 16416 | tf_op jit(solution)/shard_map/ppermute | solution.py:346
  13.6 0.2 widen.1
  13.8 1.6 %collective-permute-start.2 = (f32[6,16,128]{2,1,0:T(8,128)S(1)}, f32[6,16,128]{2,1,0:T(8,128)S(1)}, u32[]{:S(2)}, u32[]{:S(2)}) collective-permute-start(f32[6,16,128]{2,1,0:T(8,128)S(1)} %get-tuple-element.23), channel_id=1, source_target_pairs={{0,1},{2,3},{1,0},{3,2},{4,5},{6,7},{5,4},{7,6},{8,9},{10,11},{9,8... | collective-permute-start | bytes 147464 | tf_op jit(solution)/shard_map/ppermute | solution.py:368
  15.5 1.9 %collective-permute-start.3 = (f32[6,16,128]{2,1,0:T(8,128)S(1)}, f32[6,16,128]{2,1,0:T(8,128)S(1)}, u32[]{:S(2)}, u32[]{:S(2)}) collective-permute-start(f32[6,16,128]{2,1,0:T(8,128)S(1)} %get-tuple-element.24), channel_id=1, source_target_pairs={{1,2},{2,1},{5,6},{6,5},{9,10},{10,9},{13,14},{14,13},{17,18},{18,... | collective-permute-start | bytes 147464 | tf_op jit(solution)/shard_map/ppermute | solution.py:369
  17.4 0.6 %collective-permute-done.2.refs_2_ = f32[6,16,128]{2,1,0:T(8,128)S(1)} collective-permute-done((f32[6,16,128]{2,1,0:T(8,128)S(1)}, f32[6,16,128]{2,1,0:T(8,128)S(1)}, u32[]{:S(2)}, u32[]{:S(2)}) %collective-permute-start.2) | collective-permute-done | bytes 49184 | tf_op jit(solution)/shard_map/ppermute | solution.py:368
  18.0 3.5 %collective-permute-done.3.refs_3_ = f32[6,16,128]{2,1,0:T(8,128)S(1)} collective-permute-done((f32[6,16,128]{2,1,0:T(8,128)S(1)}, f32[6,16,128]{2,1,0:T(8,128)S(1)}, u32[]{:S(2)}, u32[]{:S(2)}) %collective-permute-start.3) | collective-permute-done | bytes 49184 | tf_op jit(solution)/shard_map/ppermute | solution.py:369
  21.5 0.0 all-to-all-done.refs_0_
  21.5 3.5 %model.1 = f32[6,32,32]{2,1,0:T(8,128)} custom-call(f32[8,32,128]{2,1,0:T(8,128)S(1)} %all-to-all-done.refs_0_, f32[6,32,128]{2,1,0:T(8,128)S(1)} %get-tuple-element.22.refs_1_, f32[6,16,128]{2,1,0:T(8,128)S(1)} %collective-permute-done.2.refs_2_, f32[6,16,128]{2,1,0:T(8,128)S(1)} %collective-permute-done.3.refs_3_, bf16[384,192]{1,0:T(8,128)(2,1)} %constant.8.clone.refs_4_, ...), custom_call_target="tpu_custom_call" | custom-call | tf_op jit(solution)/shard_map/model/pallas_call | solution.py:373
Async XLA Ops:
  3.3 18.1 %all-to-all-start = ((f32[8,32,128]{2,1,0:T(8,128)}), f32[8,32,128]{2,1,0:T(8,128)S(1)}, u32[]{:S(2)}, u32[]{:S(2)}) async-start(f32[8,32,128]{2,1,0:T(8,128)} %pack.1), calls=%async_computation | async-start | bytes 262144 | tf_op jit(solution)/shard_map/all_to_all | solution.py:358
  7.6 3.5 %collective-permute-start = (f32[32,128]{1,0:T(8,128)S(1)}, f32[32,128]{1,0:T(8,128)S(1)}, u32[]{:S(2)}, u32[]{:S(2)}) collective-permute-start(f32[32,128]{1,0:T(8,128)S(1)} %get-tuple-element.20), channel_id=1, source_target_pairs={{0,4},{8,12},{16,20},{24,28},{4,0},{12,8},{20,16},{28,24},{1,5},{9... | collective-permute-start | bytes 49160 | tf_op jit(solution)/shard_map/ppermute | solution.py:345
  7.7 5.9 %collective-permute-start.1 = (f32[32,128]{1,0:T(8,128)S(1)}, f32[32,128]{1,0:T(8,128)S(1)}, u32[]{:S(2)}, u32[]{:S(2)}) collective-permute-start(f32[32,128]{1,0:T(8,128)S(1)} %get-tuple-element.21), channel_id=1, source_target_pairs={{4,8},{12,16},{20,24},{8,4},{16,12},{24,20},{5,9},{13,17},{21,25},... | collective-permute-start | bytes 49160 | tf_op jit(solution)/shard_map/ppermute | solution.py:346
  13.8 4.2 %collective-permute-start.2 = (f32[6,16,128]{2,1,0:T(8,128)S(1)}, f32[6,16,128]{2,1,0:T(8,128)S(1)}, u32[]{:S(2)}, u32[]{:S(2)}) collective-permute-start(f32[6,16,128]{2,1,0:T(8,128)S(1)} %get-tuple-element.23), channel_id=1, source_target_pairs={{0,1},{2,3},{1,0},{3,2},{4,5},{6,7},{5,4},{7,6},{8,9},{10,11},{9,8... | collective-permute-start | bytes 147464 | tf_op jit(solution)/shard_map/ppermute | solution.py:368
  15.5 6.0 %collective-permute-start.3 = (f32[6,16,128]{2,1,0:T(8,128)S(1)}, f32[6,16,128]{2,1,0:T(8,128)S(1)}, u32[]{:S(2)}, u32[]{:S(2)}) collective-permute-start(f32[6,16,128]{2,1,0:T(8,128)S(1)} %get-tuple-element.24), channel_id=1, source_target_pairs={{1,2},{2,1},{5,6},{6,5},{9,10},{10,9},{13,14},{14,13},{17,18},{18,... | collective-permute-start | bytes 147464 | tf_op jit(solution)/shard_map/ppermute | solution.py:369

commit v3 on v1

v3 whole, which is shorter than its diff:
```python
import functools

import jax
import jax.numpy as jnp
import numpy as np
from jax import lax
from jax.experimental import pallas as pl
from jax.experimental.pallas import tpu as pltpu
from jax.sharding import PartitionSpec as P


RAD = 10
EDGE = 16
SIGMAS = (1.0, 2.5, 5.0)
DEGREES = (4, 3, 2)
GROUP = 4
F32 = jnp.float32
BF16 = jnp.bfloat16


def taps(sigma, power):
    offsets = np.arange(-RAD, RAD + 1).astype(np.float64)
    bell = np.exp(-offsets * offsets / (2.0 * sigma * sigma))
    return bell / bell.sum() * (offsets / sigma) ** power


def band_matrix(positions, outs):
    tables = []
    for sigma, degree in zip(SIGMAS, DEGREES):
        for power in range(degree + 1):
            filt = taps(sigma, power)
            offset = positions[None, :] - np.arange(outs)[:, None]
            inside = np.abs(offset) <= RAD
            tables.append(np.where(inside, filt[np.clip(offset + RAD, 0, 2 * RAD)], 0.0))
    return np.stack(tables).astype(np.float32)


def split(array):
    high = array.astype(BF16)
    low = (array.astype(F32) - high.astype(F32)).astype(BF16)
    return high, low


def np_split(array):
    high = array.astype(jnp.bfloat16)
    low = (array - high.astype(np.float32)).astype(jnp.bfloat16)
    return high, low


def row_weights(rows):
    positions = np.concatenate(
        [np.arange(rows), np.arange(EDGE) - EDGE, rows + np.arange(EDGE)]
    )
    table = band_matrix(positions, rows).reshape(-1, rows + 2 * EDGE)
    high, low = np_split(table)
    return np.concatenate([high, high, low], axis=1)


def column_weights(cols, lanes):
    far = 10 * cols + 1000
    positions = np.concatenate(
        [
            np.arange(cols),
            np.arange(RAD) - RAD,
            cols + np.arange(RAD),
            np.full(lanes - cols - 2 * RAD, far),
        ]
    )
    table = band_matrix(positions, cols)
    count = table.shape[0]
    wide = np.zeros((GROUP, lanes, count, GROUP, cols), np.float32)
    for v in range(GROUP):
        wide[v, :, :, v, :] = table.transpose(2, 0, 1)
    return np_split(wide.reshape(GROUP * lanes, count * GROUP * cols))


def lanes_of(shape):
    return lax.broadcasted_iota(jnp.int32, shape, 1)


def packed(tiles, cols):
    lane = lanes_of(tiles[0].shape)
    out = []
    for b in range(0, len(tiles), GROUP):
        tile = tiles[b]
        for k in range(1, min(GROUP, len(tiles) - b)):
            tile = jnp.where(lane < k * cols, tile, pltpu.roll(tiles[b + k], k * cols, 1))
        out.append(tile)
    return out


def load_kernel(count, *refs):
    sources, refs = refs[:count], refs[count:]
    (first_ref, second_ref, wide_ref), refs = refs[:3], refs[3:]
    targets, (t_ref, sems) = refs[: count - 1], refs[count - 1 :]
    copies = [
        pltpu.make_async_copy(a, b, sems.at[i])
        for i, (a, b) in enumerate(zip(sources, (t_ref, *targets)))
    ]
    for copy in copies:
        copy.start()
    for copy in copies:
        copy.wait()
    bands, rows, cols = t_ref.shape
    even = lax.axis_index("quad") % 2 == 0
    wide_ref[:, :, 0:cols] = t_ref[...]
    for k, tile in enumerate(packed([wide_ref[b] for b in range(bands)], cols)):
        last, leading = tile[rows - EDGE :], tile[:EDGE]
        first_ref[k] = jnp.where(even, last, leading)
        second_ref[k] = jnp.where(even, leading, last)


def pack_kernel(
    visits, cols, sci_ref, var_ref, coef_ref, foot_ref, meta_ref, mine_ref, away_ref, blocks
):
    rows = sci_ref.shape[1]
    short = rows // 2
    chips = visits // 2
    me = lax.axis_index("visit")
    chip, side = me // 2, me % 2
    at = chips * short
    weight = jnp.broadcast_to(meta_ref[:, 0:1], (rows, 128))
    coef = coef_ref[:, 0, :]
    terms, basis = coef.shape
    which = jnp.broadcast_to(meta_ref[:, 1:2], (1, 128))
    for ref in (mine_ref, away_ref):
        ref[at : at + terms, 0:basis] = coef
        ref[at + terms : at + terms + 1] = which
    tile_rows, tile_cols = foot_ref.shape[1], foot_ref.shape[2]
    foot = foot_ref[0].astype(F32)
    width = sci_ref.shape[2]
    height = rows // tile_rows
    span = width // tile_cols
    per = 128 // span
    tcol = lax.broadcasted_iota(jnp.int32, (tile_cols, 128), 0)
    tlane = lanes_of((tile_cols, 128)) // span
    parts = []
    for chunk in range(width // 128):
        pick = jnp.where(tcol == tlane + chunk * per, 1.0, 0.0).astype(F32)
        cover = jnp.dot(foot, pick, preferred_element_type=F32)
        cover = jnp.concatenate(
            [jnp.broadcast_to(cover[k : k + 1], (height, 128)) for k in range(tile_rows)], axis=0
        )
        inside = slice(chunk * 128, chunk * 128 + 128)
        scale = weight * cover / var_ref[0, :, inside]
        parts.append((scale * sci_ref[0, :, inside], scale))
    flat = lanes_of((short, 128))
    for d in range(visits):
        whole, within = (d * cols) // 128, (d * cols) % 128
        first, second = parts[whole]
        pieces = (first[:short], first[short:], second[:short], second[short:])
        block = pltpu.roll(pieces[0], (128 - within) % 128, 1)
        for k in range(1, 4):
            turned = pltpu.roll(pieces[k], (128 + 32 * k - within) % 128, 1)
            block = jnp.where(flat < 32 * k, block, turned)
        blocks[d] = block
    for m in range(chips):
        other = chip ^ m
        mine_ref[m * short : (m + 1) * short] = blocks[2 * other + side]
        away_ref[m * short : (m + 1) * short] = blocks[2 * other + 1 - side]


def edge_kernel(cols, wide_ref, a_ref, b_ref, own_ref, out_ref):
    bands, rows, _ = wide_ref.shape
    ext = rows + 2 * EDGE
    lane = lanes_of((ext, 128))
    upper = lax.axis_index("quad") % 2 == 0
    left = jnp.zeros((ext, 128), F32)
    right = jnp.zeros((ext, 128), F32)
    for b in range(bands):
        halo = [
            pltpu.roll(ref[b // GROUP], (128 - (b % GROUP) * cols) % 128, 1)
            for ref in (a_ref, b_ref)
        ]
        north = jnp.where(upper, halo[1], halo[0])
        south = jnp.where(upper, halo[0], halo[1])
        tile = jnp.concatenate([wide_ref[b], north, south], axis=0)
        own_ref[b] = tile
        at = RAD * b
        here = (lane >= at) & (lane < at + RAD)
        left = jnp.where(here, pltpu.roll(tile, at, 1), left)
        right = jnp.where(here, pltpu.roll(tile, (at - (cols - RAD)) % 128, 1), right)
    even = lax.axis_index("visit") % 2 == 0
    inner = jnp.where(even, right, left)
    outer = jnp.where(even, left, right)
    out_ref[...] = jnp.where(lane < 64, inner, pltpu.roll(outer, 64, 1))


def merge_kernel(rows, steps, mine_ref, got_ref, edge_ref, *out_refs):
    chips = len(out_refs) + 1
    short = rows // 2
    base = chips * short
    half = lanes_of((rows, 128)) < 64
    middle = edge_ref.shape[0] // 2
    edge = jnp.where(
        half[:middle], pltpu.roll(edge_ref[:middle], 64, 1), edge_ref[middle:]
    )
    coefs = jnp.where(
        half[:8], mine_ref[base : base + 8], pltpu.roll(got_ref[base : base + 8], 64, 1)
    )
    for m in range(1, chips):
        out_ref = out_refs[m - 1]
        at = slice(m * short, (m + 1) * short)
        out_ref[0:short] = mine_ref[at]
        out_ref[short:rows] = got_ref[at]
        out_ref[rows : rows + 8] = coefs
        if m in steps:
            out_ref[rows + 8 : rows + 8 + middle] = edge


def table_kernel(*refs):
    refs, sems = refs[1:-1], refs[-1]
    count = len(refs) // 2
    copies = [
        pltpu.make_async_copy(refs[i], refs[count + i], sems.at[i]) for i in range(count)
    ]
    for copy in copies:
        copy.start()
    for copy in copies:
        copy.wait()


def choose(which, tiles):
    shape = tiles[0].shape
    which = jnp.broadcast_to(which, shape)
    picked = jnp.zeros(shape, F32)
    for b, tile in enumerate(tiles):
        picked = jnp.where(which == float(b), tile, picked)
    return picked


def model_kernel(
    visits, quads, steps, mine_ref, got_ref, own_ref, inner_ref, tab_ref, dh_ref, dl_ref, *refs
):
    message_refs, (out_ref, near) = refs[:-2], refs[-2:]
    bands, rows, cols = out_ref.shape
    short = rows // 2
    ext = rows + 2 * EDGE
    chips = visits // 2
    groups = visits // GROUP
    me = lax.axis_index("visit")
    quad = lax.axis_index("quad")
    chip = me // 2
    even = me % 2 == 0

    wide_lane = lanes_of((ext, 128))
    middle = ext // 2
    beside = jnp.where(even, chip - 1, chip + 1)
    exists = (beside >= 0) & (beside < chips)
    edge = jnp.zeros((middle, 128), F32)
    for m in steps:
        arrived = message_refs[m - 1][rows + 8 : rows + 8 + middle]
        edge = jnp.where(exists & ((chip ^ beside) == m), arrived, edge)
    outer = jnp.concatenate([edge, pltpu.roll(edge, 64, 1)], axis=0)
    inner = inner_ref[...]
    west = jnp.where(even, outer, inner)
    east = jnp.where(even, inner, outer)
    for b in range(bands):
        at = RAD * b
        tile = jnp.where(
            wide_lane < cols,
            own_ref[b],
            jnp.where(
                wide_lane < cols + RAD,
                pltpu.roll(west, (cols - at) % 128, 1),
                jnp.where(
                    wide_lane < cols + 2 * RAD,
                    pltpu.roll(east, (cols + RAD - at) % 128, 1),
                    0.0,
                ),
            ),
        )
        near[b] = jnp.where(wide_lane < 64, tile, pltpu.roll(tile, 64, 1))

    lane = lanes_of((rows, 128))
    flat = lane[:short]
    low_half = lane[:1] < 64
    x = (((lane % cols) + me * cols).astype(F32) + 0.5) / (visits * cols) * 2.0 - 1.0
    trow = lax.broadcasted_iota(jnp.int32, (rows, 256), 0)
    y = ((trow + quad * rows).astype(F32) + 0.5) / (quads * rows) * 2.0 - 1.0
    yy = y * y
    base = 8 * (lane // cols)
    base_row = chips * short
    slots = [
        (mine_ref, 0, mine_ref, base_row, False),
        (got_ref, 0, got_ref, base_row, False),
    ]
    for ref in message_refs:
        slots += [(ref, 0, ref, rows, False), (ref, short, ref, rows, True)]

    def gather(members):
        blocks, tails, band_rows = [], [], []
        for ref, at, tail_ref, tail_at, high in members:
            blocks.append(ref[at : at + short])
            tail = tail_ref[tail_at : tail_at + 8]
            turned = pltpu.roll(tail, 64, 1)
            tails.append(turned if high else tail)
            band_rows.append(jnp.where(low_half == (not high), tail[6:7], turned[6:7]))
        pieces = [jnp.zeros((short, 128), F32)] * 4
        which = jnp.zeros((1, 128), F32)
        for v in range(GROUP):
            here = (flat >= v * cols) & (flat < (v + 1) * cols)
            pieces = [
                jnp.where(here, pltpu.roll(blocks[v], (v * cols - 32 * k) % 128, 1), piece)
                for k, piece in enumerate(pieces)
            ]
            which = jnp.where(here[:1], band_rows[v], which)
        tails.append(jnp.zeros((128 - 8 * GROUP, 128), F32))
        cmat = jnp.transpose(jnp.concatenate(tails, axis=0))[0:rows]
        terms = [jnp.take_along_axis(cmat, base + s, axis=1) for s in range(6)]
        polys = (
            terms[0] + x * (terms[1] + x * terms[3]),
            terms[2] + x * terms[4],
            terms[5],
        )
        images = [
            choose(
                jnp.where(low_half, band_rows[2 * p], band_rows[2 * p + 1]),
                [near[b] for b in range(bands)],
            )
            for p in range(GROUP // 2)
        ]
        first = jnp.concatenate(pieces[:2], axis=0)
        second = jnp.concatenate(pieces[2:], axis=0)
        return polys, jnp.concatenate(images, axis=1), first, second, which

    totals = [jnp.zeros((rows, 128), F32) for _ in range(bands)]
    for start in range(0, groups, 2):
        pair = [gather(slots[g * GROUP : (g + 1) * GROUP]) for g in (start, start + 1)]
        parts = [split(image) for _, image, _, _, _ in pair]
        both = jnp.concatenate([p[0] for p in parts] + [p[1] for p in parts], axis=0)
        poly0, poly1, poly2 = [
            jnp.concatenate([pair[0][0][k], pair[1][0][k]], axis=1) for k in range(3)
        ]
        model = jnp.zeros((rows, 256), F32)
        basis_start = 0
        filt = 0
        for degree in DEGREES:
            count = degree + 1
            index = {}
            k = basis_start
            for i in range(count):
                for j in range(count - i):
                    index[i, j] = k
                    k += 1
            for j0 in range(0, count, 2):
                js = range(j0, min(j0 + 2, count))
                lanes = slice((filt + j0) * 128, (filt + js[-1] + 1) * 128)
                wide = jnp.dot(both, dh_ref[:, lanes], preferred_element_type=F32)
                conv = (
                    wide[: 2 * ext]
                    + wide[2 * ext :]
                    + jnp.dot(both[: 2 * ext], dl_ref[:, lanes], preferred_element_type=F32)
                )
                for j in js:
                    part = conv[:, (j - j0) * 128 : (j - j0 + 1) * 128]
                    part = jnp.concatenate([part[:ext], part[ext:]], axis=1)
                    high, low = split(part)
                    rowed = jnp.dot(
                        tab_ref[filt * rows : (filt + count - j) * rows],
                        jnp.concatenate([high, low, high], axis=0),
                        preferred_element_type=F32,
                    )
                    for i in range(count - j):
                        n = index[i, j]
                        spatial = (
                            poly0[n : n + 1] + y * poly1[n : n + 1] + yy * poly2[n : n + 1]
                        )
                        model = model + spatial * rowed[i * rows : (i + 1) * rows]
            basis_start = k
            filt += count
        for g in range(2):
            _, _, first, second, which = pair[g]
            part = first - second * model[:, g * 128 : (g + 1) * 128]
            which = jnp.broadcast_to(which, (rows, 128))
            for b in range(bands):
                totals[b] = totals[b] + jnp.where(which == float(b), part, 0.0)
    for b in range(bands):
        folded = totals[b] + pltpu.roll(totals[b], 64, 1)
        out_ref[b] = (folded + pltpu.roll(folded, 96, 1))[:, 0:cols]


def swaps(count, start):
    pairs = [(i, i + 1) for i in range(start, count - 1, 2)]
    return pairs + [(j, i) for i, j in pairs]


def stay(array):
    return pltpu.with_memory_space_constraint(array, pltpu.HBM)


def per_device(template, science, variance, coeffs, visit_weight, band, footprint):
    visits, quads = lax.axis_size("visit"), lax.axis_size("quad")
    chips = visits // 2
    bands, rows, cols = template.shape
    ext = rows + 2 * EDGE
    short = rows // 2
    vmem = pl.BlockSpec(memory_space=pltpu.VMEM)
    hbm = pl.BlockSpec(memory_space=pltpu.HBM)
    params = pltpu.CompilerParams(vmem_limit_bytes=24 * 1024 * 1024)
    struct = jax.ShapeDtypeStruct

    def call(kernel, outs, ins, scratch=()):
        return pl.pallas_call(
            kernel,
            out_shape=outs,
            in_specs=ins,
            out_specs=jax.tree.map(lambda _: vmem, outs),
            scratch_shapes=scratch,
            compiler_params=params,
        )

    turned = jnp.transpose(coeffs, (2, 0, 1))
    sources = [stay(array) for array in (template, science, variance, turned, footprint)]
    strip = struct((-(-bands // GROUP), EDGE, 128), F32)
    first, second, wide, *loaded = call(
        functools.partial(load_kernel, len(sources)),
        [strip, strip, struct((bands, rows, 128), F32)]
        + [struct(a.shape, a.dtype) for a in sources[1:]],
        [hbm] * 5,
        [pltpu.VMEM(template.shape, F32), pltpu.SemaphoreType.DMA((5,))],
    )(*sources)
    halo_a = lax.ppermute(first, "quad", swaps(quads, 0))
    halo_b = lax.ppermute(second, "quad", swaps(quads, 1))
    meta = lax.pad(visit_weight, np.float32(0), ((0, 127, 0),)) + lax.pad(
        band.astype(F32), np.float32(0), ((1, 126, 0),)
    )
    height = chips * short + 8
    mine, away = call(
        functools.partial(pack_kernel, visits, cols),
        [struct((height, 128), F32)] * 2,
        [vmem] * 5,
        [pltpu.VMEM((visits, short, 128), F32)],
    )(*loaded, meta[None])
    got = lax.ppermute(away, "visit", swaps(visits, 0))
    own, to_core = call(
        functools.partial(edge_kernel, cols),
        [struct((bands, ext, 128), F32), struct((ext, 128), F32)],
        [vmem] * 3,
    )(wide, halo_a, halo_b)
    edge = lax.ppermute(to_core, "visit", swaps(visits, 0))
    steps = sorted({c ^ (c + 1) for c in range(chips - 1)})
    outgoing = call(
        functools.partial(merge_kernel, rows, steps),
        [
            struct((rows + 8 + (ext // 2 if m in steps else 0), 128), F32)
            for m in range(1, chips)
        ],
        [vmem] * 3,
    )(mine, got, edge)
    incoming = [
        lax.ppermute(array, "visit", [(i, i ^ (2 * m)) for i in range(visits)])
        for m, array in enumerate(outgoing, 1)
    ]
    tables = [
        stay(jnp.asarray(array)) for array in (row_weights(rows),) + column_weights(cols, 64)
    ]
    tables = call(
        table_kernel,
        [struct(a.shape, a.dtype) for a in tables],
        [vmem] + [hbm] * 3,
        [pltpu.SemaphoreType.DMA((3,))],
    )(outgoing[0], *tables)
    return call(
        functools.partial(model_kernel, visits, quads, steps),
        struct((bands, rows, cols), F32),
        [vmem] * (7 + chips - 1),
        [pltpu.VMEM((bands, ext, 128), F32)],
    )(mine, got, own, edge, *tables, *incoming)


def solution(mesh):
    placed = (
        P(None, "quad", "visit"),
        P("visit", "quad", None),
        P("visit", "quad", None),
        P("visit", None, None),
        P("visit"),
        P("visit"),
        P("visit", "quad", None),
    )
    return jax.shard_map(
        per_device, mesh=mesh, in_specs=placed, out_specs=P(None, "quad", "visit"), check_vma=False
    )
```

time: 28.2 us -> 19.8 us (0.70)
  the two profiles are of different devices: /device:TPU:0 before, /device:TPU:18 now
where the time goes in v3:
time: 19.8 us; the launch traced here: 19.6 us
  starting transfers between devices  7.13 us (36%)
  Pallas kernels  6.07 us (31%)
  waiting for transfers between devices  4.95 us (25%)
  between operations  1.36 us (7%)
    ppermute x3, starting transfers between devices, per_device(): lax.ppermute(array, 'visit', [(i, i ^ 2 * m) for i in range(visits)])  3.49 us
    pallas_call x1, Pallas kernels, per_device(): call(functools.partial(model_kernel, visits, quads, steps), struct((bands...  2.94 us
    ppermute x1, waiting for transfers between devices, per_device(): halo_b = lax.ppermute(second, 'quad', swaps(quads, 1))  1.99 us
    ppermute x1, starting transfers between devices, per_device(): halo_b = lax.ppermute(second, 'quad', swaps(quads, 1))  1.91 us
    ppermute x3, waiting for transfers between devices, per_device(): lax.ppermute(array, 'visit', [(i, i ^ 2 * m) for i in range(visits)])  1.77 us
    ppermute x1, starting transfers between devices, per_device(): halo_a = lax.ppermute(first, 'quad', swaps(quads, 0))  1.64 us
    pallas_call x1, Pallas kernels, per_device(): call(table_kernel, [struct(a.shape, a.dtype) for a in tables], [vmem] + [...  1.5 us
    ppermute x1, waiting for transfers between devices, per_device(): edge = lax.ppermute(to_core, 'visit', swaps(visits, 0))  1.18 us
  transfers between devices with their start and end apart: 7, of which 3 were waited for; matrix products, arithmetic and copies ran while one was open for 0% of the time, Pallas kernels for 10%

profile of v3, /device:TPU:18, one launch (start us, length us, event | category | flops | bytes accessed | tf_op | source)
XLA Modules:
  0.0 19.6 jit_solution(1176719022456189976)
XLA Ops:
  0.0 1.0 %shard_map.100 = (f32[2,16,128]{2,1,0:T(8,128)S(1)}, f32[2,16,128]{2,1,0:T(8,128)S(1)}, f32[6,32,128]{2,1,0:T(8,128)S(1)}, f32[1,32,256]{2,1,0:T(8,128)S(1)}, f3...) custom-call(f32[6,32,32]{2,1,0:T(8,128)} %refs_0_.1, f32[1,32,256]{2,1,0:T(8,128)} %refs_1_.2, ...), custom_call_target="tpu_custom_call" | custom-call | tf_op jit(solution)/shard_map/pallas_call | solution.py:416
  1.0 1.6 %collective-permute-start.1 = (f32[2,16,128]{2,1,0:T(8,128)S(1)}, f32[2,16,128]{2,1,0:T(8,128)S(1)}, u32[]{:S(2)}, u32[]{:S(2)}) collective-permute-start(f32[2,16,128]{2,1,0:T(8,128)S(1)} %get-tuple-element.29), channel_id=1, source_target_pairs={{0,1},{2,3},{1,0},{3,2},{4,5},{6,7},{5,4},{7,6},{8,9},{10,11},{9,8... | collective-permute-start | bytes 49160 | tf_op jit(solution)/shard_map/ppermute | solution.py:423
  2.7 1.9 %collective-permute-start.2 = (f32[2,16,128]{2,1,0:T(8,128)S(1)}, f32[2,16,128]{2,1,0:T(8,128)S(1)}, u32[]{:S(2)}, u32[]{:S(2)}) collective-permute-start(f32[2,16,128]{2,1,0:T(8,128)S(1)} %get-tuple-element.30), channel_id=1, source_target_pairs={{1,2},{2,1},{5,6},{6,5},{9,10},{10,9},{13,14},{14,13},{17,18},{18,... | collective-permute-start | bytes 49160 | tf_op jit(solution)/shard_map/ppermute | solution.py:424
  5.9 0.1 add_bitcast_fusion.meta_ref
  6.0 0.2 %shard_map.101 = (f32[72,128]{1,0:T(8,128)S(1)}, f32[72,128]{1,0:T(8,128)S(1)}) custom-call(f32[1,32,256]{2,1,0:T(8,128)S(1)} %get-tuple-element.22.sci_ref, f32[1,32,256]{2,1,0:T(8,128)S(1)} %get-tuple-element.23.var_ref, f32[6,1,31]{2,1,0:T(1,128)S(1)} %get-tuple-element.24.coef_ref, s32[1,2,16]{2,1,0:T(2,128)S(1)} %get-tuple-element.25.foot_ref, ...), custom_call_target="tpu_custom_call" | custom-call | tf_op jit(solution)/shard_map/pallas_call | solution.py:429
  6.2 0.1 collective-permute-start
  6.3 0.0 collective-permute-done.1.a_ref
  6.3 2.0 %collective-permute-done.2.b_ref = f32[2,16,128]{2,1,0:T(8,128)S(1)} collective-permute-done((f32[2,16,128]{2,1,0:T(8,128)S(1)}, f32[2,16,128]{2,1,0:T(8,128)S(1)}, u32[]{:S(2)}, u32[]{:S(2)}) %collective-permute-start.2) | collective-permute-done | bytes 16416 | tf_op jit(solution)/shard_map/ppermute | solution.py:424
  8.3 0.3 %shard_map.102 = (f32[6,64,128]{2,1,0:T(8,128)S(1)}, f32[64,128]{1,0:T(8,128)S(1)}) custom-call(f32[6,32,128]{2,1,0:T(8,128)S(1)} %get-tuple-element.28.wide_ref, f32[2,16,128]{2,1,0:T(8,128)S(1)} %collective-permute-done.1.a_ref, f32[2,16,128]{2,1,0:T(8,128)S(1)} %collective-permute-done.2.b_ref), custom_call_target="tpu_custom_call" | custom-call | tf_op jit(solution)/shard_map/pallas_call | solution.py:436
  8.6 0.0 collective-permute-start.3
  8.6 0.0 collective-permute-done.got_ref
  8.6 1.2 %collective-permute-done.3.edge_ref.inner_ref = f32[64,128]{1,0:T(8,128)S(1)} collective-permute-done((f32[64,128]{1,0:T(8,128)S(1)}, f32[64,128]{1,0:T(8,128)S(1)}, u32[]{:S(2)}, u32[]{:S(2)}) %collective-permute-start.3) | collective-permute-done | bytes 32800 | tf_op jit(solution)/shard_map/ppermute | solution.py:441
  9.8 0.1 shard_map.103
  9.9 1.5 %collective-permute-start.6 = (f32[72,128]{1,0:T(8,128)S(1)}, f32[72,128]{1,0:T(8,128)S(1)}, u32[]{:S(2)}, u32[]{:S(2)}) collective-permute-start(f32[72,128]{1,0:T(8,128)S(1)} %get-tuple-element.38), channel_id=1, source_target_pairs={{0,24},{4,28},{8,16},{12,20},{16,8},{20,12},{24,0},{28,4},{1,25},{... | collective-permute-start | bytes 110600 | tf_op jit(solution)/shard_map/ppermute | solution.py:452
  11.4 1.5 %collective-permute-start.4 = (f32[72,128]{1,0:T(8,128)S(1)}, f32[72,128]{1,0:T(8,128)S(1)}, u32[]{:S(2)}, u32[]{:S(2)}) collective-permute-start(f32[72,128]{1,0:T(8,128)S(1)} %get-tuple-element.33.refs_0_), channel_id=1, source_target_pairs={{0,8},{4,12},{8,0},{12,4},{16,24},{20,28},{24,16},{28,20},{1,9},{5... | collective-permute-start | bytes 110600 | tf_op jit(solution)/shard_map/ppermute | solution.py:452
  12.9 0.5 %collective-permute-start.5 = (f32[40,128]{1,0:T(8,128)S(1)}, f32[40,128]{1,0:T(8,128)S(1)}, u32[]{:S(2)}, u32[]{:S(2)}) collective-permute-start(f32[40,128]{1,0:T(8,128)S(1)} %get-tuple-element.37), channel_id=1, source_target_pairs={{0,16},{4,20},{8,24},{12,28},{16,0},{20,4},{24,8},{28,12},{1,17},{... | collective-permute-start | bytes 61448 | tf_op jit(solution)/shard_map/ppermute | solution.py:452
  13.4 1.5 %shard_map.104 = (bf16[384,192]{1,0:T(8,128)(2,1)S(1)}, bf16[256,1536]{1,0:T(8,128)(2,1)S(1)}, bf16[256,1536]{1,0:T(8,128)(2,1)S(1)}) custom-call(f32[72,128]{1,0:T(8,128)S(1)} %get-tuple-element.33.refs_0_, bf16[384,192]{1,0:T(8,128)(2,1)} %constant.8.clone.refs_1_, bf16[256,1536]{1,0:T(8,128)(2,1)} %constant.9.clone.refs_2_, ...), custom_call_target="tpu_custom_call" | custom-call | tf_op jit(solution)/shard_map/pallas_call | solution.py:458
  14.9 1.8 %collective-permute-done.5.refs_1_ = f32[40,128]{1,0:T(8,128)S(1)} collective-permute-done((f32[40,128]{1,0:T(8,128)S(1)}, f32[40,128]{1,0:T(8,128)S(1)}, u32[]{:S(2)}, u32[]{:S(2)}) %collective-permute-start.5) | collective-permute-done | bytes 20512 | tf_op jit(solution)/shard_map/ppermute | solution.py:452
  16.6 0.0 collective-permute-done.6.refs_2_
  16.6 0.0 collective-permute-done.4.refs_0_
  16.7 2.9 %shard_map.105 = f32[6,32,32]{2,1,0:T(8,128)} custom-call(f32[72,128]{1,0:T(8,128)S(1)} %get-tuple-element.26.mine_ref, f32[72,128]{1,0:T(8,128)S(1)} %collective-permute-done.got_ref, f32[6,64,128]{2,1,0:T(8,128)S(1)} %get-tuple-element.31.own_ref, f32[64,128]{1,0:T(8,128)S(1)} %collective-permute-done.3.edge_ref.inner_ref, ...), custom_call_target="tpu_custom_call" | custom-call | tf_op jit(solution)/shard_map/pallas_call | solution.py:464
Async XLA Ops:
  1.0 5.3 %collective-permute-start.1 = (f32[2,16,128]{2,1,0:T(8,128)S(1)}, f32[2,16,128]{2,1,0:T(8,128)S(1)}, u32[]{:S(2)}, u32[]{:S(2)}) collective-permute-start(f32[2,16,128]{2,1,0:T(8,128)S(1)} %get-tuple-element.29), channel_id=1, source_target_pairs={{0,1},{2,3},{1,0},{3,2},{4,5},{6,7},{5,4},{7,6},{8,9},{10,11},{9,8... | collective-permute-start | bytes 49160 | tf_op jit(solution)/shard_map/ppermute | solution.py:423
  2.7 5.6 %collective-permute-start.2 = (f32[2,16,128]{2,1,0:T(8,128)S(1)}, f32[2,16,128]{2,1,0:T(8,128)S(1)}, u32[]{:S(2)}, u32[]{:S(2)}) collective-permute-start(f32[2,16,128]{2,1,0:T(8,128)S(1)} %get-tuple-element.30), channel_id=1, source_target_pairs={{1,2},{2,1},{5,6},{6,5},{9,10},{10,9},{13,14},{14,13},{17,18},{18,... | collective-permute-start | bytes 49160 | tf_op jit(solution)/shard_map/ppermute | solution.py:424
  6.2 2.4 %collective-permute-start = (f32[72,128]{1,0:T(8,128)S(1)}, f32[72,128]{1,0:T(8,128)S(1)}, u32[]{:S(2)}, u32[]{:S(2)}) collective-permute-start(f32[72,128]{1,0:T(8,128)S(1)} %get-tuple-element.27), channel_id=1, source_target_pairs={{0,4},{8,12},{16,20},{24,28},{4,0},{12,8},{20,16},{28,24},{1,5},{9... | collective-permute-start | bytes 110600 | tf_op jit(solution)/shard_map/ppermute | solution.py:435
  8.6 1.2 %collective-permute-start.3 = (f32[64,128]{1,0:T(8,128)S(1)}, f32[64,128]{1,0:T(8,128)S(1)}, u32[]{:S(2)}, u32[]{:S(2)}) collective-permute-start(f32[64,128]{1,0:T(8,128)S(1)} %get-tuple-element.32), channel_id=1, source_target_pairs={{0,4},{8,12},{16,20},{24,28},{4,0},{12,8},{20,16},{28,24},{1,5},{9... | collective-permute-start | bytes 98312 | tf_op jit(solution)/shard_map/ppermute | solution.py:441
  9.9 6.8 %collective-permute-start.6 = (f32[72,128]{1,0:T(8,128)S(1)}, f32[72,128]{1,0:T(8,128)S(1)}, u32[]{:S(2)}, u32[]{:S(2)}) collective-permute-start(f32[72,128]{1,0:T(8,128)S(1)} %get-tuple-element.38), channel_id=1, source_target_pairs={{0,24},{4,28},{8,16},{12,20},{16,8},{20,12},{24,0},{28,4},{1,25},{... | collective-permute-start | bytes 110600 | tf_op jit(solution)/shard_map/ppermute | solution.py:452
  11.4 5.3 %collective-permute-start.4 = (f32[72,128]{1,0:T(8,128)S(1)}, f32[72,128]{1,0:T(8,128)S(1)}, u32[]{:S(2)}, u32[]{:S(2)}) collective-permute-start(f32[72,128]{1,0:T(8,128)S(1)} %get-tuple-element.33.refs_0_), channel_id=1, source_target_pairs={{0,8},{4,12},{8,0},{12,4},{16,24},{20,28},{24,16},{28,20},{1,9},{5... | collective-permute-start | bytes 110600 | tf_op jit(solution)/shard_map/ppermute | solution.py:452
  12.9 3.8 %collective-permute-start.5 = (f32[40,128]{1,0:T(8,128)S(1)}, f32[40,128]{1,0:T(8,128)S(1)}, u32[]{:S(2)}, u32[]{:S(2)}) collective-permute-start(f32[40,128]{1,0:T(8,128)S(1)} %get-tuple-element.37), channel_id=1, source_target_pairs={{0,16},{4,20},{8,24},{12,28},{16,0},{20,4},{24,8},{28,12},{1,17},{... | collective-permute-start | bytes 61448 | tf_op jit(solution)/shard_map/ppermute | solution.py:452

commit v4 on v3

--- a/solution.py
+++ b/solution.py
@@ -102,12 +102,11 @@
     for copy in copies:
         copy.wait()
     bands, rows, cols = t_ref.shape
-    even = lax.axis_index("quad") % 2 == 0
     wide_ref[:, :, 0:cols] = t_ref[...]
     for k, tile in enumerate(packed([wide_ref[b] for b in range(bands)], cols)):
         last, leading = tile[rows - EDGE :], tile[:EDGE]
-        first_ref[k] = jnp.where(even, last, leading)
-        second_ref[k] = jnp.where(even, leading, last)
+        first_ref[k] = last
+        second_ref[k] = leading
 
 
 def pack_kernel(
@@ -160,11 +159,11 @@
         away_ref[m * short : (m + 1) * short] = blocks[2 * other + 1 - side]
 
 
-def edge_kernel(cols, wide_ref, a_ref, b_ref, own_ref, out_ref):
+def edge_kernel(cols, quads, wide_ref, a_ref, b_ref, own_ref, out_ref):
     bands, rows, _ = wide_ref.shape
     ext = rows + 2 * EDGE
     lane = lanes_of((ext, 128))
-    upper = lax.axis_index("quad") % 2 == 0
+    quad = lax.axis_index("quad")
     left = jnp.zeros((ext, 128), F32)
     right = jnp.zeros((ext, 128), F32)
     for b in range(bands):
@@ -172,8 +171,8 @@
             pltpu.roll(ref[b // GROUP], (128 - (b % GROUP) * cols) % 128, 1)
             for ref in (a_ref, b_ref)
         ]
-        north = jnp.where(upper, halo[1], halo[0])
-        south = jnp.where(upper, halo[0], halo[1])
+        north = jnp.where(quad > 0, halo[0], 0.0)
+        south = jnp.where(quad < quads - 1, halo[1], 0.0)
         tile = jnp.concatenate([wide_ref[b], north, south], axis=0)
         own_ref[b] = tile
         at = RAD * b
@@ -232,7 +231,7 @@
 def model_kernel(
     visits, quads, steps, mine_ref, got_ref, own_ref, inner_ref, tab_ref, dh_ref, dl_ref, *refs
 ):
-    message_refs, (out_ref, near) = refs[:-2], refs[-2:]
+    message_refs, (out_ref, near, stack) = refs[:-3], refs[-3:]
     bands, rows, cols = out_ref.shape
     short = rows // 2
     ext = rows + 2 * EDGE
@@ -332,6 +331,26 @@
         poly0, poly1, poly2 = [
             jnp.concatenate([pair[0][0][k], pair[1][0][k]], axis=1) for k in range(3)
         ]
+        filt = 0
+        for degree in DEGREES:
+            count = degree + 1
+            for j0 in range(0, count, 2):
+                js = range(j0, min(j0 + 2, count))
+                lanes = slice((filt + j0) * 128, (filt + js[-1] + 1) * 128)
+                wide = jnp.dot(both, dh_ref[:, lanes], preferred_element_type=F32)
+                conv = (
+                    wide[: 2 * ext]
+                    + wide[2 * ext :]
+                    + jnp.dot(both[: 2 * ext], dl_ref[:, lanes], preferred_element_type=F32)
+                )
+                for j in js:
+                    part = conv[:, (j - j0) * 128 : (j - j0 + 1) * 128]
+                    high, low = split(jnp.concatenate([part[:ext], part[ext:]], axis=1))
+                    at = (filt + j) * 3 * ext
+                    stack[at : at + ext] = high
+                    stack[at + ext : at + 2 * ext] = low
+                    stack[at + 2 * ext : at + 3 * ext] = high
+            filt += count
         model = jnp.zeros((rows, 256), F32)
         basis_start = 0
         filt = 0
@@ -343,30 +362,17 @@
                 for j in range(count - i):
                     index[i, j] = k
                     k += 1
-            for j0 in range(0, count, 2):
-                js = range(j0, min(j0 + 2, count))
-                lanes = slice((filt + j0) * 128, (filt + js[-1] + 1) * 128)
-                wide = jnp.dot(both, dh_ref[:, lanes], preferred_element_type=F32)
-                conv = (
-                    wide[: 2 * ext]
-                    + wide[2 * ext :]
-                    + jnp.dot(both[: 2 * ext], dl_ref[:, lanes], preferred_element_type=F32)
+            for j in range(count):
+                at = (filt + j) * 3 * ext
+                rowed = jnp.dot(
+                    tab_ref[filt * rows : (filt + count - j) * rows],
+                    stack[at : at + 3 * ext],
+                    preferred_element_type=F32,
                 )
-                for j in js:
-                    part = conv[:, (j - j0) * 128 : (j - j0 + 1) * 128]
-                    part = jnp.concatenate([part[:ext], part[ext:]], axis=1)
-                    high, low = split(part)
-                    rowed = jnp.dot(
-                        tab_ref[filt * rows : (filt + count - j) * rows],
-                        jnp.concatenate([high, low, high], axis=0),
-                        preferred_element_type=F32,
-                    )
-                    for i in range(count - j):
-                        n = index[i, j]
-                        spatial = (
-                            poly0[n : n + 1] + y * poly1[n : n + 1] + yy * poly2[n : n + 1]
-                        )
-                        model = model + spatial * rowed[i * rows : (i + 1) * rows]
+                for i in range(count - j):
+                    n = index[i, j]
+                    spatial = poly0[n : n + 1] + y * poly1[n : n + 1] + yy * poly2[n : n + 1]
+                    model = model + spatial * rowed[i * rows : (i + 1) * rows]
             basis_start = k
             filt += count
         for g in range(2):
@@ -420,8 +426,8 @@
         [hbm] * 5,
         [pltpu.VMEM(template.shape, F32), pltpu.SemaphoreType.DMA((5,))],
     )(*sources)
-    halo_a = lax.ppermute(first, "quad", swaps(quads, 0))
-    halo_b = lax.ppermute(second, "quad", swaps(quads, 1))
+    halo_a = lax.ppermute(first, "quad", [(i, (i + 1) % quads) for i in range(quads)])
+    halo_b = lax.ppermute(second, "quad", [((i + 1) % quads, i) for i in range(quads)])
     meta = lax.pad(visit_weight, np.float32(0), ((0, 127, 0),)) + lax.pad(
         band.astype(F32), np.float32(0), ((1, 126, 0),)
     )
@@ -434,7 +440,7 @@
     )(*loaded, meta[None])
     got = lax.ppermute(away, "visit", swaps(visits, 0))
     own, to_core = call(
-        functools.partial(edge_kernel, cols),
+        functools.partial(edge_kernel, cols, quads),
         [struct((bands, ext, 128), F32), struct((ext, 128), F32)],
         [vmem] * 3,
     )(wide, halo_a, halo_b)
@@ -465,7 +471,7 @@
         functools.partial(model_kernel, visits, quads, steps),
         struct((bands, rows, cols), F32),
         [vmem] * (7 + chips - 1),
-        [pltpu.VMEM((bands, ext, 128), F32)],
+        [pltpu.VMEM((bands, ext, 128), F32), pltpu.VMEM((12 * 3 * ext, 256), BF16)],
     )(mine, got, own, edge, *tables, *incoming)
 
 

time: 19.8 us -> 18.6 us (0.939)
  the two profiles are of different devices: /device:TPU:18 before, /device:TPU:0 now
where the time goes in v4:
time: 18.6 us; the launch traced here: 18.4 us
  starting transfers between devices  9.16 us (49%)
  Pallas kernels  4.97 us (27%)
  waiting for transfers between devices  2.9 us (16%)
  between operations  1.34 us (7%)
    ppermute x3, starting transfers between devices, per_device(): lax.ppermute(array, 'visit', [(i, i ^ 2 * m) for i in range(visits)])  3.49 us
    ppermute x1, starting transfers between devices, per_device(): lax.ppermute(first, 'quad', [(i, (i + 1) % quads) for i in range(quads)])  3.1 us
    ppermute x1, starting transfers between devices, per_device(): lax.ppermute(second, 'quad', [((i + 1) % quads, i) for i in range(quads)])  2.09 us
    ppermute x3, waiting for transfers between devices, per_device(): lax.ppermute(array, 'visit', [(i, i ^ 2 * m) for i in range(visits)])  1.93 us
    pallas_call x1, Pallas kernels, per_device(): call(functools.partial(model_kernel, visits, quads, steps), struct((bands...  1.84 us
    pallas_call x1, Pallas kernels, per_device(): call(table_kernel, [struct(a.shape, a.dtype) for a in tables], [vmem] + [...  1.5 us
    pallas_call x1, Pallas kernels, per_device(): call(functools.partial(load_kernel, len(sources)), [strip, strip, struct(...  1.03 us
    ppermute x1, waiting for transfers between devices, per_device(): edge = lax.ppermute(to_core, 'visit', swaps(visits, 0))  0.45 us
  transfers between devices with their start and end apart: 7, of which 4 were waited for; matrix products, arithmetic and copies ran while one was open for 0% of the time, Pallas kernels for 11%

profile of v4, /device:TPU:0, one launch (start us, length us, event | category | flops | bytes accessed | tf_op | source)
XLA Modules:
  0.0 18.4 jit_solution(8277561672097636167)
XLA Ops:
  0.0 1.0 %shard_map.100 = (f32[2,16,128]{2,1,0:T(8,128)S(1)}, f32[2,16,128]{2,1,0:T(8,128)S(1)}, f32[6,32,128]{2,1,0:T(8,128)S(1)}, f32[1,32,256]{2,1,0:T(8,128)S(1)}, f3...) custom-call(f32[6,32,32]{2,1,0:T(8,128)} %refs_0_.1, f32[1,32,256]{2,1,0:T(8,128)} %refs_1_.2, ...), custom_call_target="tpu_custom_call" | custom-call | tf_op jit(solution)/shard_map/pallas_call | solution.py:422
  1.0 3.1 %collective-permute-start.1 = (f32[2,16,128]{2,1,0:T(8,128)S(1)}, f32[2,16,128]{2,1,0:T(8,128)S(1)}, u32[]{:S(2)}, u32[]{:S(2)}) collective-permute-start(f32[2,16,128]{2,1,0:T(8,128)S(1)} %get-tuple-element.29), channel_id=1, source_target_pairs={{0,1},{1,2},{2,3},{3,0},{4,5},{5,6},{6,7},{7,4},{8,9},{9,10},{10,1... | collective-permute-start | bytes 49160 | tf_op jit(solution)/shard_map/ppermute | solution.py:429
  4.1 2.1 %collective-permute-start.2 = (f32[2,16,128]{2,1,0:T(8,128)S(1)}, f32[2,16,128]{2,1,0:T(8,128)S(1)}, u32[]{:S(2)}, u32[]{:S(2)}) collective-permute-start(f32[2,16,128]{2,1,0:T(8,128)S(1)} %get-tuple-element.30), channel_id=1, source_target_pairs={{1,0},{2,1},{3,2},{0,3},{5,4},{6,5},{7,6},{4,7},{9,8},{10,9},{11,1... | collective-permute-start | bytes 49160 | tf_op jit(solution)/shard_map/ppermute | solution.py:430
  7.5 0.1 add_bitcast_fusion.meta_ref
  7.6 0.2 %shard_map.101 = (f32[72,128]{1,0:T(8,128)S(1)}, f32[72,128]{1,0:T(8,128)S(1)}) custom-call(f32[1,32,256]{2,1,0:T(8,128)S(1)} %get-tuple-element.22.sci_ref, f32[1,32,256]{2,1,0:T(8,128)S(1)} %get-tuple-element.23.var_ref, f32[6,1,31]{2,1,0:T(1,128)S(1)} %get-tuple-element.24.coef_ref, s32[1,2,16]{2,1,0:T(2,128)S(1)} %get-tuple-element.25.foot_ref, ...), custom_call_target="tpu_custom_call" | custom-call | tf_op jit(solution)/shard_map/pallas_call | solution.py:435
  7.9 0.1 collective-permute-start
  7.9 0.0 collective-permute-done.1.a_ref
  8.0 0.1 collective-permute-done.2.b_ref
  8.1 0.3 %shard_map.102 = (f32[6,64,128]{2,1,0:T(8,128)S(1)}, f32[64,128]{1,0:T(8,128)S(1)}) custom-call(f32[6,32,128]{2,1,0:T(8,128)S(1)} %get-tuple-element.28.wide_ref, f32[2,16,128]{2,1,0:T(8,128)S(1)} %collective-permute-done.1.a_ref, f32[2,16,128]{2,1,0:T(8,128)S(1)} %collective-permute-done.2.b_ref), custom_call_target="tpu_custom_call" | custom-call | tf_op jit(solution)/shard_map/pallas_call | solution.py:442
  8.3 0.4 %collective-permute-start.3 = (f32[64,128]{1,0:T(8,128)S(1)}, f32[64,128]{1,0:T(8,128)S(1)}, u32[]{:S(2)}, u32[]{:S(2)}) collective-permute-start(f32[64,128]{1,0:T(8,128)S(1)} %get-tuple-element.32), channel_id=1, source_target_pairs={{0,4},{8,12},{16,20},{24,28},{4,0},{12,8},{20,16},{28,24},{1,5},{9... | collective-permute-start | bytes 98312 | tf_op jit(solution)/shard_map/ppermute | solution.py:447
  8.7 0.4 %collective-permute-done.got_ref = f32[72,128]{1,0:T(8,128)S(1)} collective-permute-done((f32[72,128]{1,0:T(8,128)S(1)}, f32[72,128]{1,0:T(8,128)S(1)}, u32[]{:S(2)}, u32[]{:S(2)}) %collective-permute-start) | collective-permute-done | bytes 36896 | tf_op jit(solution)/shard_map/ppermute | solution.py:441
  9.1 0.4 %collective-permute-done.3.edge_ref.inner_ref = f32[64,128]{1,0:T(8,128)S(1)} collective-permute-done((f32[64,128]{1,0:T(8,128)S(1)}, f32[64,128]{1,0:T(8,128)S(1)}, u32[]{:S(2)}, u32[]{:S(2)}) %collective-permute-start.3) | collective-permute-done | bytes 32800 | tf_op jit(solution)/shard_map/ppermute | solution.py:447
  9.6 0.1 shard_map.103
  9.7 2.6 %collective-permute-start.6 = (f32[72,128]{1,0:T(8,128)S(1)}, f32[72,128]{1,0:T(8,128)S(1)}, u32[]{:S(2)}, u32[]{:S(2)}) collective-permute-start(f32[72,128]{1,0:T(8,128)S(1)} %get-tuple-element.38), channel_id=1, source_target_pairs={{0,24},{4,28},{8,16},{12,20},{16,8},{20,12},{24,0},{28,4},{1,25},{... | collective-permute-start | bytes 110600 | tf_op jit(solution)/shard_map/ppermute | solution.py:458
  12.3 0.5 %collective-permute-start.4 = (f32[72,128]{1,0:T(8,128)S(1)}, f32[72,128]{1,0:T(8,128)S(1)}, u32[]{:S(2)}, u32[]{:S(2)}) collective-permute-start(f32[72,128]{1,0:T(8,128)S(1)} %get-tuple-element.33.refs_0_), channel_id=1, source_target_pairs={{0,8},{4,12},{8,0},{12,4},{16,24},{20,28},{24,16},{28,20},{1,9},{5... | collective-permute-start | bytes 110600 | tf_op jit(solution)/shard_map/ppermute | solution.py:458
  12.8 0.3 %collective-permute-start.5 = (f32[40,128]{1,0:T(8,128)S(1)}, f32[40,128]{1,0:T(8,128)S(1)}, u32[]{:S(2)}, u32[]{:S(2)}) collective-permute-start(f32[40,128]{1,0:T(8,128)S(1)} %get-tuple-element.37), channel_id=1, source_target_pairs={{0,16},{4,20},{8,24},{12,28},{16,0},{20,4},{24,8},{28,12},{1,17},{... | collective-permute-start | bytes 61448 | tf_op jit(solution)/shard_map/ppermute | solution.py:458
  13.2 1.5 %shard_map.104 = (bf16[384,192]{1,0:T(8,128)(2,1)S(1)}, bf16[256,1536]{1,0:T(8,128)(2,1)S(1)}, bf16[256,1536]{1,0:T(8,128)(2,1)S(1)}) custom-call(f32[72,128]{1,0:T(8,128)S(1)} %get-tuple-element.33.refs_0_, bf16[384,192]{1,0:T(8,128)(2,1)} %constant.8.clone.refs_1_, bf16[256,1536]{1,0:T(8,128)(2,1)} %constant.9.clone.refs_2_, ...), custom_call_target="tpu_custom_call" | custom-call | tf_op jit(solution)/shard_map/pallas_call | solution.py:464
  14.7 1.9 %collective-permute-done.5.refs_1_ = f32[40,128]{1,0:T(8,128)S(1)} collective-permute-done((f32[40,128]{1,0:T(8,128)S(1)}, f32[40,128]{1,0:T(8,128)S(1)}, u32[]{:S(2)}, u32[]{:S(2)}) %collective-permute-start.5) | collective-permute-done | bytes 20512 | tf_op jit(solution)/shard_map/ppermute | solution.py:458
  16.6 0.0 collective-permute-done.6.refs_2_
  16.6 0.0 collective-permute-done.4.refs_0_
  16.6 1.8 %shard_map.105 = f32[6,32,32]{2,1,0:T(8,128)} custom-call(f32[72,128]{1,0:T(8,128)S(1)} %get-tuple-element.26.mine_ref, f32[72,128]{1,0:T(8,128)S(1)} %collective-permute-done.got_ref, f32[6,64,128]{2,1,0:T(8,128)S(1)} %get-tuple-element.31.own_ref, f32[64,128]{1,0:T(8,128)S(1)} %collective-permute-done.3.edge_ref.inner_ref, ...), custom_call_target="tpu_custom_call" | custom-call | tf_op jit(solution)/shard_map/pallas_call | solution.py:470
Async XLA Ops:
  1.0 6.9 %collective-permute-start.1 = (f32[2,16,128]{2,1,0:T(8,128)S(1)}, f32[2,16,128]{2,1,0:T(8,128)S(1)}, u32[]{:S(2)}, u32[]{:S(2)}) collective-permute-start(f32[2,16,128]{2,1,0:T(8,128)S(1)} %get-tuple-element.29), channel_id=1, source_target_pairs={{0,1},{1,2},{2,3},{3,0},{4,5},{5,6},{6,7},{7,4},{8,9},{9,10},{10,1... | collective-permute-start | bytes 49160 | tf_op jit(solution)/shard_map/ppermute | solution.py:429
  4.1 3.9 %collective-permute-start.2 = (f32[2,16,128]{2,1,0:T(8,128)S(1)}, f32[2,16,128]{2,1,0:T(8,128)S(1)}, u32[]{:S(2)}, u32[]{:S(2)}) collective-permute-start(f32[2,16,128]{2,1,0:T(8,128)S(1)} %get-tuple-element.30), channel_id=1, source_target_pairs={{1,0},{2,1},{3,2},{0,3},{5,4},{6,5},{7,6},{4,7},{9,8},{10,9},{11,1... | collective-permute-start | bytes 49160 | tf_op jit(solution)/shard_map/ppermute | solution.py:430
  7.9 1.3 %collective-permute-start = (f32[72,128]{1,0:T(8,128)S(1)}, f32[72,128]{1,0:T(8,128)S(1)}, u32[]{:S(2)}, u32[]{:S(2)}) collective-permute-start(f32[72,128]{1,0:T(8,128)S(1)} %get-tuple-element.27), channel_id=1, source_target_pairs={{0,4},{8,12},{16,20},{24,28},{4,0},{12,8},{20,16},{28,24},{1,5},{9... | collective-permute-start | bytes 110600 | tf_op jit(solution)/shard_map/ppermute | solution.py:441
  8.3 1.3 %collective-permute-start.3 = (f32[64,128]{1,0:T(8,128)S(1)}, f32[64,128]{1,0:T(8,128)S(1)}, u32[]{:S(2)}, u32[]{:S(2)}) collective-permute-start(f32[64,128]{1,0:T(8,128)S(1)} %get-tuple-element.32), channel_id=1, source_target_pairs={{0,4},{8,12},{16,20},{24,28},{4,0},{12,8},{20,16},{28,24},{1,5},{9... | collective-permute-start | bytes 98312 | tf_op jit(solution)/shard_map/ppermute | solution.py:447
  9.7 6.9 %collective-permute-start.6 = (f32[72,128]{1,0:T(8,128)S(1)}, f32[72,128]{1,0:T(8,128)S(1)}, u32[]{:S(2)}, u32[]{:S(2)}) collective-permute-start(f32[72,128]{1,0:T(8,128)S(1)} %get-tuple-element.38), channel_id=1, source_target_pairs={{0,24},{4,28},{8,16},{12,20},{16,8},{20,12},{24,0},{28,4},{1,25},{... | collective-permute-start | bytes 110600 | tf_op jit(solution)/shard_map/ppermute | solution.py:458
  12.3 4.3 %collective-permute-start.4 = (f32[72,128]{1,0:T(8,128)S(1)}, f32[72,128]{1,0:T(8,128)S(1)}, u32[]{:S(2)}, u32[]{:S(2)}) collective-permute-start(f32[72,128]{1,0:T(8,128)S(1)} %get-tuple-element.33.refs_0_), channel_id=1, source_target_pairs={{0,8},{4,12},{8,0},{12,4},{16,24},{20,28},{24,16},{28,20},{1,9},{5... | collective-permute-start | bytes 110600 | tf_op jit(solution)/shard_map/ppermute | solution.py:458
  12.8 3.8 %collective-permute-start.5 = (f32[40,128]{1,0:T(8,128)S(1)}, f32[40,128]{1,0:T(8,128)S(1)}, u32[]{:S(2)}, u32[]{:S(2)}) collective-permute-start(f32[40,128]{1,0:T(8,128)S(1)} %get-tuple-element.37), channel_id=1, source_target_pairs={{0,16},{4,20},{8,24},{12,28},{16,0},{20,4},{24,8},{28,12},{1,17},{... | collective-permute-start | bytes 61448 | tf_op jit(solution)/shard_map/ppermute | solution.py:458

commit v5 on v4

--- a/solution.py
+++ b/solution.py
@@ -154,12 +154,13 @@
             block = jnp.where(flat < 32 * k, block, turned)
         blocks[d] = block
     for m in range(chips):
+        near = side if m == 0 else 1 - side
         other = chip ^ m
-        mine_ref[m * short : (m + 1) * short] = blocks[2 * other + side]
-        away_ref[m * short : (m + 1) * short] = blocks[2 * other + 1 - side]
-
-
-def edge_kernel(cols, quads, wide_ref, a_ref, b_ref, own_ref, out_ref):
+        mine_ref[m * short : (m + 1) * short] = blocks[2 * other + near]
+        away_ref[m * short : (m + 1) * short] = blocks[2 * other + 1 - near]
+
+
+def edge_kernel(cols, quads, wide_ref, a_ref, b_ref, own_ref, inner_ref, outer_ref):
     bands, rows, _ = wide_ref.shape
     ext = rows + 2 * EDGE
     lane = lanes_of((ext, 128))
@@ -180,22 +181,23 @@
         left = jnp.where(here, pltpu.roll(tile, at, 1), left)
         right = jnp.where(here, pltpu.roll(tile, (at - (cols - RAD)) % 128, 1), right)
     even = lax.axis_index("visit") % 2 == 0
-    inner = jnp.where(even, right, left)
-    outer = jnp.where(even, left, right)
-    out_ref[...] = jnp.where(lane < 64, inner, pltpu.roll(outer, 64, 1))
+    half = lane[: ext // 2] < 64
+    for ref, edge in (
+        (inner_ref, jnp.where(even, right, left)),
+        (outer_ref, jnp.where(even, left, right)),
+    ):
+        ref[...] = jnp.where(half, edge[: ext // 2], pltpu.roll(edge[ext // 2 :], 64, 1))
 
 
 def merge_kernel(rows, steps, mine_ref, got_ref, edge_ref, *out_refs):
     chips = len(out_refs) + 1
     short = rows // 2
     base = chips * short
-    half = lanes_of((rows, 128)) < 64
-    middle = edge_ref.shape[0] // 2
-    edge = jnp.where(
-        half[:middle], pltpu.roll(edge_ref[:middle], 64, 1), edge_ref[middle:]
-    )
+    middle = edge_ref.shape[0]
     coefs = jnp.where(
-        half[:8], mine_ref[base : base + 8], pltpu.roll(got_ref[base : base + 8], 64, 1)
+        lanes_of((8, 128)) < 64,
+        mine_ref[base : base + 8],
+        pltpu.roll(got_ref[base : base + 8], 64, 1),
     )
     for m in range(1, chips):
         out_ref = out_refs[m - 1]
@@ -204,7 +206,7 @@
         out_ref[short:rows] = got_ref[at]
         out_ref[rows : rows + 8] = coefs
         if m in steps:
-            out_ref[rows + 8 : rows + 8 + middle] = edge
+            out_ref[rows + 8 : rows + 8 + middle] = edge_ref[...]
 
 
 def table_kernel(*refs):
@@ -250,8 +252,9 @@
     for m in steps:
         arrived = message_refs[m - 1][rows + 8 : rows + 8 + middle]
         edge = jnp.where(exists & ((chip ^ beside) == m), arrived, edge)
-    outer = jnp.concatenate([edge, pltpu.roll(edge, 64, 1)], axis=0)
-    inner = inner_ref[...]
+    outer, inner = [
+        jnp.concatenate([part, pltpu.roll(part, 64, 1)], axis=0) for part in (edge, inner_ref[...])
+    ]
     west = jnp.where(even, outer, inner)
     east = jnp.where(even, inner, outer)
     for b in range(bands):
@@ -439,9 +442,9 @@
         [pltpu.VMEM((visits, short, 128), F32)],
     )(*loaded, meta[None])
     got = lax.ppermute(away, "visit", swaps(visits, 0))
-    own, to_core = call(
+    own, to_core, to_chips = call(
         functools.partial(edge_kernel, cols, quads),
-        [struct((bands, ext, 128), F32), struct((ext, 128), F32)],
+        [struct((bands, ext, 128), F32)] + [struct((ext // 2, 128), F32)] * 2,
         [vmem] * 3,
     )(wide, halo_a, halo_b)
     edge = lax.ppermute(to_core, "visit", swaps(visits, 0))
@@ -453,9 +456,9 @@
             for m in range(1, chips)
         ],
         [vmem] * 3,
-    )(mine, got, edge)
+    )(mine, got, to_chips)
     incoming = [
-        lax.ppermute(array, "visit", [(i, i ^ (2 * m)) for i in range(visits)])
+        lax.ppermute(array, "visit", [(i, i ^ (2 * m + 1)) for i in range(visits)])
         for m, array in enumerate(outgoing, 1)
     ]
     tables = [

time: 18.6 us -> 18.4 us (0.989)
  starting transfers between devices: 9.16 us -> 8.61 us
  waiting for transfers between devices: 2.9 us -> 3.22 us
    ppermute x1, waiting for transfers between devices: 0.04 us -> 1.75 us  [per_device(): lax.ppermute(first, 'quad', [(i, (i + 1) % quads) for i in range(quads)])]
    ppermute x3, waiting for transfers between devices: 1.93 us -> 1.39 us  [per_device(): lax.ppermute(array, 'visit', [(i, i ^ 2 * m + 1) for i in range(visits)])]
    ppermute x3, starting transfers between devices: 3.49 us -> 2.97 us  [per_device(): lax.ppermute(array, 'visit', [(i, i ^ 2 * m + 1) for i in range(visits)])]
    ppermute x1, starting transfers between devices: 0.07 us -> 0.56 us  [per_device(): got = lax.ppermute(away, 'visit', swaps(visits, 0))]
    ppermute x1, starting transfers between devices: 3.1 us -> 2.63 us  [per_device(): lax.ppermute(first, 'quad', [(i, (i + 1) % quads) for i in range(quads)])]
    ppermute x1, waiting for transfers between devices: 0.45 us -> 0.01 us  [per_device(): edge = lax.ppermute(to_core, 'visit', swaps(visits, 0))]
    ppermute x1, waiting for transfers between devices: 0.41 us -> 0.01 us  [per_device(): got = lax.ppermute(away, 'visit', swaps(visits, 0))]
  transfers between devices with their start and end apart: 7 -> 7, of which waited for: 4 -> 3; matrix products, arithmetic and copies ran while one was open for 0% -> 0% of each run, Pallas kernels for 11% -> 10%
where the time goes in v5:
time: 18.4 us; the launch traced here: 18.2 us
  starting transfers between devices  8.61 us (47%)
  Pallas kernels  4.95 us (27%)
  waiting for transfers between devices  3.22 us (18%)
  between operations  1.34 us (7%)
    ppermute x3, starting transfers between devices, per_device(): lax.ppermute(array, 'visit', [(i, i ^ 2 * m + 1) for i in range(visits)])  2.97 us
    ppermute x1, starting transfers between devices, per_device(): lax.ppermute(first, 'quad', [(i, (i + 1) % quads) for i in range(quads)])  2.63 us
    ppermute x1, starting transfers between devices, per_device(): lax.ppermute(second, 'quad', [((i + 1) % quads, i) for i in range(quads)])  2.09 us
    pallas_call x1, Pallas kernels, per_device(): call(functools.partial(model_kernel, visits, quads, steps), struct((bands...  1.85 us
    ppermute x1, waiting for transfers between devices, per_device(): lax.ppermute(first, 'quad', [(i, (i + 1) % quads) for i in range(quads)])  1.75 us
    pallas_call x1, Pallas kernels, per_device(): call(table_kernel, [struct(a.shape, a.dtype) for a in tables], [vmem] + [...  1.5 us
    ppermute x3, waiting for transfers between devices, per_device(): lax.ppermute(array, 'visit', [(i, i ^ 2 * m + 1) for i in range(visits)])  1.39 us
    pallas_call x1, Pallas kernels, per_device(): call(functools.partial(load_kernel, len(sources)), [strip, strip, struct(...  1.03 us
  transfers between devices with their start and end apart: 7, of which 3 were waited for; matrix products, arithmetic and copies ran while one was open for 0% of the time, Pallas kernels for 10%

profile of v5, /device:TPU:0, one launch (start us, length us, event | category | flops | bytes accessed | tf_op | source)
XLA Modules:
  0.0 18.2 jit_solution(12181102213027680039)
XLA Ops:
  1.3 0.1 add_bitcast_fusion.meta_ref
  1.4 1.0 %shard_map.100 = (f32[2,16,128]{2,1,0:T(8,128)S(1)}, f32[2,16,128]{2,1,0:T(8,128)S(1)}, f32[6,32,128]{2,1,0:T(8,128)S(1)}, f32[1,32,256]{2,1,0:T(8,128)S(1)}, f3...) custom-call(f32[6,32,32]{2,1,0:T(8,128)} %refs_0_.1, f32[1,32,256]{2,1,0:T(8,128)} %refs_1_.2, ...), custom_call_target="tpu_custom_call" | custom-call | tf_op jit(solution)/shard_map/pallas_call | solution.py:425
  2.4 0.2 %shard_map.101 = (f32[72,128]{1,0:T(8,128)S(1)}, f32[72,128]{1,0:T(8,128)S(1)}) custom-call(f32[1,32,256]{2,1,0:T(8,128)S(1)} %get-tuple-element.23.sci_ref, f32[1,32,256]{2,1,0:T(8,128)S(1)} %get-tuple-element.24.var_ref, f32[6,1,31]{2,1,0:T(1,128)S(1)} %get-tuple-element.25.coef_ref, s32[1,2,16]{2,1,0:T(2,128)S(1)} %get-tuple-element.26.foot_ref, ...), custom_call_target="tpu_custom_call" | custom-call | tf_op jit(solution)/shard_map/pallas_call | solution.py:438
  2.7 0.6 %collective-permute-start = (f32[72,128]{1,0:T(8,128)S(1)}, f32[72,128]{1,0:T(8,128)S(1)}, u32[]{:S(2)}, u32[]{:S(2)}) collective-permute-start(f32[72,128]{1,0:T(8,128)S(1)} %get-tuple-element.28), channel_id=1, source_target_pairs={{0,4},{8,12},{16,20},{24,28},{4,0},{12,8},{20,16},{28,24},{1,5},{9... | collective-permute-start | bytes 110600 | tf_op jit(solution)/shard_map/ppermute | solution.py:444
  3.2 2.6 %collective-permute-start.1 = (f32[2,16,128]{2,1,0:T(8,128)S(1)}, f32[2,16,128]{2,1,0:T(8,128)S(1)}, u32[]{:S(2)}, u32[]{:S(2)}) collective-permute-start(f32[2,16,128]{2,1,0:T(8,128)S(1)} %get-tuple-element.30), channel_id=1, source_target_pairs={{0,1},{1,2},{2,3},{3,0},{4,5},{5,6},{6,7},{7,4},{8,9},{9,10},{10,1... | collective-permute-start | bytes 49160 | tf_op jit(solution)/shard_map/ppermute | solution.py:432
  5.9 2.1 %collective-permute-start.2 = (f32[2,16,128]{2,1,0:T(8,128)S(1)}, f32[2,16,128]{2,1,0:T(8,128)S(1)}, u32[]{:S(2)}, u32[]{:S(2)}) collective-permute-start(f32[2,16,128]{2,1,0:T(8,128)S(1)} %get-tuple-element.31), channel_id=1, source_target_pairs={{1,0},{2,1},{3,2},{0,3},{5,4},{6,5},{7,6},{4,7},{9,8},{10,9},{11,1... | collective-permute-start | bytes 49160 | tf_op jit(solution)/shard_map/ppermute | solution.py:433
  7.9 1.8 %collective-permute-done.1.a_ref = f32[2,16,128]{2,1,0:T(8,128)S(1)} collective-permute-done((f32[2,16,128]{2,1,0:T(8,128)S(1)}, f32[2,16,128]{2,1,0:T(8,128)S(1)}, u32[]{:S(2)}, u32[]{:S(2)}) %collective-permute-start.1) | collective-permute-done | bytes 16416 | tf_op jit(solution)/shard_map/ppermute | solution.py:432
  9.7 0.1 collective-permute-done.2.b_ref
  9.8 0.2 %shard_map.102 = (f32[6,64,128]{2,1,0:T(8,128)S(1)}, f32[32,128]{1,0:T(8,128)S(1)}, f32[32,128]{1,0:T(8,128)S(1)}) custom-call(f32[6,32,128]{2,1,0:T(8,128)S(1)} %get-tuple-element.29.wide_ref, f32[2,16,128]{2,1,0:T(8,128)S(1)} %collective-permute-done.1.a_ref, f32[2,16,128]{2,1,0:T(8,128)S(1)} %collective-permute-done.2.b_ref), custom_call_target="tpu_custom_call" | custom-call | tf_op jit(solution)/shard_map/pallas_call | solution.py:445
  10.0 0.0 collective-permute-done.got_ref
  10.0 0.1 shard_map.103
  10.1 1.5 %collective-permute-start.6 = (f32[72,128]{1,0:T(8,128)S(1)}, f32[72,128]{1,0:T(8,128)S(1)}, u32[]{:S(2)}, u32[]{:S(2)}) collective-permute-start(f32[72,128]{1,0:T(8,128)S(1)} %get-tuple-element.40), channel_id=1, source_target_pairs={{0,28},{4,24},{8,20},{12,16},{16,12},{20,8},{24,4},{28,0},{1,29},{... | collective-permute-start | bytes 110600 | tf_op jit(solution)/shard_map/ppermute | solution.py:461
  11.6 1.4 %collective-permute-start.4 = (f32[72,128]{1,0:T(8,128)S(1)}, f32[72,128]{1,0:T(8,128)S(1)}, u32[]{:S(2)}, u32[]{:S(2)}) collective-permute-start(f32[72,128]{1,0:T(8,128)S(1)} %get-tuple-element.35.refs_0_), channel_id=1, source_target_pairs={{0,12},{4,8},{8,4},{12,0},{16,28},{20,24},{24,20},{28,16},{1,13},{... | collective-permute-start | bytes 110600 | tf_op jit(solution)/shard_map/ppermute | solution.py:461
  13.0 0.1 collective-permute-start.5
  13.1 0.4 %collective-permute-start.3 = (f32[32,128]{1,0:T(8,128)S(1)}, f32[32,128]{1,0:T(8,128)S(1)}, u32[]{:S(2)}, u32[]{:S(2)}) collective-permute-start(f32[32,128]{1,0:T(8,128)S(1)} %get-tuple-element.33), channel_id=1, source_target_pairs={{0,4},{8,12},{16,20},{24,28},{4,0},{12,8},{20,16},{28,24},{1,5},{9... | collective-permute-start | bytes 49160 | tf_op jit(solution)/shard_map/ppermute | solution.py:450
  13.4 1.5 %shard_map.104 = (bf16[384,192]{1,0:T(8,128)(2,1)S(1)}, bf16[256,1536]{1,0:T(8,128)(2,1)S(1)}, bf16[256,1536]{1,0:T(8,128)(2,1)S(1)}) custom-call(f32[72,128]{1,0:T(8,128)S(1)} %get-tuple-element.35.refs_0_, bf16[384,192]{1,0:T(8,128)(2,1)} %constant.8.clone.refs_1_, bf16[256,1536]{1,0:T(8,128)(2,1)} %constant.9.clone.refs_2_, ...), custom_call_target="tpu_custom_call" | custom-call | tf_op jit(solution)/shard_map/pallas_call | solution.py:467
  14.9 0.0 collective-permute-done.3.inner_ref
  14.9 1.4 %collective-permute-done.5.refs_1_ = f32[40,128]{1,0:T(8,128)S(1)} collective-permute-done((f32[40,128]{1,0:T(8,128)S(1)}, f32[40,128]{1,0:T(8,128)S(1)}, u32[]{:S(2)}, u32[]{:S(2)}) %collective-permute-start.5) | collective-permute-done | bytes 20512 | tf_op jit(solution)/shard_map/ppermute | solution.py:461
  16.3 0.0 collective-permute-done.6.refs_2_
  16.3 0.0 collective-permute-done.4.refs_0_
  16.3 1.8 %shard_map.105 = f32[6,32,32]{2,1,0:T(8,128)} custom-call(f32[72,128]{1,0:T(8,128)S(1)} %get-tuple-element.27.mine_ref, f32[72,128]{1,0:T(8,128)S(1)} %collective-permute-done.got_ref, f32[6,64,128]{2,1,0:T(8,128)S(1)} %get-tuple-element.32.own_ref, f32[32,128]{1,0:T(8,128)S(1)} %collective-permute-done.3.inner_ref, ...), custom_call_target="tpu_custom_call" | custom-call | tf_op jit(solution)/shard_map/pallas_call | solution.py:473
Async XLA Ops:
  2.7 7.3 %collective-permute-start = (f32[72,128]{1,0:T(8,128)S(1)}, f32[72,128]{1,0:T(8,128)S(1)}, u32[]{:S(2)}, u32[]{:S(2)}) collective-permute-start(f32[72,128]{1,0:T(8,128)S(1)} %get-tuple-element.28), channel_id=1, source_target_pairs={{0,4},{8,12},{16,20},{24,28},{4,0},{12,8},{20,16},{28,24},{1,5},{9... | collective-permute-start | bytes 110600 | tf_op jit(solution)/shard_map/ppermute | solution.py:444
  3.2 6.5 %collective-permute-start.1 = (f32[2,16,128]{2,1,0:T(8,128)S(1)}, f32[2,16,128]{2,1,0:T(8,128)S(1)}, u32[]{:S(2)}, u32[]{:S(2)}) collective-permute-start(f32[2,16,128]{2,1,0:T(8,128)S(1)} %get-tuple-element.30), channel_id=1, source_target_pairs={{0,1},{1,2},{2,3},{3,0},{4,5},{5,6},{6,7},{7,4},{8,9},{9,10},{10,1... | collective-permute-start | bytes 49160 | tf_op jit(solution)/shard_map/ppermute | solution.py:432
  5.9 3.9 %collective-permute-start.2 = (f32[2,16,128]{2,1,0:T(8,128)S(1)}, f32[2,16,128]{2,1,0:T(8,128)S(1)}, u32[]{:S(2)}, u32[]{:S(2)}) collective-permute-start(f32[2,16,128]{2,1,0:T(8,128)S(1)} %get-tuple-element.31), channel_id=1, source_target_pairs={{1,0},{2,1},{3,2},{0,3},{5,4},{6,5},{7,6},{4,7},{9,8},{10,9},{11,1... | collective-permute-start | bytes 49160 | tf_op jit(solution)/shard_map/ppermute | solution.py:433
  10.1 6.3 %collective-permute-start.6 = (f32[72,128]{1,0:T(8,128)S(1)}, f32[72,128]{1,0:T(8,128)S(1)}, u32[]{:S(2)}, u32[]{:S(2)}) collective-permute-start(f32[72,128]{1,0:T(8,128)S(1)} %get-tuple-element.40), channel_id=1, source_target_pairs={{0,28},{4,24},{8,20},{12,16},{16,12},{20,8},{24,4},{28,0},{1,29},{... | collective-permute-start | bytes 110600 | tf_op jit(solution)/shard_map/ppermute | solution.py:461
  11.6 4.8 %collective-permute-start.4 = (f32[72,128]{1,0:T(8,128)S(1)}, f32[72,128]{1,0:T(8,128)S(1)}, u32[]{:S(2)}, u32[]{:S(2)}) collective-permute-start(f32[72,128]{1,0:T(8,128)S(1)} %get-tuple-element.35.refs_0_), channel_id=1, source_target_pairs={{0,12},{4,8},{8,4},{12,0},{16,28},{20,24},{24,20},{28,16},{1,13},{... | collective-permute-start | bytes 110600 | tf_op jit(solution)/shard_map/ppermute | solution.py:461
  13.0 3.4 %collective-permute-start.5 = (f32[40,128]{1,0:T(8,128)S(1)}, f32[40,128]{1,0:T(8,128)S(1)}, u32[]{:S(2)}, u32[]{:S(2)}) collective-permute-start(f32[40,128]{1,0:T(8,128)S(1)} %get-tuple-element.39), channel_id=1, source_target_pairs={{0,20},{4,16},{8,28},{12,24},{16,4},{20,0},{24,12},{28,8},{1,21},{... | collective-permute-start | bytes 61448 | tf_op jit(solution)/shard_map/ppermute | solution.py:461
  13.1 1.9 %collective-permute-start.3 = (f32[32,128]{1,0:T(8,128)S(1)}, f32[32,128]{1,0:T(8,128)S(1)}, u32[]{:S(2)}, u32[]{:S(2)}) collective-permute-start(f32[32,128]{1,0:T(8,128)S(1)} %get-tuple-element.33), channel_id=1, source_target_pairs={{0,4},{8,12},{16,20},{24,28},{4,0},{12,8},{20,16},{28,24},{1,5},{9... | collective-permute-start | bytes 49160 | tf_op jit(solution)/shard_map/ppermute | solution.py:450

commit v6 on v5

--- a/solution.py
+++ b/solution.py
@@ -110,7 +110,7 @@
 
 
 def pack_kernel(
-    visits, cols, sci_ref, var_ref, coef_ref, foot_ref, meta_ref, mine_ref, away_ref, blocks
+    visits, cols, sci_ref, var_ref, coef_ref, foot_ref, w_ref, band_ref, mine_ref, away_ref, blocks
 ):
     rows = sci_ref.shape[1]
     short = rows // 2
@@ -118,10 +118,10 @@
     me = lax.axis_index("visit")
     chip, side = me // 2, me % 2
     at = chips * short
-    weight = jnp.broadcast_to(meta_ref[:, 0:1], (rows, 128))
+    weight = w_ref[0]
     coef = coef_ref[:, 0, :]
     terms, basis = coef.shape
-    which = jnp.broadcast_to(meta_ref[:, 1:2], (1, 128))
+    which = jnp.full((1, 128), band_ref[0].astype(F32), F32)
     for ref in (mine_ref, away_ref):
         ref[at : at + terms, 0:basis] = coef
         ref[at + terms : at + terms + 1] = which
@@ -233,7 +233,7 @@
 def model_kernel(
     visits, quads, steps, mine_ref, got_ref, own_ref, inner_ref, tab_ref, dh_ref, dl_ref, *refs
 ):
-    message_refs, (out_ref, near, stack) = refs[:-3], refs[-3:]
+    message_refs, (out_ref, near, stack, convs, fields) = refs[:-5], refs[-5:]
     bands, rows, cols = out_ref.shape
     short = rows // 2
     ext = rows + 2 * EDGE
@@ -354,7 +354,6 @@
                     stack[at + ext : at + 2 * ext] = low
                     stack[at + 2 * ext : at + 3 * ext] = high
             filt += count
-        model = jnp.zeros((rows, 256), F32)
         basis_start = 0
         filt = 0
         for degree in DEGREES:
@@ -374,10 +373,21 @@
                 )
                 for i in range(count - j):
                     n = index[i, j]
-                    spatial = poly0[n : n + 1] + y * poly1[n : n + 1] + yy * poly2[n : n + 1]
-                    model = model + spatial * rowed[i * rows : (i + 1) * rows]
+                    convs[n * rows : (n + 1) * rows] = rowed[i * rows : (i + 1) * rows]
             basis_start = k
             filt += count
+        for k, poly in enumerate((poly0, poly1, poly2)):
+            fields[k] = poly
+        pieces = []
+        for at in range(0, rows, 8):
+            level, square = y[at : at + 8], yy[at : at + 8]
+            total = jnp.zeros((8, 256), F32)
+            for n in range(basis_start):
+                row = [fields[k, pl.ds(n, 8, stride=0), :] for k in range(3)]
+                spatial = row[0] + level * row[1] + square * row[2]
+                total = total + spatial * convs[n * rows + at : n * rows + at + 8]
+            pieces.append(total)
+        model = jnp.concatenate(pieces, axis=0)
         for g in range(2):
             _, _, first, second, which = pair[g]
             part = first - second * model[:, g * 128 : (g + 1) * 128]
@@ -409,7 +419,7 @@
     params = pltpu.CompilerParams(vmem_limit_bytes=24 * 1024 * 1024)
     struct = jax.ShapeDtypeStruct
 
-    def call(kernel, outs, ins, scratch=()):
+    def call(kernel, outs, ins, scratch=(), params=params):
         return pl.pallas_call(
             kernel,
             out_shape=outs,
@@ -431,16 +441,13 @@
     )(*sources)
     halo_a = lax.ppermute(first, "quad", [(i, (i + 1) % quads) for i in range(quads)])
     halo_b = lax.ppermute(second, "quad", [((i + 1) % quads, i) for i in range(quads)])
-    meta = lax.pad(visit_weight, np.float32(0), ((0, 127, 0),)) + lax.pad(
-        band.astype(F32), np.float32(0), ((1, 126, 0),)
-    )
     height = chips * short + 8
     mine, away = call(
         functools.partial(pack_kernel, visits, cols),
         [struct((height, 128), F32)] * 2,
-        [vmem] * 5,
+        [vmem] * 4 + [pl.BlockSpec(memory_space=pltpu.SMEM)] * 2,
         [pltpu.VMEM((visits, short, 128), F32)],
-    )(*loaded, meta[None])
+    )(*loaded, visit_weight, band)
     got = lax.ppermute(away, "visit", swaps(visits, 0))
     own, to_core, to_chips = call(
         functools.partial(edge_kernel, cols, quads),
@@ -474,7 +481,8 @@
         functools.partial(model_kernel, visits, quads, steps),
         struct((bands, rows, cols), F32),
         [vmem] * (7 + chips - 1),
-        [pltpu.VMEM((bands, ext, 128), F32), pltpu.VMEM((12 * 3 * ext, 256), BF16)],
+        [pltpu.VMEM((bands, ext, 128), F32), pltpu.VMEM((12 * 3 * ext, 256), BF16), pltpu.VMEM((coeffs.shape[1] * rows, 256), F32), pltpu.VMEM((3, rows, 256), F32)],
+        params=pltpu.CompilerParams(vmem_limit_bytes=24 * 1024 * 1024),
     )(mine, got, own, edge, *tables, *incoming)
 
 

time: 18.4 us -> 18.3 us (level)
  no operation moved by 1% of the time
where the time goes in v6:
time: 18.3 us; the launch traced here: 18.1 us
  starting transfers between devices  8.61 us (47%)
  Pallas kernels  4.94 us (27%)
  waiting for transfers between devices  3.22 us (18%)
  between operations  1.34 us (7%)
    ppermute x3, starting transfers between devices, per_device(): lax.ppermute(array, 'visit', [(i, i ^ 2 * m + 1) for i in range(visits)])  2.97 us
    ppermute x1, starting transfers between devices, per_device(): lax.ppermute(first, 'quad', [(i, (i + 1) % quads) for i in range(quads)])  2.63 us
    ppermute x1, starting transfers between devices, per_device(): lax.ppermute(second, 'quad', [((i + 1) % quads, i) for i in range(quads)])  2.09 us
    pallas_call x1, Pallas kernels, per_device(): call(functools.partial(model_kernel, visits, quads, steps), struct((bands...  1.84 us
    ppermute x1, waiting for transfers between devices, per_device(): lax.ppermute(first, 'quad', [(i, (i + 1) % quads) for i in range(quads)])  1.75 us
    pallas_call x1, Pallas kernels, per_device(): call(table_kernel, [struct(a.shape, a.dtype) for a in tables], [vmem] + [...  1.5 us
    ppermute x3, waiting for transfers between devices, per_device(): lax.ppermute(array, 'visit', [(i, i ^ 2 * m + 1) for i in range(visits)])  1.39 us
    pallas_call x1, Pallas kernels, per_device(): call(functools.partial(load_kernel, len(sources)), [strip, strip, struct(...  1.04 us
  transfers between devices with their start and end apart: 7, of which 3 were waited for; matrix products, arithmetic and copies ran while one was open for 0% of the time, Pallas kernels for 10%

profile of v6, /device:TPU:0, one launch (start us, length us, event | category | flops | bytes accessed | tf_op | source)
XLA Modules:
  0.0 18.1 jit_solution(2101979923647973591)
XLA Ops:
  1.3 1.0 %shard_map.100 = (f32[2,16,128]{2,1,0:T(8,128)S(1)}, f32[2,16,128]{2,1,0:T(8,128)S(1)}, f32[6,32,128]{2,1,0:T(8,128)S(1)}, f32[1,32,256]{2,1,0:T(8,128)S(1)}, f3...) custom-call(f32[6,32,32]{2,1,0:T(8,128)} %refs_0_.1, f32[1,32,256]{2,1,0:T(8,128)} %refs_1_.2, ...), custom_call_target="tpu_custom_call" | custom-call | tf_op jit(solution)/shard_map/pallas_call | solution.py:435
  2.3 0.2 %shard_map.101 = (f32[72,128]{1,0:T(8,128)S(1)}, f32[72,128]{1,0:T(8,128)S(1)}) custom-call(f32[1,32,256]{2,1,0:T(8,128)S(1)} %get-tuple-element.23.sci_ref, f32[1,32,256]{2,1,0:T(8,128)S(1)} %get-tuple-element.24.var_ref, f32[6,1,31]{2,1,0:T(1,128)S(1)} %get-tuple-element.25.coef_ref, s32[1,2,16]{2,1,0:T(2,128)S(1)} %get-tuple-element.26.foot_ref, ...), custom_call_target="tpu_custom_call" | custom-call | tf_op jit(solution)/shard_map/pallas_call | solution.py:445
  2.6 0.6 %collective-permute-start = (f32[72,128]{1,0:T(8,128)S(1)}, f32[72,128]{1,0:T(8,128)S(1)}, u32[]{:S(2)}, u32[]{:S(2)}) collective-permute-start(f32[72,128]{1,0:T(8,128)S(1)} %get-tuple-element.28), channel_id=1, source_target_pairs={{0,4},{8,12},{16,20},{24,28},{4,0},{12,8},{20,16},{28,24},{1,5},{9... | collective-permute-start | bytes 110600 | tf_op jit(solution)/shard_map/ppermute | solution.py:451
  3.2 2.6 %collective-permute-start.1 = (f32[2,16,128]{2,1,0:T(8,128)S(1)}, f32[2,16,128]{2,1,0:T(8,128)S(1)}, u32[]{:S(2)}, u32[]{:S(2)}) collective-permute-start(f32[2,16,128]{2,1,0:T(8,128)S(1)} %get-tuple-element.30), channel_id=1, source_target_pairs={{0,1},{1,2},{2,3},{3,0},{4,5},{5,6},{6,7},{7,4},{8,9},{9,10},{10,1... | collective-permute-start | bytes 49160 | tf_op jit(solution)/shard_map/ppermute | solution.py:442
  5.8 2.1 %collective-permute-start.2 = (f32[2,16,128]{2,1,0:T(8,128)S(1)}, f32[2,16,128]{2,1,0:T(8,128)S(1)}, u32[]{:S(2)}, u32[]{:S(2)}) collective-permute-start(f32[2,16,128]{2,1,0:T(8,128)S(1)} %get-tuple-element.31), channel_id=1, source_target_pairs={{1,0},{2,1},{3,2},{0,3},{5,4},{6,5},{7,6},{4,7},{9,8},{10,9},{11,1... | collective-permute-start | bytes 49160 | tf_op jit(solution)/shard_map/ppermute | solution.py:443
  7.9 1.8 %collective-permute-done.1.a_ref = f32[2,16,128]{2,1,0:T(8,128)S(1)} collective-permute-done((f32[2,16,128]{2,1,0:T(8,128)S(1)}, f32[2,16,128]{2,1,0:T(8,128)S(1)}, u32[]{:S(2)}, u32[]{:S(2)}) %collective-permute-start.1) | collective-permute-done | bytes 16416 | tf_op jit(solution)/shard_map/ppermute | solution.py:442
  9.6 0.1 collective-permute-done.2.b_ref
  9.7 0.2 %shard_map.102 = (f32[6,64,128]{2,1,0:T(8,128)S(1)}, f32[32,128]{1,0:T(8,128)S(1)}, f32[32,128]{1,0:T(8,128)S(1)}) custom-call(f32[6,32,128]{2,1,0:T(8,128)S(1)} %get-tuple-element.29.wide_ref, f32[2,16,128]{2,1,0:T(8,128)S(1)} %collective-permute-done.1.a_ref, f32[2,16,128]{2,1,0:T(8,128)S(1)} %collective-permute-done.2.b_ref), custom_call_target="tpu_custom_call" | custom-call | tf_op jit(solution)/shard_map/pallas_call | solution.py:452
  9.9 0.0 collective-permute-done.got_ref
  9.9 0.1 shard_map.103
  10.0 1.5 %collective-permute-start.6 = (f32[72,128]{1,0:T(8,128)S(1)}, f32[72,128]{1,0:T(8,128)S(1)}, u32[]{:S(2)}, u32[]{:S(2)}) collective-permute-start(f32[72,128]{1,0:T(8,128)S(1)} %get-tuple-element.40), channel_id=1, source_target_pairs={{0,28},{4,24},{8,20},{12,16},{16,12},{20,8},{24,4},{28,0},{1,29},{... | collective-permute-start | bytes 110600 | tf_op jit(solution)/shard_map/ppermute | solution.py:468
  11.5 1.4 %collective-permute-start.4 = (f32[72,128]{1,0:T(8,128)S(1)}, f32[72,128]{1,0:T(8,128)S(1)}, u32[]{:S(2)}, u32[]{:S(2)}) collective-permute-start(f32[72,128]{1,0:T(8,128)S(1)} %get-tuple-element.35.refs_0_), channel_id=1, source_target_pairs={{0,12},{4,8},{8,4},{12,0},{16,28},{20,24},{24,20},{28,16},{1,13},{... | collective-permute-start | bytes 110600 | tf_op jit(solution)/shard_map/ppermute | solution.py:468
  12.9 0.1 collective-permute-start.5
  13.0 0.4 %collective-permute-start.3 = (f32[32,128]{1,0:T(8,128)S(1)}, f32[32,128]{1,0:T(8,128)S(1)}, u32[]{:S(2)}, u32[]{:S(2)}) collective-permute-start(f32[32,128]{1,0:T(8,128)S(1)} %get-tuple-element.33), channel_id=1, source_target_pairs={{0,4},{8,12},{16,20},{24,28},{4,0},{12,8},{20,16},{28,24},{1,5},{9... | collective-permute-start | bytes 49160 | tf_op jit(solution)/shard_map/ppermute | solution.py:457
  13.4 1.5 %shard_map.104 = (bf16[384,192]{1,0:T(8,128)(2,1)S(1)}, bf16[256,1536]{1,0:T(8,128)(2,1)S(1)}, bf16[256,1536]{1,0:T(8,128)(2,1)S(1)}) custom-call(f32[72,128]{1,0:T(8,128)S(1)} %get-tuple-element.35.refs_0_, bf16[384,192]{1,0:T(8,128)(2,1)} %constant.6.clone.refs_1_, bf16[256,1536]{1,0:T(8,128)(2,1)} %constant.7.clone.refs_2_, ...), custom_call_target="tpu_custom_call" | custom-call | tf_op jit(solution)/shard_map/pallas_call | solution.py:474
  14.9 0.0 collective-permute-done.3.inner_ref
  14.9 1.4 %collective-permute-done.5.refs_1_ = f32[40,128]{1,0:T(8,128)S(1)} collective-permute-done((f32[40,128]{1,0:T(8,128)S(1)}, f32[40,128]{1,0:T(8,128)S(1)}, u32[]{:S(2)}, u32[]{:S(2)}) %collective-permute-start.5) | collective-permute-done | bytes 20512 | tf_op jit(solution)/shard_map/ppermute | solution.py:468
  16.3 0.0 collective-permute-done.6.refs_2_
  16.3 0.0 collective-permute-done.4.refs_0_
  16.3 1.8 %shard_map.105 = f32[6,32,32]{2,1,0:T(8,128)} custom-call(f32[72,128]{1,0:T(8,128)S(1)} %get-tuple-element.27.mine_ref, f32[72,128]{1,0:T(8,128)S(1)} %collective-permute-done.got_ref, f32[6,64,128]{2,1,0:T(8,128)S(1)} %get-tuple-element.32.own_ref, f32[32,128]{1,0:T(8,128)S(1)} %collective-permute-done.3.inner_ref, ...), custom_call_target="tpu_custom_call" | custom-call | tf_op jit(solution)/shard_map/pallas_call | solution.py:480
Async XLA Ops:
  2.6 7.3 %collective-permute-start = (f32[72,128]{1,0:T(8,128)S(1)}, f32[72,128]{1,0:T(8,128)S(1)}, u32[]{:S(2)}, u32[]{:S(2)}) collective-permute-start(f32[72,128]{1,0:T(8,128)S(1)} %get-tuple-element.28), channel_id=1, source_target_pairs={{0,4},{8,12},{16,20},{24,28},{4,0},{12,8},{20,16},{28,24},{1,5},{9... | collective-permute-start | bytes 110600 | tf_op jit(solution)/shard_map/ppermute | solution.py:451
  3.2 6.5 %collective-permute-start.1 = (f32[2,16,128]{2,1,0:T(8,128)S(1)}, f32[2,16,128]{2,1,0:T(8,128)S(1)}, u32[]{:S(2)}, u32[]{:S(2)}) collective-permute-start(f32[2,16,128]{2,1,0:T(8,128)S(1)} %get-tuple-element.30), channel_id=1, source_target_pairs={{0,1},{1,2},{2,3},{3,0},{4,5},{5,6},{6,7},{7,4},{8,9},{9,10},{10,1... | collective-permute-start | bytes 49160 | tf_op jit(solution)/shard_map/ppermute | solution.py:442
  5.8 3.9 %collective-permute-start.2 = (f32[2,16,128]{2,1,0:T(8,128)S(1)}, f32[2,16,128]{2,1,0:T(8,128)S(1)}, u32[]{:S(2)}, u32[]{:S(2)}) collective-permute-start(f32[2,16,128]{2,1,0:T(8,128)S(1)} %get-tuple-element.31), channel_id=1, source_target_pairs={{1,0},{2,1},{3,2},{0,3},{5,4},{6,5},{7,6},{4,7},{9,8},{10,9},{11,1... | collective-permute-start | bytes 49160 | tf_op jit(solution)/shard_map/ppermute | solution.py:443
  10.0 6.3 %collective-permute-start.6 = (f32[72,128]{1,0:T(8,128)S(1)}, f32[72,128]{1,0:T(8,128)S(1)}, u32[]{:S(2)}, u32[]{:S(2)}) collective-permute-start(f32[72,128]{1,0:T(8,128)S(1)} %get-tuple-element.40), channel_id=1, source_target_pairs={{0,28},{4,24},{8,20},{12,16},{16,12},{20,8},{24,4},{28,0},{1,29},{... | collective-permute-start | bytes 110600 | tf_op jit(solution)/shard_map/ppermute | solution.py:468
  11.5 4.8 %collective-permute-start.4 = (f32[72,128]{1,0:T(8,128)S(1)}, f32[72,128]{1,0:T(8,128)S(1)}, u32[]{:S(2)}, u32[]{:S(2)}) collective-permute-start(f32[72,128]{1,0:T(8,128)S(1)} %get-tuple-element.35.refs_0_), channel_id=1, source_target_pairs={{0,12},{4,8},{8,4},{12,0},{16,28},{20,24},{24,20},{28,16},{1,13},{... | collective-permute-start | bytes 110600 | tf_op jit(solution)/shard_map/ppermute | solution.py:468
  12.9 3.4 %collective-permute-start.5 = (f32[40,128]{1,0:T(8,128)S(1)}, f32[40,128]{1,0:T(8,128)S(1)}, u32[]{:S(2)}, u32[]{:S(2)}) collective-permute-start(f32[40,128]{1,0:T(8,128)S(1)} %get-tuple-element.39), channel_id=1, source_target_pairs={{0,20},{4,16},{8,28},{12,24},{16,4},{20,0},{24,12},{28,8},{1,21},{... | collective-permute-start | bytes 61448 | tf_op jit(solution)/shard_map/ppermute | solution.py:468
  13.0 1.9 %collective-permute-start.3 = (f32[32,128]{1,0:T(8,128)S(1)}, f32[32,128]{1,0:T(8,128)S(1)}, u32[]{:S(2)}, u32[]{:S(2)}) collective-permute-start(f32[32,128]{1,0:T(8,128)S(1)} %get-tuple-element.33), channel_id=1, source_target_pairs={{0,4},{8,12},{16,20},{24,28},{4,0},{12,8},{20,16},{28,24},{1,5},{9... | collective-permute-start | bytes 49160 | tf_op jit(solution)/shard_map/ppermute | solution.py:457

commit v7 on v5

--- a/solution.py
+++ b/solution.py
@@ -99,18 +99,19 @@
     ]
     for copy in copies:
         copy.start()
-    for copy in copies:
-        copy.wait()
+    copies[0].wait()
     bands, rows, cols = t_ref.shape
     wide_ref[:, :, 0:cols] = t_ref[...]
     for k, tile in enumerate(packed([wide_ref[b] for b in range(bands)], cols)):
         last, leading = tile[rows - EDGE :], tile[:EDGE]
         first_ref[k] = last
         second_ref[k] = leading
+    for copy in copies[1:]:
+        copy.wait()
 
 
 def pack_kernel(
-    visits, cols, sci_ref, var_ref, coef_ref, foot_ref, meta_ref, mine_ref, away_ref, blocks
+    visits, cols, sci_ref, var_ref, coef_ref, foot_ref, w_ref, band_ref, mine_ref, away_ref, blocks
 ):
     rows = sci_ref.shape[1]
     short = rows // 2
@@ -118,10 +119,10 @@
     me = lax.axis_index("visit")
     chip, side = me // 2, me % 2
     at = chips * short
-    weight = jnp.broadcast_to(meta_ref[:, 0:1], (rows, 128))
+    weight = w_ref[0]
     coef = coef_ref[:, 0, :]
     terms, basis = coef.shape
-    which = jnp.broadcast_to(meta_ref[:, 1:2], (1, 128))
+    which = jnp.full((1, 128), band_ref[0].astype(F32), F32)
     for ref in (mine_ref, away_ref):
         ref[at : at + terms, 0:basis] = coef
         ref[at + terms : at + terms + 1] = which
@@ -431,16 +432,13 @@
     )(*sources)
     halo_a = lax.ppermute(first, "quad", [(i, (i + 1) % quads) for i in range(quads)])
     halo_b = lax.ppermute(second, "quad", [((i + 1) % quads, i) for i in range(quads)])
-    meta = lax.pad(visit_weight, np.float32(0), ((0, 127, 0),)) + lax.pad(
-        band.astype(F32), np.float32(0), ((1, 126, 0),)
-    )
     height = chips * short + 8
     mine, away = call(
         functools.partial(pack_kernel, visits, cols),
         [struct((height, 128), F32)] * 2,
-        [vmem] * 5,
+        [vmem] * 4 + [pl.BlockSpec(memory_space=pltpu.SMEM)] * 2,
         [pltpu.VMEM((visits, short, 128), F32)],
-    )(*loaded, meta[None])
+    )(*loaded, visit_weight, band)
     got = lax.ppermute(away, "visit", swaps(visits, 0))
     own, to_core, to_chips = call(
         functools.partial(edge_kernel, cols, quads),

time: 18.4 us -> 18.3 us (level)
  no operation moved by 1% of the time
where the time goes in v7:
time: 18.3 us; the launch traced here: 18.1 us
  starting transfers between devices  8.61 us (47%)
  Pallas kernels  4.95 us (27%)
  waiting for transfers between devices  3.22 us (18%)
  between operations  1.34 us (7%)
    ppermute x3, starting transfers between devices, per_device(): lax.ppermute(array, 'visit', [(i, i ^ 2 * m + 1) for i in range(visits)])  2.97 us
    ppermute x1, starting transfers between devices, per_device(): lax.ppermute(first, 'quad', [(i, (i + 1) % quads) for i in range(quads)])  2.63 us
    ppermute x1, starting transfers between devices, per_device(): lax.ppermute(second, 'quad', [((i + 1) % quads, i) for i in range(quads)])  2.09 us
    pallas_call x1, Pallas kernels, per_device(): call(functools.partial(model_kernel, visits, quads, steps), struct((bands...  1.84 us
    ppermute x1, waiting for transfers between devices, per_device(): lax.ppermute(first, 'quad', [(i, (i + 1) % quads) for i in range(quads)])  1.75 us
    pallas_call x1, Pallas kernels, per_device(): call(table_kernel, [struct(a.shape, a.dtype) for a in tables], [vmem] + [...  1.5 us
    ppermute x3, waiting for transfers between devices, per_device(): lax.ppermute(array, 'visit', [(i, i ^ 2 * m + 1) for i in range(visits)])  1.39 us
    pallas_call x1, Pallas kernels, per_device(): call(functools.partial(load_kernel, len(sources)), [strip, strip, struct(...  1.04 us
  transfers between devices with their start and end apart: 7, of which 3 were waited for; matrix products, arithmetic and copies ran while one was open for 0% of the time, Pallas kernels for 10%

profile of v7, /device:TPU:0, one launch (start us, length us, event | category | flops | bytes accessed | tf_op | source)
XLA Modules:
  0.0 18.1 jit_solution(1676710280848375185)
XLA Ops:
  1.3 1.0 %shard_map.100 = (f32[2,16,128]{2,1,0:T(8,128)S(1)}, f32[2,16,128]{2,1,0:T(8,128)S(1)}, f32[6,32,128]{2,1,0:T(8,128)S(1)}, f32[1,32,256]{2,1,0:T(8,128)S(1)}, f3...) custom-call(f32[6,32,32]{2,1,0:T(8,128)} %refs_0_.1, f32[1,32,256]{2,1,0:T(8,128)} %refs_1_.2, ...), custom_call_target="tpu_custom_call" | custom-call | tf_op jit(solution)/shard_map/pallas_call | solution.py:426
  2.3 0.2 %shard_map.101 = (f32[72,128]{1,0:T(8,128)S(1)}, f32[72,128]{1,0:T(8,128)S(1)}) custom-call(f32[1,32,256]{2,1,0:T(8,128)S(1)} %get-tuple-element.23.sci_ref, f32[1,32,256]{2,1,0:T(8,128)S(1)} %get-tuple-element.24.var_ref, f32[6,1,31]{2,1,0:T(1,128)S(1)} %get-tuple-element.25.coef_ref, s32[1,2,16]{2,1,0:T(2,128)S(1)} %get-tuple-element.26.foot_ref, ...), custom_call_target="tpu_custom_call" | custom-call | tf_op jit(solution)/shard_map/pallas_call | solution.py:436
  2.6 0.6 %collective-permute-start = (f32[72,128]{1,0:T(8,128)S(1)}, f32[72,128]{1,0:T(8,128)S(1)}, u32[]{:S(2)}, u32[]{:S(2)}) collective-permute-start(f32[72,128]{1,0:T(8,128)S(1)} %get-tuple-element.28), channel_id=1, source_target_pairs={{0,4},{8,12},{16,20},{24,28},{4,0},{12,8},{20,16},{28,24},{1,5},{9... | collective-permute-start | bytes 110600 | tf_op jit(solution)/shard_map/ppermute | solution.py:442
  3.2 2.6 %collective-permute-start.1 = (f32[2,16,128]{2,1,0:T(8,128)S(1)}, f32[2,16,128]{2,1,0:T(8,128)S(1)}, u32[]{:S(2)}, u32[]{:S(2)}) collective-permute-start(f32[2,16,128]{2,1,0:T(8,128)S(1)} %get-tuple-element.30), channel_id=1, source_target_pairs={{0,1},{1,2},{2,3},{3,0},{4,5},{5,6},{6,7},{7,4},{8,9},{9,10},{10,1... | collective-permute-start | bytes 49160 | tf_op jit(solution)/shard_map/ppermute | solution.py:433
  5.8 2.1 %collective-permute-start.2 = (f32[2,16,128]{2,1,0:T(8,128)S(1)}, f32[2,16,128]{2,1,0:T(8,128)S(1)}, u32[]{:S(2)}, u32[]{:S(2)}) collective-permute-start(f32[2,16,128]{2,1,0:T(8,128)S(1)} %get-tuple-element.31), channel_id=1, source_target_pairs={{1,0},{2,1},{3,2},{0,3},{5,4},{6,5},{7,6},{4,7},{9,8},{10,9},{11,1... | collective-permute-start | bytes 49160 | tf_op jit(solution)/shard_map/ppermute | solution.py:434
  7.9 1.8 %collective-permute-done.1.a_ref = f32[2,16,128]{2,1,0:T(8,128)S(1)} collective-permute-done((f32[2,16,128]{2,1,0:T(8,128)S(1)}, f32[2,16,128]{2,1,0:T(8,128)S(1)}, u32[]{:S(2)}, u32[]{:S(2)}) %collective-permute-start.1) | collective-permute-done | bytes 16416 | tf_op jit(solution)/shard_map/ppermute | solution.py:433
  9.6 0.1 collective-permute-done.2.b_ref
  9.7 0.2 %shard_map.102 = (f32[6,64,128]{2,1,0:T(8,128)S(1)}, f32[32,128]{1,0:T(8,128)S(1)}, f32[32,128]{1,0:T(8,128)S(1)}) custom-call(f32[6,32,128]{2,1,0:T(8,128)S(1)} %get-tuple-element.29.wide_ref, f32[2,16,128]{2,1,0:T(8,128)S(1)} %collective-permute-done.1.a_ref, f32[2,16,128]{2,1,0:T(8,128)S(1)} %collective-permute-done.2.b_ref), custom_call_target="tpu_custom_call" | custom-call | tf_op jit(solution)/shard_map/pallas_call | solution.py:443
  9.9 0.0 collective-permute-done.got_ref
  9.9 0.1 shard_map.103
  10.0 1.5 %collective-permute-start.6 = (f32[72,128]{1,0:T(8,128)S(1)}, f32[72,128]{1,0:T(8,128)S(1)}, u32[]{:S(2)}, u32[]{:S(2)}) collective-permute-start(f32[72,128]{1,0:T(8,128)S(1)} %get-tuple-element.40), channel_id=1, source_target_pairs={{0,28},{4,24},{8,20},{12,16},{16,12},{20,8},{24,4},{28,0},{1,29},{... | collective-permute-start | bytes 110600 | tf_op jit(solution)/shard_map/ppermute | solution.py:459
  11.5 1.4 %collective-permute-start.4 = (f32[72,128]{1,0:T(8,128)S(1)}, f32[72,128]{1,0:T(8,128)S(1)}, u32[]{:S(2)}, u32[]{:S(2)}) collective-permute-start(f32[72,128]{1,0:T(8,128)S(1)} %get-tuple-element.35.refs_0_), channel_id=1, source_target_pairs={{0,12},{4,8},{8,4},{12,0},{16,28},{20,24},{24,20},{28,16},{1,13},{... | collective-permute-start | bytes 110600 | tf_op jit(solution)/shard_map/ppermute | solution.py:459
  12.9 0.1 collective-permute-start.5
  13.0 0.4 %collective-permute-start.3 = (f32[32,128]{1,0:T(8,128)S(1)}, f32[32,128]{1,0:T(8,128)S(1)}, u32[]{:S(2)}, u32[]{:S(2)}) collective-permute-start(f32[32,128]{1,0:T(8,128)S(1)} %get-tuple-element.33), channel_id=1, source_target_pairs={{0,4},{8,12},{16,20},{24,28},{4,0},{12,8},{20,16},{28,24},{1,5},{9... | collective-permute-start | bytes 49160 | tf_op jit(solution)/shard_map/ppermute | solution.py:448
  13.4 1.5 %shard_map.104 = (bf16[384,192]{1,0:T(8,128)(2,1)S(1)}, bf16[256,1536]{1,0:T(8,128)(2,1)S(1)}, bf16[256,1536]{1,0:T(8,128)(2,1)S(1)}) custom-call(f32[72,128]{1,0:T(8,128)S(1)} %get-tuple-element.35.refs_0_, bf16[384,192]{1,0:T(8,128)(2,1)} %constant.6.clone.refs_1_, bf16[256,1536]{1,0:T(8,128)(2,1)} %constant.7.clone.refs_2_, ...), custom_call_target="tpu_custom_call" | custom-call | tf_op jit(solution)/shard_map/pallas_call | solution.py:465
  14.9 0.0 collective-permute-done.3.inner_ref
  14.9 1.4 %collective-permute-done.5.refs_1_ = f32[40,128]{1,0:T(8,128)S(1)} collective-permute-done((f32[40,128]{1,0:T(8,128)S(1)}, f32[40,128]{1,0:T(8,128)S(1)}, u32[]{:S(2)}, u32[]{:S(2)}) %collective-permute-start.5) | collective-permute-done | bytes 20512 | tf_op jit(solution)/shard_map/ppermute | solution.py:459
  16.3 0.0 collective-permute-done.6.refs_2_
  16.3 0.0 collective-permute-done.4.refs_0_
  16.3 1.8 %shard_map.105 = f32[6,32,32]{2,1,0:T(8,128)} custom-call(f32[72,128]{1,0:T(8,128)S(1)} %get-tuple-element.27.mine_ref, f32[72,128]{1,0:T(8,128)S(1)} %collective-permute-done.got_ref, f32[6,64,128]{2,1,0:T(8,128)S(1)} %get-tuple-element.32.own_ref, f32[32,128]{1,0:T(8,128)S(1)} %collective-permute-done.3.inner_ref, ...), custom_call_target="tpu_custom_call" | custom-call | tf_op jit(solution)/shard_map/pallas_call | solution.py:471
Async XLA Ops:
  2.6 7.3 %collective-permute-start = (f32[72,128]{1,0:T(8,128)S(1)}, f32[72,128]{1,0:T(8,128)S(1)}, u32[]{:S(2)}, u32[]{:S(2)}) collective-permute-start(f32[72,128]{1,0:T(8,128)S(1)} %get-tuple-element.28), channel_id=1, source_target_pairs={{0,4},{8,12},{16,20},{24,28},{4,0},{12,8},{20,16},{28,24},{1,5},{9... | collective-permute-start | bytes 110600 | tf_op jit(solution)/shard_map/ppermute | solution.py:442
  3.2 6.5 %collective-permute-start.1 = (f32[2,16,128]{2,1,0:T(8,128)S(1)}, f32[2,16,128]{2,1,0:T(8,128)S(1)}, u32[]{:S(2)}, u32[]{:S(2)}) collective-permute-start(f32[2,16,128]{2,1,0:T(8,128)S(1)} %get-tuple-element.30), channel_id=1, source_target_pairs={{0,1},{1,2},{2,3},{3,0},{4,5},{5,6},{6,7},{7,4},{8,9},{9,10},{10,1... | collective-permute-start | bytes 49160 | tf_op jit(solution)/shard_map/ppermute | solution.py:433
  5.8 3.9 %collective-permute-start.2 = (f32[2,16,128]{2,1,0:T(8,128)S(1)}, f32[2,16,128]{2,1,0:T(8,128)S(1)}, u32[]{:S(2)}, u32[]{:S(2)}) collective-permute-start(f32[2,16,128]{2,1,0:T(8,128)S(1)} %get-tuple-element.31), channel_id=1, source_target_pairs={{1,0},{2,1},{3,2},{0,3},{5,4},{6,5},{7,6},{4,7},{9,8},{10,9},{11,1... | collective-permute-start | bytes 49160 | tf_op jit(solution)/shard_map/ppermute | solution.py:434
  10.0 6.3 %collective-permute-start.6 = (f32[72,128]{1,0:T(8,128)S(1)}, f32[72,128]{1,0:T(8,128)S(1)}, u32[]{:S(2)}, u32[]{:S(2)}) collective-permute-start(f32[72,128]{1,0:T(8,128)S(1)} %get-tuple-element.40), channel_id=1, source_target_pairs={{0,28},{4,24},{8,20},{12,16},{16,12},{20,8},{24,4},{28,0},{1,29},{... | collective-permute-start | bytes 110600 | tf_op jit(solution)/shard_map/ppermute | solution.py:459
  11.5 4.8 %collective-permute-start.4 = (f32[72,128]{1,0:T(8,128)S(1)}, f32[72,128]{1,0:T(8,128)S(1)}, u32[]{:S(2)}, u32[]{:S(2)}) collective-permute-start(f32[72,128]{1,0:T(8,128)S(1)} %get-tuple-element.35.refs_0_), channel_id=1, source_target_pairs={{0,12},{4,8},{8,4},{12,0},{16,28},{20,24},{24,20},{28,16},{1,13},{... | collective-permute-start | bytes 110600 | tf_op jit(solution)/shard_map/ppermute | solution.py:459
  12.9 3.4 %collective-permute-start.5 = (f32[40,128]{1,0:T(8,128)S(1)}, f32[40,128]{1,0:T(8,128)S(1)}, u32[]{:S(2)}, u32[]{:S(2)}) collective-permute-start(f32[40,128]{1,0:T(8,128)S(1)} %get-tuple-element.39), channel_id=1, source_target_pairs={{0,20},{4,16},{8,28},{12,24},{16,4},{20,0},{24,12},{28,8},{1,21},{... | collective-permute-start | bytes 61448 | tf_op jit(solution)/shard_map/ppermute | solution.py:459
  13.0 1.9 %collective-permute-start.3 = (f32[32,128]{1,0:T(8,128)S(1)}, f32[32,128]{1,0:T(8,128)S(1)}, u32[]{:S(2)}, u32[]{:S(2)}) collective-permute-start(f32[32,128]{1,0:T(8,128)S(1)} %get-tuple-element.33), channel_id=1, source_target_pairs={{0,4},{8,12},{16,20},{24,28},{4,0},{12,8},{20,16},{28,24},{1,5},{9... | collective-permute-start | bytes 49160 | tf_op jit(solution)/shard_map/ppermute | solution.py:448

commit v8 on v7

--- a/solution.py
+++ b/solution.py
@@ -291,31 +291,13 @@
     for ref in message_refs:
         slots += [(ref, 0, ref, rows, False), (ref, short, ref, rows, True)]
 
-    def gather(members):
-        blocks, tails, band_rows = [], [], []
-        for ref, at, tail_ref, tail_at, high in members:
-            blocks.append(ref[at : at + short])
+    def select(members):
+        tails, band_rows = [], []
+        for _, _, tail_ref, tail_at, high in members:
             tail = tail_ref[tail_at : tail_at + 8]
             turned = pltpu.roll(tail, 64, 1)
             tails.append(turned if high else tail)
             band_rows.append(jnp.where(low_half == (not high), tail[6:7], turned[6:7]))
-        pieces = [jnp.zeros((short, 128), F32)] * 4
-        which = jnp.zeros((1, 128), F32)
-        for v in range(GROUP):
-            here = (flat >= v * cols) & (flat < (v + 1) * cols)
-            pieces = [
-                jnp.where(here, pltpu.roll(blocks[v], (v * cols - 32 * k) % 128, 1), piece)
-                for k, piece in enumerate(pieces)
-            ]
-            which = jnp.where(here[:1], band_rows[v], which)
-        tails.append(jnp.zeros((128 - 8 * GROUP, 128), F32))
-        cmat = jnp.transpose(jnp.concatenate(tails, axis=0))[0:rows]
-        terms = [jnp.take_along_axis(cmat, base + s, axis=1) for s in range(6)]
-        polys = (
-            terms[0] + x * (terms[1] + x * terms[3]),
-            terms[2] + x * terms[4],
-            terms[5],
-        )
         images = [
             choose(
                 jnp.where(low_half, band_rows[2 * p], band_rows[2 * p + 1]),
@@ -323,18 +305,37 @@
             )
             for p in range(GROUP // 2)
         ]
+        return jnp.concatenate(images, axis=1), tails, band_rows
+
+    def gather(members, tails, band_rows):
+        pieces = [jnp.zeros((short, 128), F32)] * 4
+        which = jnp.zeros((1, 128), F32)
+        for v, (ref, at, _, _, _) in enumerate(members):
+            block = ref[at : at + short]
+            here = (flat >= v * cols) & (flat < (v + 1) * cols)
+            pieces = [
+                jnp.where(here, pltpu.roll(block, (v * cols - 32 * k) % 128, 1), piece)
+                for k, piece in enumerate(pieces)
+            ]
+            which = jnp.where(here[:1], band_rows[v], which)
+        padded = tails + [jnp.zeros((128 - 8 * GROUP, 128), F32)]
+        cmat = jnp.transpose(jnp.concatenate(padded, axis=0))[0:rows]
+        terms = [jnp.take_along_axis(cmat, base + s, axis=1) for s in range(6)]
+        polys = (
+            terms[0] + x * (terms[1] + x * terms[3]),
+            terms[2] + x * terms[4],
+            terms[5],
+        )
         first = jnp.concatenate(pieces[:2], axis=0)
         second = jnp.concatenate(pieces[2:], axis=0)
-        return polys, jnp.concatenate(images, axis=1), first, second, which
+        return polys, first, second, which
 
     totals = [jnp.zeros((rows, 128), F32) for _ in range(bands)]
     for start in range(0, groups, 2):
-        pair = [gather(slots[g * GROUP : (g + 1) * GROUP]) for g in (start, start + 1)]
-        parts = [split(image) for _, image, _, _, _ in pair]
+        members = [slots[g * GROUP : (g + 1) * GROUP] for g in (start, start + 1)]
+        chosen = [select(m) for m in members]
+        parts = [split(image) for image, _, _ in chosen]
         both = jnp.concatenate([p[0] for p in parts] + [p[1] for p in parts], axis=0)
-        poly0, poly1, poly2 = [
-            jnp.concatenate([pair[0][0][k], pair[1][0][k]], axis=1) for k in range(3)
-        ]
         filt = 0
         for degree in DEGREES:
             count = degree + 1
@@ -355,6 +356,10 @@
                     stack[at + ext : at + 2 * ext] = low
                     stack[at + 2 * ext : at + 3 * ext] = high
             filt += count
+        pair = [gather(m, *c[1:]) for m, c in zip(members, chosen)]
+        poly0, poly1, poly2 = [
+            jnp.concatenate([pair[0][0][k], pair[1][0][k]], axis=1) for k in range(3)
+        ]
         model = jnp.zeros((rows, 256), F32)
         basis_start = 0
         filt = 0
@@ -380,7 +385,7 @@
             basis_start = k
             filt += count
         for g in range(2):
-            _, _, first, second, which = pair[g]
+            _, first, second, which = pair[g]
             part = first - second * model[:, g * 128 : (g + 1) * 128]
             which = jnp.broadcast_to(which, (rows, 128))
             for b in range(bands):

time: 18.3 us -> 18.3 us (level)
  no operation moved by 1% of the time
where the time goes in v8:
time: 18.3 us; the launch traced here: 18.1 us
  starting transfers between devices  8.61 us (47%)
  Pallas kernels  4.95 us (27%)
  waiting for transfers between devices  3.22 us (18%)
  between operations  1.34 us (7%)
    ppermute x3, starting transfers between devices, per_device(): lax.ppermute(array, 'visit', [(i, i ^ 2 * m + 1) for i in range(visits)])  2.97 us
    ppermute x1, starting transfers between devices, per_device(): lax.ppermute(first, 'quad', [(i, (i + 1) % quads) for i in range(quads)])  2.63 us
    ppermute x1, starting transfers between devices, per_device(): lax.ppermute(second, 'quad', [((i + 1) % quads, i) for i in range(quads)])  2.09 us
    pallas_call x1, Pallas kernels, per_device(): call(functools.partial(model_kernel, visits, quads, steps), struct((bands...  1.84 us
    ppermute x1, waiting for transfers between devices, per_device(): lax.ppermute(first, 'quad', [(i, (i + 1) % quads) for i in range(quads)])  1.75 us
    pallas_call x1, Pallas kernels, per_device(): call(table_kernel, [struct(a.shape, a.dtype) for a in tables], [vmem] + [...  1.5 us
    ppermute x3, waiting for transfers between devices, per_device(): lax.ppermute(array, 'visit', [(i, i ^ 2 * m + 1) for i in range(visits)])  1.39 us
    pallas_call x1, Pallas kernels, per_device(): call(functools.partial(load_kernel, len(sources)), [strip, strip, struct(...  1.04 us
  transfers between devices with their start and end apart: 7, of which 3 were waited for; matrix products, arithmetic and copies ran while one was open for 0% of the time, Pallas kernels for 10%

profile of v8, /device:TPU:0, one launch (start us, length us, event | category | flops | bytes accessed | tf_op | source)
XLA Modules:
  0.0 18.1 jit_solution(1676710280848375185)
XLA Ops:
  1.3 1.0 %shard_map.100 = (f32[2,16,128]{2,1,0:T(8,128)S(1)}, f32[2,16,128]{2,1,0:T(8,128)S(1)}, f32[6,32,128]{2,1,0:T(8,128)S(1)}, f32[1,32,256]{2,1,0:T(8,128)S(1)}, f3...) custom-call(f32[6,32,32]{2,1,0:T(8,128)} %refs_0_.1, f32[1,32,256]{2,1,0:T(8,128)} %refs_1_.2, ...), custom_call_target="tpu_custom_call" | custom-call | tf_op jit(solution)/shard_map/pallas_call | solution.py:431
  2.3 0.2 %shard_map.101 = (f32[72,128]{1,0:T(8,128)S(1)}, f32[72,128]{1,0:T(8,128)S(1)}) custom-call(f32[1,32,256]{2,1,0:T(8,128)S(1)} %get-tuple-element.23.sci_ref, f32[1,32,256]{2,1,0:T(8,128)S(1)} %get-tuple-element.24.var_ref, f32[6,1,31]{2,1,0:T(1,128)S(1)} %get-tuple-element.25.coef_ref, s32[1,2,16]{2,1,0:T(2,128)S(1)} %get-tuple-element.26.foot_ref, ...), custom_call_target="tpu_custom_call" | custom-call | tf_op jit(solution)/shard_map/pallas_call | solution.py:441
  2.6 0.6 %collective-permute-start = (f32[72,128]{1,0:T(8,128)S(1)}, f32[72,128]{1,0:T(8,128)S(1)}, u32[]{:S(2)}, u32[]{:S(2)}) collective-permute-start(f32[72,128]{1,0:T(8,128)S(1)} %get-tuple-element.28), channel_id=1, source_target_pairs={{0,4},{8,12},{16,20},{24,28},{4,0},{12,8},{20,16},{28,24},{1,5},{9... | collective-permute-start | bytes 110600 | tf_op jit(solution)/shard_map/ppermute | solution.py:447
  3.2 2.6 %collective-permute-start.1 = (f32[2,16,128]{2,1,0:T(8,128)S(1)}, f32[2,16,128]{2,1,0:T(8,128)S(1)}, u32[]{:S(2)}, u32[]{:S(2)}) collective-permute-start(f32[2,16,128]{2,1,0:T(8,128)S(1)} %get-tuple-element.30), channel_id=1, source_target_pairs={{0,1},{1,2},{2,3},{3,0},{4,5},{5,6},{6,7},{7,4},{8,9},{9,10},{10,1... | collective-permute-start | bytes 49160 | tf_op jit(solution)/shard_map/ppermute | solution.py:438
  5.8 2.1 %collective-permute-start.2 = (f32[2,16,128]{2,1,0:T(8,128)S(1)}, f32[2,16,128]{2,1,0:T(8,128)S(1)}, u32[]{:S(2)}, u32[]{:S(2)}) collective-permute-start(f32[2,16,128]{2,1,0:T(8,128)S(1)} %get-tuple-element.31), channel_id=1, source_target_pairs={{1,0},{2,1},{3,2},{0,3},{5,4},{6,5},{7,6},{4,7},{9,8},{10,9},{11,1... | collective-permute-start | bytes 49160 | tf_op jit(solution)/shard_map/ppermute | solution.py:439
  7.9 1.8 %collective-permute-done.1.a_ref = f32[2,16,128]{2,1,0:T(8,128)S(1)} collective-permute-done((f32[2,16,128]{2,1,0:T(8,128)S(1)}, f32[2,16,128]{2,1,0:T(8,128)S(1)}, u32[]{:S(2)}, u32[]{:S(2)}) %collective-permute-start.1) | collective-permute-done | bytes 16416 | tf_op jit(solution)/shard_map/ppermute | solution.py:438
  9.6 0.1 collective-permute-done.2.b_ref
  9.7 0.2 %shard_map.102 = (f32[6,64,128]{2,1,0:T(8,128)S(1)}, f32[32,128]{1,0:T(8,128)S(1)}, f32[32,128]{1,0:T(8,128)S(1)}) custom-call(f32[6,32,128]{2,1,0:T(8,128)S(1)} %get-tuple-element.29.wide_ref, f32[2,16,128]{2,1,0:T(8,128)S(1)} %collective-permute-done.1.a_ref, f32[2,16,128]{2,1,0:T(8,128)S(1)} %collective-permute-done.2.b_ref), custom_call_target="tpu_custom_call" | custom-call | tf_op jit(solution)/shard_map/pallas_call | solution.py:448
  9.9 0.0 collective-permute-done.got_ref
  9.9 0.1 shard_map.103
  10.0 1.5 %collective-permute-start.6 = (f32[72,128]{1,0:T(8,128)S(1)}, f32[72,128]{1,0:T(8,128)S(1)}, u32[]{:S(2)}, u32[]{:S(2)}) collective-permute-start(f32[72,128]{1,0:T(8,128)S(1)} %get-tuple-element.40), channel_id=1, source_target_pairs={{0,28},{4,24},{8,20},{12,16},{16,12},{20,8},{24,4},{28,0},{1,29},{... | collective-permute-start | bytes 110600 | tf_op jit(solution)/shard_map/ppermute | solution.py:464
  11.5 1.4 %collective-permute-start.4 = (f32[72,128]{1,0:T(8,128)S(1)}, f32[72,128]{1,0:T(8,128)S(1)}, u32[]{:S(2)}, u32[]{:S(2)}) collective-permute-start(f32[72,128]{1,0:T(8,128)S(1)} %get-tuple-element.35.refs_0_), channel_id=1, source_target_pairs={{0,12},{4,8},{8,4},{12,0},{16,28},{20,24},{24,20},{28,16},{1,13},{... | collective-permute-start | bytes 110600 | tf_op jit(solution)/shard_map/ppermute | solution.py:464
  12.9 0.1 collective-permute-start.5
  13.0 0.4 %collective-permute-start.3 = (f32[32,128]{1,0:T(8,128)S(1)}, f32[32,128]{1,0:T(8,128)S(1)}, u32[]{:S(2)}, u32[]{:S(2)}) collective-permute-start(f32[32,128]{1,0:T(8,128)S(1)} %get-tuple-element.33), channel_id=1, source_target_pairs={{0,4},{8,12},{16,20},{24,28},{4,0},{12,8},{20,16},{28,24},{1,5},{9... | collective-permute-start | bytes 49160 | tf_op jit(solution)/shard_map/ppermute | solution.py:453
  13.4 1.5 %shard_map.104 = (bf16[384,192]{1,0:T(8,128)(2,1)S(1)}, bf16[256,1536]{1,0:T(8,128)(2,1)S(1)}, bf16[256,1536]{1,0:T(8,128)(2,1)S(1)}) custom-call(f32[72,128]{1,0:T(8,128)S(1)} %get-tuple-element.35.refs_0_, bf16[384,192]{1,0:T(8,128)(2,1)} %constant.6.clone.refs_1_, bf16[256,1536]{1,0:T(8,128)(2,1)} %constant.7.clone.refs_2_, ...), custom_call_target="tpu_custom_call" | custom-call | tf_op jit(solution)/shard_map/pallas_call | solution.py:470
  14.9 0.0 collective-permute-done.3.inner_ref
  14.9 1.4 %collective-permute-done.5.refs_1_ = f32[40,128]{1,0:T(8,128)S(1)} collective-permute-done((f32[40,128]{1,0:T(8,128)S(1)}, f32[40,128]{1,0:T(8,128)S(1)}, u32[]{:S(2)}, u32[]{:S(2)}) %collective-permute-start.5) | collective-permute-done | bytes 20512 | tf_op jit(solution)/shard_map/ppermute | solution.py:464
  16.3 0.0 collective-permute-done.6.refs_2_
  16.3 0.0 collective-permute-done.4.refs_0_
  16.3 1.8 %shard_map.105 = f32[6,32,32]{2,1,0:T(8,128)} custom-call(f32[72,128]{1,0:T(8,128)S(1)} %get-tuple-element.27.mine_ref, f32[72,128]{1,0:T(8,128)S(1)} %collective-permute-done.got_ref, f32[6,64,128]{2,1,0:T(8,128)S(1)} %get-tuple-element.32.own_ref, f32[32,128]{1,0:T(8,128)S(1)} %collective-permute-done.3.inner_ref, ...), custom_call_target="tpu_custom_call" | custom-call | tf_op jit(solution)/shard_map/pallas_call | solution.py:476
Async XLA Ops:
  2.6 7.3 %collective-permute-start = (f32[72,128]{1,0:T(8,128)S(1)}, f32[72,128]{1,0:T(8,128)S(1)}, u32[]{:S(2)}, u32[]{:S(2)}) collective-permute-start(f32[72,128]{1,0:T(8,128)S(1)} %get-tuple-element.28), channel_id=1, source_target_pairs={{0,4},{8,12},{16,20},{24,28},{4,0},{12,8},{20,16},{28,24},{1,5},{9... | collective-permute-start | bytes 110600 | tf_op jit(solution)/shard_map/ppermute | solution.py:447
  3.2 6.5 %collective-permute-start.1 = (f32[2,16,128]{2,1,0:T(8,128)S(1)}, f32[2,16,128]{2,1,0:T(8,128)S(1)}, u32[]{:S(2)}, u32[]{:S(2)}) collective-permute-start(f32[2,16,128]{2,1,0:T(8,128)S(1)} %get-tuple-element.30), channel_id=1, source_target_pairs={{0,1},{1,2},{2,3},{3,0},{4,5},{5,6},{6,7},{7,4},{8,9},{9,10},{10,1... | collective-permute-start | bytes 49160 | tf_op jit(solution)/shard_map/ppermute | solution.py:438
  5.8 3.9 %collective-permute-start.2 = (f32[2,16,128]{2,1,0:T(8,128)S(1)}, f32[2,16,128]{2,1,0:T(8,128)S(1)}, u32[]{:S(2)}, u32[]{:S(2)}) collective-permute-start(f32[2,16,128]{2,1,0:T(8,128)S(1)} %get-tuple-element.31), channel_id=1, source_target_pairs={{1,0},{2,1},{3,2},{0,3},{5,4},{6,5},{7,6},{4,7},{9,8},{10,9},{11,1... | collective-permute-start | bytes 49160 | tf_op jit(solution)/shard_map/ppermute | solution.py:439
  10.0 6.3 %collective-permute-start.6 = (f32[72,128]{1,0:T(8,128)S(1)}, f32[72,128]{1,0:T(8,128)S(1)}, u32[]{:S(2)}, u32[]{:S(2)}) collective-permute-start(f32[72,128]{1,0:T(8,128)S(1)} %get-tuple-element.40), channel_id=1, source_target_pairs={{0,28},{4,24},{8,20},{12,16},{16,12},{20,8},{24,4},{28,0},{1,29},{... | collective-permute-start | bytes 110600 | tf_op jit(solution)/shard_map/ppermute | solution.py:464
  11.5 4.8 %collective-permute-start.4 = (f32[72,128]{1,0:T(8,128)S(1)}, f32[72,128]{1,0:T(8,128)S(1)}, u32[]{:S(2)}, u32[]{:S(2)}) collective-permute-start(f32[72,128]{1,0:T(8,128)S(1)} %get-tuple-element.35.refs_0_), channel_id=1, source_target_pairs={{0,12},{4,8},{8,4},{12,0},{16,28},{20,24},{24,20},{28,16},{1,13},{... | collective-permute-start | bytes 110600 | tf_op jit(solution)/shard_map/ppermute | solution.py:464
  12.9 3.4 %collective-permute-start.5 = (f32[40,128]{1,0:T(8,128)S(1)}, f32[40,128]{1,0:T(8,128)S(1)}, u32[]{:S(2)}, u32[]{:S(2)}) collective-permute-start(f32[40,128]{1,0:T(8,128)S(1)} %get-tuple-element.39), channel_id=1, source_target_pairs={{0,20},{4,16},{8,28},{12,24},{16,4},{20,0},{24,12},{28,8},{1,21},{... | collective-permute-start | bytes 61448 | tf_op jit(solution)/shard_map/ppermute | solution.py:464
  13.0 1.9 %collective-permute-start.3 = (f32[32,128]{1,0:T(8,128)S(1)}, f32[32,128]{1,0:T(8,128)S(1)}, u32[]{:S(2)}, u32[]{:S(2)}) collective-permute-start(f32[32,128]{1,0:T(8,128)S(1)} %get-tuple-element.33), channel_id=1, source_target_pairs={{0,4},{8,12},{16,20},{24,28},{4,0},{12,8},{20,16},{28,24},{1,5},{9... | collective-permute-start | bytes 49160 | tf_op jit(solution)/shard_map/ppermute | solution.py:453
